TPU v7x, 256 devices: a whole 4x4x8 slice. The times are simulated.
256 devices in a mesh: gene: 4 (over z_hi, core), peak: 64 (over x, z_lo, y).
Axes of the slice: x: 4, y: 4, z: 8 (z_hi: 2, z_lo: 4; z = z_hi * 4 + z_lo), core: 2. Of those that a mesh axis runs over, the one named last changes fastest.
Arguments:
- gene_act: bfloat16 [32768, 1024], P('peak'), may hold values from -6 to 6
- peak_act: bfloat16 [131072, 1024], P('peak'), may hold values from -6 to 6
- w_query: bfloat16 [1024, 1024], P(None, 'gene'), may hold values from -0.1875 to 0.1875
- w_key: bfloat16 [1024, 1024], P(None, 'gene'), may hold values from -0.1875 to 0.1875
- w_value: bfloat16 [1024, 1024], P(None, 'gene'), may hold values from -0.1875 to 0.1875
- w_out: bfloat16 [1024, 1024], P('gene'), may hold values from -0.1875 to 0.1875
- head_bias: float32 [8], P('gene'), may hold values from -6 to -3
- block_mask: int32 [256, 1024], replicated, may hold values from 0 to 1, as said below
- gene_chrom: int32 [32768], replicated, may hold values from 0 to 22, as said below
- peak_chrom: int32 [131072], replicated, may hold values from 0 to 22, as said below
Outputs:
- mixed: bfloat16 [32768, 1024], P('peak', 'gene')
Inputs may be any that keep to these rules, and one draw needn't show every extreme that they name: For each gene tile i, the 1s of block_mask[i] form one run of consecutive peak tiles that contains tile 4i and lies within the peak tiles of the shards o - 2 to o + 2, where o = i // 4 is the shard of peak that holds gene tile i; runs of different lengths reach that limit on either side in every draw. `peak_chrom`: never falls along the peaks; each chromosome is one run of consecutive peaks. `gene_chrom`: gene query g lies at peak position 4g and carries that peak's chromosome.
All inputs are finite; a program needn't handle non-finite values.
Results may differ from a plain program's by a relative error of at most 0.0064.
Values may be sent and summed in bfloat16 or wider, within the bound.
No kernel may reach another device: no remote copies, remote signals or barrier semaphores. Data moves between devices by JAX's collectives and lax.ppermute only.
A program may use at most 128 MiB of HBM per device.

v0:
```python
import functools
import math

import jax
import jax.numpy as jnp
from jax import lax
from jax.experimental import pallas as pl
from jax.experimental.pallas import tpu as pltpu
from jax.sharding import PartitionSpec as P

TILE = 128
REACH = 2
CHUNK = 512
HEAD = 8
F32 = jnp.float32
BF16 = jnp.bfloat16
PARAMS = pltpu.CompilerParams(vmem_limit_bytes=16 << 20)
VMEM = pl.BlockSpec(memory_space=pltpu.VMEM)
SMEM = pl.BlockSpec(memory_space=pltpu.SMEM)


def swap_pairs(count, by, kind):
    pairs = []
    for i in range(count - by):
        if (i // by) % 2 == kind:
            pairs += [(i, i + by), (i + by, i)]
    return pairs


def cost(flops, arrays):
    return pl.CostEstimate(
        flops=flops, bytes_accessed=sum(a.size * a.dtype.itemsize for a in arrays), transcendentals=0
    )


def kv_kernel(act_ref, wk_ref, wv_ref, k_ref, v_ref):
    act = act_ref[...]
    k_ref[...] = jnp.dot(act, wk_ref[...], preferred_element_type=F32).astype(BF16)
    v_ref[...] = jnp.dot(act, wv_ref[...], preferred_element_type=F32).astype(BF16)


def project_kv(act, wk, wv, rows):
    total, depth = act.shape
    width = wk.shape[1]
    whole = pl.BlockSpec((depth, width), lambda i: (0, 0))
    return pl.pallas_call(
        kv_kernel,
        grid=(total // rows,),
        in_specs=[pl.BlockSpec((rows, depth), lambda i: (i, 0)), whole, whole],
        out_specs=[pl.BlockSpec((rows, width), lambda i: (i, 0))] * 2,
        out_shape=[jax.ShapeDtypeStruct((total, width), BF16)] * 2,
        cost_estimate=cost(4 * total * depth * width, [act, wk, wv, act]),
        compiler_params=PARAMS,
        name="project_kv",
    )(act, wk, wv)


def attend_kernel(slot, heads, meta_ref, bias_ref, gene_ref, peak_ref, q_ref, k_ref, v_ref, o_ref, acc):
    tiles = q_ref.shape[0] // TILE
    per_chunk = CHUNK // TILE
    dim = q_ref.shape[1] // heads
    scale = 0.5 / math.sqrt(dim)
    start = meta_ref[slot]
    base = jnp.maximum(start, 0)
    lows = [meta_ref[HEAD + 2 * (base + i)] for i in range(tiles)]
    highs = [meta_ref[HEAD + 2 * (base + i) + 1] for i in range(tiles)]
    low = functools.reduce(jnp.minimum, lows)
    high = functools.reduce(jnp.maximum, highs)
    first = low // per_chunk
    last = jnp.where(start < 0, first, (high + per_chunk - 1) // per_chunk)
    acc[...] = jnp.zeros_like(acc)
    tags = [
        jnp.broadcast_to(gene_ref[pl.ds(base + i, 1), :], (TILE, TILE)).T for i in range(tiles)
    ]

    def chunk(c, carry):
        rows = pl.ds(pl.multiple_of(c * CHUNK, CHUNK), CHUNK)
        peaks = [peak_ref[pl.ds(c * per_chunk + j, 1), :] for j in range(per_chunk)]
        for h in range(heads):
            cols = slice(h * dim, (h + 1) * dim)
            scores = lax.dot_general(
                q_ref[:, cols], k_ref[rows, cols], (((1,), (1,)), ((), ())), preferred_element_type=F32
            )
            twice = jnp.tanh(scores * scale + 0.5 * bias_ref[h]) + 1.0
            bands = []
            for i in range(tiles):
                band = []
                for j in range(per_chunk):
                    t = c * per_chunk + j
                    inside = (t >= lows[i]) & (t < highs[i])
                    allowed = tags[i] == jnp.where(inside, peaks[j], -1)
                    part = twice[i * TILE : (i + 1) * TILE, j * TILE : (j + 1) * TILE]
                    band.append(jnp.where(allowed, part, 0.0))
                bands.append(jnp.concatenate(band, 1))
            weights = jnp.concatenate(bands, 0).astype(BF16)
            acc[:, cols] += jnp.dot(weights, v_ref[rows, cols], preferred_element_type=F32)
        return carry

    lax.fori_loop(first, last, chunk, 0)
    o_ref[...] = (acc[...] * 0.5).astype(o_ref.dtype)


def attend(slot, heads, meta, bias, gene, peak, q, k, v, dtype):
    return pl.pallas_call(
        functools.partial(attend_kernel, slot, heads),
        in_specs=[SMEM, SMEM] + [VMEM] * 5,
        out_specs=VMEM,
        out_shape=jax.ShapeDtypeStruct(q.shape, dtype),
        scratch_shapes=[pltpu.VMEM(q.shape, F32)],
        cost_estimate=cost(4 * q.shape[0] * k.shape[0] * k.shape[1], [q, k, v, q]),
        compiler_params=PARAMS,
        name="attend_%d" % slot,
    )(meta, bias, gene, peak, q, k, v)


def mix_kernel(slot, meta_ref, own_ref, r1, r2, r3, r4, w_ref, send_ref, keep_ref):
    width = w_ref.shape[1] // 4
    me = meta_ref[slot]
    total = own_ref[...]
    for r in (r1, r2, r3, r4):
        total = total + r[...].astype(F32)
    attended = total.astype(BF16)

    def share(block):
        cols = pl.ds(pl.multiple_of(block * width, width), width)
        return jnp.dot(attended, w_ref[:, cols], preferred_element_type=F32)

    send_ref[:, :width] = share(me ^ 3).astype(BF16)
    send_ref[:, width:] = share(me ^ 1).astype(BF16)
    keep_ref[:, :width] = share(me ^ 2)
    keep_ref[:, width:] = share(me)


def mix(slot, meta, own, parts, w):
    shape = (own.shape[0], w.shape[1] // 2)
    return pl.pallas_call(
        functools.partial(mix_kernel, slot),
        in_specs=[SMEM] + [VMEM] * 6,
        out_specs=[VMEM, VMEM],
        out_shape=[jax.ShapeDtypeStruct(shape, BF16), jax.ShapeDtypeStruct(shape, F32)],
        cost_estimate=cost(2 * own.shape[0] * w.size, [own, w, own, own]),
        compiler_params=PARAMS,
        name="mix",
    )(meta, own, *parts, w)


def on_device(
    gene_act,
    peak_act,
    w_query,
    w_key,
    w_value,
    w_out,
    head_bias,
    block_mask,
    gene_chrom,
    peak_chrom,
):
    gene_rows = gene_act.shape[0]
    peak_rows = peak_act.shape[0]
    heads = head_bias.shape[0]
    gene_tiles = gene_rows // TILE
    peak_tiles = peak_rows // TILE
    window = (2 * REACH + 1) * gene_tiles
    me = lax.axis_index("peak")
    count = lax.axis_size("peak")
    gene_me = lax.axis_index("gene")

    queries = jnp.dot(gene_act, w_query, preferred_element_type=F32).astype(BF16)
    steps = [(1, 1), (2, 1), (1, 0), (2, 0)]
    far = [lax.ppermute(queries, "peak", swap_pairs(count, by, kind)) for by, kind in steps]

    origin = jnp.clip((me - REACH) * gene_tiles, 0, count * gene_tiles - window)
    tiles = lax.dynamic_slice(block_mask, (origin, me * peak_tiles), (window, peak_tiles))
    gene = lax.dynamic_slice_in_dim(gene_chrom, origin * TILE, window * TILE).reshape(window, TILE)
    peak = lax.dynamic_slice_in_dim(peak_chrom, me * peak_rows, peak_rows).reshape(peak_tiles, TILE)
    meet = (gene[:, :1] <= peak[None, :, -1]) & (peak[None, :, 0] <= gene[:, -1:])
    live = (tiles > 0) & meet
    place = lax.broadcasted_iota(jnp.int32, live.shape, 1)
    low = jnp.min(jnp.where(live, place, peak_tiles), axis=1)
    high = jnp.max(jnp.where(live, place + 1, 0), axis=1)
    words = []
    for by, kind in [(0, 0)] + steps:
        if by:
            by = jnp.where((me // by) % 2 == kind, by, -by)
        source = me + by
        inside = (source >= 0) & (source < count)
        words.append(jnp.where(inside, source * gene_tiles - origin, -1))
    words.append(gene_me)
    words += [jnp.zeros_like(gene_me)] * (HEAD - len(words))
    meta = jnp.concatenate([jnp.stack(words), jnp.stack([low, high], 1).reshape(-1)]).astype(jnp.int32)

    keys, values = project_kv(peak_act, w_key, w_value, 512)
    own = attend(0, heads, meta, head_bias, gene, peak, queries, keys, values, F32)
    parts = []
    for slot, (by, kind) in enumerate(steps):
        part = attend(slot + 1, heads, meta, head_bias, gene, peak, far[slot], keys, values, BF16)
        parts.append(lax.ppermute(part, "peak", swap_pairs(count, by, kind)))
    send, keep = mix(len(steps) + 1, meta, own, parts, w_out)
    width = send.shape[1] // 2
    heard = lax.ppermute(send, "gene", [(0, 1), (1, 0), (2, 3), (3, 2)])
    half = keep + heard.astype(F32)
    other = lax.ppermute(half[:, :width].astype(BF16), "gene", [(0, 2), (2, 0), (1, 3), (3, 1)])
    return (half[:, width:] + other.astype(F32)).astype(BF16)


def solution(mesh):
    placed = (
        P("peak", None),
        P("peak", None),
        P(None, "gene"),
        P(None, "gene"),
        P(None, "gene"),
        P("gene", None),
        P("gene"),
        P(),
        P(),
        P(),
    )
    return jax.shard_map(
        on_device, mesh=mesh, in_specs=placed, out_specs=P("peak", "gene"), check_vma=False
    )
```

profile of v0, /device:TPU:3, one launch (start us, length us, event | category | flops | bytes accessed | tf_op | source)
XLA Modules:
  0.0 89.1 jit_solution(429436881672578913)
XLA Ops:
  0.0 0.0 copy-start
  0.0 1.2 %copy-done = bf16[512,1024]{1,0:T(8,128)(2,1)S(1)} copy-done((bf16[512,1024]{1,0:T(8,128)(2,1)S(1)}, bf16[512,1024]{1,0:T(8,128)(2,1)}, u32[]{:S(2)}) %copy-start) | copy-done | bytes 1048600
  1.2 1.5 %convolution_convert_fusion.q_ref = bf16[512,256]{1,0:T(8,128)(2,1)S(1)} fusion(bf16[512,1024]{1,0:T(8,128)(2,1)S(1)} %copy-done, bf16[1024,256]{1,0:T(8,128)(2,1)} %param.12), kind=kOutput, calls=%fused_computation | convolution fusion | flops 268566528 | bytes 1835008 | tf_op jit(solution)/shard_map/dot_general | solution.py:169
  2.7 0.0 copy-start.5
  2.7 3.0 %collective-permute-start.6 = (bf16[512,256]{1,0:T(8,128)(2,1)S(1)}, bf16[512,256]{1,0:T(8,128)(2,1)S(1)}, u32[]{:S(2)}, u32[]{:S(2)}) collective-permute-start(bf16[512,256]{1,0:T(8,128)(2,1)S(1)} %convolution_convert_fusion.q_ref), channel_id=1, source_target_pairs={{0,2},{2,0},{1,3},{3,1},{4,6},{6,4},{5,7},{7,5},{8,10},{10,8},{9,1... | collective-permute-start | bytes 786440 | tf_op jit(solution)/shard_map/ppermute | solution.py:171
  5.7 0.4 collective-permute-start.4
  6.1 7.5 %collective-permute-start.2 = (bf16[512,256]{1,0:T(8,128)(2,1)S(1)}, bf16[512,256]{1,0:T(8,128)(2,1)S(1)}, u32[]{:S(2)}, u32[]{:S(2)}) collective-permute-start(bf16[512,256]{1,0:T(8,128)(2,1)S(1)} %convolution_convert_fusion.q_ref), channel_id=1, source_target_pairs={{2,4},{4,2},{3,5},{5,3},{6,8},{8,6},{7,9},{9,7},{10,12},{12,10},{1... | collective-permute-start | bytes 786440 | tf_op jit(solution)/shard_map/ppermute | solution.py:171
  13.6 3.4 %collective-permute-start = (bf16[512,256]{1,0:T(8,128)(2,1)S(1)}, bf16[512,256]{1,0:T(8,128)(2,1)S(1)}, u32[]{:S(2)}, u32[]{:S(2)}) collective-permute-start(bf16[512,256]{1,0:T(8,128)(2,1)S(1)} %convolution_convert_fusion.q_ref), channel_id=1, source_target_pairs={{1,2},{2,1},{3,4},{4,3},{5,6},{6,5},{7,8},{8,7},{9,10},{10,9},{11,... | collective-permute-start | bytes 786440 | tf_op jit(solution)/shard_map/ppermute | solution.py:171
  17.0 0.7 dynamic-slice_bitcast_fusion.1.peak_ref
  17.7 0.2 slice_reduce_fusion.3
  17.9 0.8 dynamic-slice_bitcast_fusion.gene_ref
  18.7 0.2 slice_reduce_fusion.1
  18.9 0.0 copy-start.2
  18.9 2.2 %copy-done.2 = bf16[2048,1024]{1,0:T(8,128)(2,1)S(1)} copy-done((bf16[2048,1024]{1,0:T(8,128)(2,1)S(1)}, bf16[2048,1024]{1,0:T(8,128)(2,1)}, u32[]{:S(2)}) %copy-start.2) | copy-done | bytes 4194328
  21.1 0.0 copy-start.3
  21.1 1.0 %copy-done.3 = bf16[1024,256]{1,0:T(8,128)(2,1)S(1)} copy-done((bf16[1024,256]{1,0:T(8,128)(2,1)S(1)}, bf16[1024,256]{1,0:T(8,128)(2,1)}, u32[]{:S(2)}) %copy-start.3) | copy-done | bytes 524312
  22.1 0.0 copy-start.4
  22.1 1.0 %copy-done.4 = bf16[1024,256]{1,0:T(8,128)(2,1)S(1)} copy-done((bf16[1024,256]{1,0:T(8,128)(2,1)S(1)}, bf16[1024,256]{1,0:T(8,128)(2,1)}, u32[]{:S(2)}) %copy-start.4) | copy-done | bytes 524312
  23.2 2.9 %project_kv.1 = (bf16[2048,256]{1,0:T(8,128)(2,1)S(1)}, bf16[2048,256]{1,0:T(8,128)(2,1)S(1)}) custom-call(bf16[2048,1024]{1,0:T(8,128)(2,1)S(1)} %copy-done.2, bf16[1024,256]{1,0:T(8,128)(2,1)S(1)} %copy-done.3, bf16[1024,256]{1,0:T(8,128)(2,1)S(1)} %copy-done.4), custom_call_target="tpu_custom_call" | custom-call | flops 2147483648 | bytes 9437184 | tf_op jit(solution)/shard_map/project_kv/pallas_call | solution.py:46
  26.0 0.0 copy-start.6
  26.0 1.0 %copy-done.6 = bf16[2048,256]{1,0:T(8,128)(2,1)} copy-done((bf16[2048,256]{1,0:T(8,128)(2,1)}, bf16[2048,256]{1,0:T(8,128)(2,1)S(1)}, u32[]{:S(2)}) %copy-start.6) | copy-done | bytes 1048600
  27.0 0.9 %select_reduce_fusion.1 = (s32[20]{0:T(128)S(1)}, s32[20]{0:T(128)S(1)}) fusion(s32[16]{0:T(128)S(1)} %iota_add_fusion, s32[20]{0:T(128)S(1)} %get-tuple-element.14, s32[16]{0:T(128)S(1)} %get-tuple-element.16, s32[16]{0:T(128)S(1)} %get-tuple-element.15, s32[20]{0:T(128)S(1)} %get-tuple-element.13, s32[256,1024]{1,0:T(8,128)} %param.17, s32[]{:T(128)S(6)} %min.4, ...), kind=kLoop, calls=%fused_computation.8 | loop fusion | flops 2840 | bytes 1800 | tf_op jit(solution)/shard_map/reduce_min | solution.py:180
  28.0 0.1 copy.12
  28.1 0.1 reshape.13
  28.3 0.1 concatenate.3.meta_ref
  28.3 0.0 collective-permute-done.q_ref
  28.3 0.0 copy-done.5
  28.4 0.0 copy-start.7
  28.4 1.2 %copy-done.7 = bf16[2048,256]{1,0:T(8,128)(2,1)S(1)} copy-done((bf16[2048,256]{1,0:T(8,128)(2,1)S(1)}, bf16[2048,256]{1,0:T(8,128)(2,1)}, u32[]{:S(2)}) %copy-start.7) | copy-done | bytes 1048600
  29.6 4.0 %attend_1.1 = bf16[512,256]{1,0:T(8,128)(2,1)S(1)} custom-call(s32[48]{0:T(128)S(1)} %concatenate.3.meta_ref, f32[2]{0:T(128)S(1)} %copy-done.5, s32[20,128]{1,0:T(8,128)S(1)} %dynamic-slice_bitcast_fusion.gene_ref, s32[16,128]{1,0:T(8,128)S(1)} %dynamic-slice_bitcast_fusion.1.peak_ref, bf16[512,256]{1,0:T(8,128)(2,1)S(1)} %collective-permute-done.q_ref, ...), custom_call_target="tpu_custom_call" | custom-call | flops 1073741824 | bytes 2621440 | tf_op jit(solution)/shard_map/attend_1/pallas_call | solution.py:104
  33.6 6.7 %collective-permute-start.1 = (bf16[512,256]{1,0:T(8,128)(2,1)S(1)}, bf16[512,256]{1,0:T(8,128)(2,1)S(1)}, u32[]{:S(2)}, u32[]{:S(2)}) collective-permute-start(bf16[512,256]{1,0:T(8,128)(2,1)S(1)} %attend_1.1), channel_id=1, source_target_pairs={{1,2},{2,1},{3,4},{4,3},{5,6},{6,5},{7,8},{8,7},{9,10},{10,9},{11,... | collective-permute-start | bytes 786440 | tf_op jit(solution)/shard_map/ppermute | solution.py:198
  40.3 0.0 collective-permute-done.2.q_ref
  40.3 4.0 %attend_2.1 = bf16[512,256]{1,0:T(8,128)(2,1)S(1)} custom-call(s32[48]{0:T(128)S(1)} %concatenate.3.meta_ref, f32[2]{0:T(128)S(1)} %copy-done.5, s32[20,128]{1,0:T(8,128)S(1)} %dynamic-slice_bitcast_fusion.gene_ref, s32[16,128]{1,0:T(8,128)S(1)} %dynamic-slice_bitcast_fusion.1.peak_ref, bf16[512,256]{1,0:T(8,128)(2,1)S(1)} %collective-permute-done.2.q_ref, ...), custom_call_target="tpu_custom_call" | custom-call | flops 1073741824 | bytes 2621440 | tf_op jit(solution)/shard_map/attend_2/pallas_call | solution.py:104
  44.4 1.9 %collective-permute-start.3 = (bf16[512,256]{1,0:T(8,128)(2,1)S(1)}, bf16[512,256]{1,0:T(8,128)(2,1)S(1)}, u32[]{:S(2)}, u32[]{:S(2)}) collective-permute-start(bf16[512,256]{1,0:T(8,128)(2,1)S(1)} %attend_2.1), channel_id=1, source_target_pairs={{2,4},{4,2},{3,5},{5,3},{6,8},{8,6},{7,9},{9,7},{10,12},{12,10},{1... | collective-permute-start | bytes 786440 | tf_op jit(solution)/shard_map/ppermute | solution.py:198
  46.3 0.0 collective-permute-done.4.q_ref
  46.3 4.0 %attend_3.1 = bf16[512,256]{1,0:T(8,128)(2,1)S(1)} custom-call(s32[48]{0:T(128)S(1)} %concatenate.3.meta_ref, f32[2]{0:T(128)S(1)} %copy-done.5, s32[20,128]{1,0:T(8,128)S(1)} %dynamic-slice_bitcast_fusion.gene_ref, s32[16,128]{1,0:T(8,128)S(1)} %dynamic-slice_bitcast_fusion.1.peak_ref, bf16[512,256]{1,0:T(8,128)(2,1)S(1)} %collective-permute-done.4.q_ref, ...), custom_call_target="tpu_custom_call" | custom-call | flops 1073741824 | bytes 2621440 | tf_op jit(solution)/shard_map/attend_3/pallas_call | solution.py:104
  50.4 0.0 copy-start.1
  50.4 2.1 %collective-permute-start.5 = (bf16[512,256]{1,0:T(8,128)(2,1)S(1)}, bf16[512,256]{1,0:T(8,128)(2,1)S(1)}, u32[]{:S(2)}, u32[]{:S(2)}) collective-permute-start(bf16[512,256]{1,0:T(8,128)(2,1)S(1)} %attend_3.1), channel_id=1, source_target_pairs={{0,1},{1,0},{2,3},{3,2},{4,5},{5,4},{6,7},{7,6},{8,9},{9,8},{10,11... | collective-permute-start | bytes 786440 | tf_op jit(solution)/shard_map/ppermute | solution.py:198
  52.5 0.0 collective-permute-done.6.q_ref
  52.5 3.2 %attend_4.1 = bf16[512,256]{1,0:T(8,128)(2,1)S(1)} custom-call(s32[48]{0:T(128)S(1)} %concatenate.3.meta_ref, f32[2]{0:T(128)S(1)} %copy-done.5, s32[20,128]{1,0:T(8,128)S(1)} %dynamic-slice_bitcast_fusion.gene_ref, s32[16,128]{1,0:T(8,128)S(1)} %dynamic-slice_bitcast_fusion.1.peak_ref, bf16[512,256]{1,0:T(8,128)(2,1)S(1)} %collective-permute-done.6.q_ref, ...), custom_call_target="tpu_custom_call" | custom-call | flops 1073741824 | bytes 2621440 | tf_op jit(solution)/shard_map/attend_4/pallas_call | solution.py:104
  55.7 0.1 collective-permute-start.7
  55.8 4.0 %attend_0.1.own_ref = f32[512,256]{1,0:T(8,128)S(1)} custom-call(s32[48]{0:T(128)S(1)} %concatenate.3.meta_ref, f32[2]{0:T(128)S(1)} %copy-done.5, s32[20,128]{1,0:T(8,128)S(1)} %dynamic-slice_bitcast_fusion.gene_ref, s32[16,128]{1,0:T(8,128)S(1)} %dynamic-slice_bitcast_fusion.1.peak_ref, bf16[512,256]{1,0:T(8,128)(2,1)S(1)} %convolution_convert_fusion.q_ref, ...), custom_call_target="tpu_custom_call" | custom-call | flops 1073741824 | bytes 2621440 | tf_op jit(solution)/shard_map/attend_0/pallas_call | solution.py:104
  59.8 0.0 collective-permute-done.1.r1
  59.8 0.0 collective-permute-done.3.r2
  59.9 0.0 collective-permute-done.5.r3
  59.9 2.6 %collective-permute-done.7.r4 = bf16[512,256]{1,0:T(8,128)(2,1)S(1)} collective-permute-done((bf16[512,256]{1,0:T(8,128)(2,1)S(1)}, bf16[512,256]{1,0:T(8,128)(2,1)S(1)}, u32[]{:S(2)}, u32[]{:S(2)}) %collective-permute-start.7) | collective-permute-done | bytes 262176 | tf_op jit(solution)/shard_map/ppermute | solution.py:198
  62.5 0.0 copy-done.1
  62.5 1.0 %mix.1 = (bf16[512,512]{1,0:T(8,128)(2,1)S(1)}, f32[512,512]{1,0:T(8,128)S(1)}) custom-call(s32[48]{0:T(128)S(1)} %concatenate.3.meta_ref, f32[512,256]{1,0:T(8,128)S(1)} %attend_0.1.own_ref, bf16[512,256]{1,0:T(8,128)(2,1)S(1)} %collective-permute-done.1.r1, bf16[512,256]{1,0:T(8,128)(2,1)S(1)} %collective-permute-done.3.r2, ...), custom_call_target="tpu_custom_call" | custom-call | flops 268435456 | bytes 2097152 | tf_op jit(solution)/shard_map/mix/pallas_call | solution.py:136
  63.6 3.9 %collective-permute-start.8 = (bf16[512,512]{1,0:T(8,128)(2,1)S(1)}, bf16[512,512]{1,0:T(8,128)(2,1)S(1)}, u32[]{:S(2)}, u32[]{:S(2)}) collective-permute-start(bf16[512,512]{1,0:T(8,128)(2,1)S(1)} %get-tuple-element.12), channel_id=1, source_target_pairs={{0,64},{64,0},{128,192},{192,128},{1,65},{65,1},{129,193},{193,129... | collective-permute-start | bytes 1572872 | tf_op jit(solution)/shard_map/ppermute | solution.py:201
  67.4 1.5 %collective-permute-done.8 = bf16[512,512]{1,0:T(8,128)(2,1)S(1)} collective-permute-done((bf16[512,512]{1,0:T(8,128)(2,1)S(1)}, bf16[512,512]{1,0:T(8,128)(2,1)S(1)}, u32[]{:S(2)}, u32[]{:S(2)}) %collective-permute-start.8) | collective-permute-done | bytes 524320 | tf_op jit(solution)/shard_map/ppermute | solution.py:201
  69.0 0.2 convert_add_fusion
  69.2 7.0 %collective-permute-start.9 = (bf16[512,256]{1,0:T(8,128)(2,1)S(1)}, bf16[512,256]{1,0:T(8,128)(2,1)S(1)}, u32[]{:S(2)}, u32[]{:S(2)}) collective-permute-start(bf16[512,256]{1,0:T(8,128)(2,1)S(1)} %slice.39), channel_id=1, source_target_pairs={{0,128},{128,0},{64,192},{192,64},{1,129},{129,1},{65,193},{193,65... | collective-permute-start | bytes 786440 | tf_op jit(solution)/shard_map/ppermute | solution.py:203
  76.2 12.1 %collective-permute-done.9 = bf16[512,256]{1,0:T(8,128)(2,1)S(1)} collective-permute-done((bf16[512,256]{1,0:T(8,128)(2,1)S(1)}, bf16[512,256]{1,0:T(8,128)(2,1)S(1)}, u32[]{:S(2)}, u32[]{:S(2)}) %collective-permute-start.9) | collective-permute-done | bytes 262176 | tf_op jit(solution)/shard_map/ppermute | solution.py:203
  88.3 0.8 fusion
  (4 shorter events, 0.1 us)
Async XLA Ops:
  0.0 1.2 %copy-start = (bf16[512,1024]{1,0:T(8,128)(2,1)S(1)}, bf16[512,1024]{1,0:T(8,128)(2,1)}, u32[]{:S(2)}) copy-start(bf16[512,1024]{1,0:T(8,128)(2,1)} %param.10) | copy-start | bytes 3145732
  2.7 25.6 %copy-start.5 = (f32[2]{0:T(128)S(1)}, f32[2]{0:T(128)}, u32[]{:S(2)}) copy-start(f32[2]{0:T(128)} %bias_ref.9) | copy-start | bytes 28
  2.7 49.8 %collective-permute-start.6 = (bf16[512,256]{1,0:T(8,128)(2,1)S(1)}, bf16[512,256]{1,0:T(8,128)(2,1)S(1)}, u32[]{:S(2)}, u32[]{:S(2)}) collective-permute-start(bf16[512,256]{1,0:T(8,128)(2,1)S(1)} %convolution_convert_fusion.q_ref), channel_id=1, source_target_pairs={{0,2},{2,0},{1,3},{3,1},{4,6},{6,4},{5,7},{7,5},{8,10},{10,8},{9,1... | collective-permute-start | bytes 786440 | tf_op jit(solution)/shard_map/ppermute | solution.py:171
  5.7 40.6 %collective-permute-start.4 = (bf16[512,256]{1,0:T(8,128)(2,1)S(1)}, bf16[512,256]{1,0:T(8,128)(2,1)S(1)}, u32[]{:S(2)}, u32[]{:S(2)}) collective-permute-start(bf16[512,256]{1,0:T(8,128)(2,1)S(1)} %convolution_convert_fusion.q_ref), channel_id=1, source_target_pairs={{0,1},{1,0},{2,3},{3,2},{4,5},{5,4},{6,7},{7,6},{8,9},{9,8},{10,11... | collective-permute-start | bytes 786440 | tf_op jit(solution)/shard_map/ppermute | solution.py:171
  6.1 34.2 %collective-permute-start.2 = (bf16[512,256]{1,0:T(8,128)(2,1)S(1)}, bf16[512,256]{1,0:T(8,128)(2,1)S(1)}, u32[]{:S(2)}, u32[]{:S(2)}) collective-permute-start(bf16[512,256]{1,0:T(8,128)(2,1)S(1)} %convolution_convert_fusion.q_ref), channel_id=1, source_target_pairs={{2,4},{4,2},{3,5},{5,3},{6,8},{8,6},{7,9},{9,7},{10,12},{12,10},{1... | collective-permute-start | bytes 786440 | tf_op jit(solution)/shard_map/ppermute | solution.py:171
  13.6 14.7 %collective-permute-start = (bf16[512,256]{1,0:T(8,128)(2,1)S(1)}, bf16[512,256]{1,0:T(8,128)(2,1)S(1)}, u32[]{:S(2)}, u32[]{:S(2)}) collective-permute-start(bf16[512,256]{1,0:T(8,128)(2,1)S(1)} %convolution_convert_fusion.q_ref), channel_id=1, source_target_pairs={{1,2},{2,1},{3,4},{4,3},{5,6},{6,5},{7,8},{8,7},{9,10},{10,9},{11,... | collective-permute-start | bytes 786440 | tf_op jit(solution)/shard_map/ppermute | solution.py:171
  18.9 2.2 %copy-start.2 = (bf16[2048,1024]{1,0:T(8,128)(2,1)S(1)}, bf16[2048,1024]{1,0:T(8,128)(2,1)}, u32[]{:S(2)}) copy-start(bf16[2048,1024]{1,0:T(8,128)(2,1)} %act_ref.1) | copy-start | bytes 12582916
  21.1 1.0 %copy-start.3 = (bf16[1024,256]{1,0:T(8,128)(2,1)S(1)}, bf16[1024,256]{1,0:T(8,128)(2,1)}, u32[]{:S(2)}) copy-start(bf16[1024,256]{1,0:T(8,128)(2,1)} %wk_ref.1) | copy-start | bytes 1572868
  22.1 1.0 %copy-start.4 = (bf16[1024,256]{1,0:T(8,128)(2,1)S(1)}, bf16[1024,256]{1,0:T(8,128)(2,1)}, u32[]{:S(2)}) copy-start(bf16[1024,256]{1,0:T(8,128)(2,1)} %wv_ref.1) | copy-start | bytes 1572868
  26.0 1.0 %copy-start.6 = (bf16[2048,256]{1,0:T(8,128)(2,1)}, bf16[2048,256]{1,0:T(8,128)(2,1)S(1)}, u32[]{:S(2)}) copy-start(bf16[2048,256]{1,0:T(8,128)(2,1)S(1)} %get-tuple-element.10.v_ref) | copy-start | bytes 3145732
  28.4 1.2 %copy-start.7 = (bf16[2048,256]{1,0:T(8,128)(2,1)S(1)}, bf16[2048,256]{1,0:T(8,128)(2,1)}, u32[]{:S(2)}) copy-start(bf16[2048,256]{1,0:T(8,128)(2,1)} %copy-done.6) | copy-start | bytes 3145732
  33.6 26.2 %collective-permute-start.1 = (bf16[512,256]{1,0:T(8,128)(2,1)S(1)}, bf16[512,256]{1,0:T(8,128)(2,1)S(1)}, u32[]{:S(2)}, u32[]{:S(2)}) collective-permute-start(bf16[512,256]{1,0:T(8,128)(2,1)S(1)} %attend_1.1), channel_id=1, source_target_pairs={{1,2},{2,1},{3,4},{4,3},{5,6},{6,5},{7,8},{8,7},{9,10},{10,9},{11,... | collective-permute-start | bytes 786440 | tf_op jit(solution)/shard_map/ppermute | solution.py:198
  44.4 15.5 %collective-permute-start.3 = (bf16[512,256]{1,0:T(8,128)(2,1)S(1)}, bf16[512,256]{1,0:T(8,128)(2,1)S(1)}, u32[]{:S(2)}, u32[]{:S(2)}) collective-permute-start(bf16[512,256]{1,0:T(8,128)(2,1)S(1)} %attend_2.1), channel_id=1, source_target_pairs={{2,4},{4,2},{3,5},{5,3},{6,8},{8,6},{7,9},{9,7},{10,12},{12,10},{1... | collective-permute-start | bytes 786440 | tf_op jit(solution)/shard_map/ppermute | solution.py:198
  50.4 12.2 %copy-start.1 = (bf16[256,1024]{1,0:T(8,128)(2,1)S(1)}, bf16[256,1024]{1,0:T(8,128)(2,1)}, u32[]{:S(2)}) copy-start(bf16[256,1024]{1,0:T(8,128)(2,1)} %w_ref.1) | copy-start | bytes 1572868
  50.4 9.5 %collective-permute-start.5 = (bf16[512,256]{1,0:T(8,128)(2,1)S(1)}, bf16[512,256]{1,0:T(8,128)(2,1)S(1)}, u32[]{:S(2)}, u32[]{:S(2)}) collective-permute-start(bf16[512,256]{1,0:T(8,128)(2,1)S(1)} %attend_3.1), channel_id=1, source_target_pairs={{0,1},{1,0},{2,3},{3,2},{4,5},{5,4},{6,7},{7,6},{8,9},{9,8},{10,11... | collective-permute-start | bytes 786440 | tf_op jit(solution)/shard_map/ppermute | solution.py:198
  55.7 6.8 %collective-permute-start.7 = (bf16[512,256]{1,0:T(8,128)(2,1)S(1)}, bf16[512,256]{1,0:T(8,128)(2,1)S(1)}, u32[]{:S(2)}, u32[]{:S(2)}) collective-permute-start(bf16[512,256]{1,0:T(8,128)(2,1)S(1)} %attend_4.1), channel_id=1, source_target_pairs={{0,2},{2,0},{1,3},{3,1},{4,6},{6,4},{5,7},{7,5},{8,10},{10,8},{9,1... | collective-permute-start | bytes 786440 | tf_op jit(solution)/shard_map/ppermute | solution.py:198
  63.6 5.4 %collective-permute-start.8 = (bf16[512,512]{1,0:T(8,128)(2,1)S(1)}, bf16[512,512]{1,0:T(8,128)(2,1)S(1)}, u32[]{:S(2)}, u32[]{:S(2)}) collective-permute-start(bf16[512,512]{1,0:T(8,128)(2,1)S(1)} %get-tuple-element.12), channel_id=1, source_target_pairs={{0,64},{64,0},{128,192},{192,128},{1,65},{65,1},{129,193},{193,129... | collective-permute-start | bytes 1572872 | tf_op jit(solution)/shard_map/ppermute | solution.py:201
  69.2 19.1 %collective-permute-start.9 = (bf16[512,256]{1,0:T(8,128)(2,1)S(1)}, bf16[512,256]{1,0:T(8,128)(2,1)S(1)}, u32[]{:S(2)}, u32[]{:S(2)}) collective-permute-start(bf16[512,256]{1,0:T(8,128)(2,1)S(1)} %slice.39), channel_id=1, source_target_pairs={{0,128},{128,0},{64,192},{192,64},{1,129},{129,1},{65,193},{193,65... | collective-permute-start | bytes 786440 | tf_op jit(solution)/shard_map/ppermute | solution.py:203
where the time goes:
time: 89.6 us; the launch traced here: 89.1 us
  starting transfers between devices  36 us (40%)
  Pallas kernels  23.2 us (26%)
  waiting for transfers between devices  16.3 us (18%)
  local copies, waits for them, and re-layouts  9.86 us (11%)
  other arithmetic  1.88 us (2%)
  matrix products  1.48 us (2%)
    pallas_call x5, Pallas kernels, attend(): pl.pallas_call(functools.partial(attend_kernel, slot, heads), in_specs=[S...  19.3 us
    ppermute x4, starting transfers between devices, on_device(): lax.ppermute(queries, 'peak', swap_pairs(count, by, kind))  14.3 us
    ppermute x1, waiting for transfers between devices, on_device(): lax.ppermute(half[:, :width].astype(BF16), 'gene', [(0, 2), (2, 0), (1, 3...  12.1 us
    ppermute x4, starting transfers between devices, on_device(): parts.append(lax.ppermute(part, 'peak', swap_pairs(count, by, kind)))  10.9 us
    unnamed x16, local copies, waits for them, and re-layouts  7.69 us
    ppermute x1, starting transfers between devices, on_device(): lax.ppermute(half[:, :width].astype(BF16), 'gene', [(0, 2), (2, 0), (1, 3...  6.99 us
    ppermute x1, starting transfers between devices, on_device(): heard = lax.ppermute(send, 'gene', [(0, 1), (1, 0), (2, 3), (3, 2)])  3.86 us
    pallas_call x1, Pallas kernels, project_kv(): pl.pallas_call(kv_kernel, grid=(total // rows,), in_specs=[pl.BlockSpec((...  2.86 us
  transfers between devices with their start and end apart: 10, of which 3 were waited for; matrix products, arithmetic and copies ran while one was open for 3% of the time, Pallas kernels for 25%

commit v1 on v0

v1 whole, which is shorter than its diff:
```python
import functools
import math

import jax
import jax.numpy as jnp
from jax import lax
from jax.experimental import pallas as pl
from jax.experimental.pallas import tpu as pltpu
from jax.sharding import PartitionSpec as P


TILE = 128
REACH = 2
CHUNK = 512
SPAN = 32
F32 = jnp.float32
BF16 = jnp.bfloat16
I32 = jnp.int32
VMEM = pl.BlockSpec(memory_space=pltpu.VMEM)
SMEM = pl.BlockSpec(memory_space=pltpu.SMEM)
ANY = pl.BlockSpec(memory_space=pl.ANY)
PARAMS = pltpu.CompilerParams(vmem_limit_bytes=20 << 20)


def swap_pairs(genes, count, by):
    pairs = []
    for g in range(genes):
        for i in range(count - by):
            if (i // by) % 2 == g % 2:
                a, b = g * count + i, g * count + i + by
                pairs += [(a, b), (b, a)]
    return pairs


def core_swap(x):
    return lax.ppermute(x, "gene", [(0, 1), (1, 0), (2, 3), (3, 2)])


def cost(flops, arrays):
    return pl.CostEstimate(
        flops=flops, bytes_accessed=sum(a.size * a.dtype.itemsize for a in arrays), transcendentals=0
    )


def window_origin(gene_tiles):
    me, count = lax.axis_index("peak"), lax.axis_size("peak")
    first = jnp.maximum((me - REACH) * gene_tiles, 0)
    return jnp.minimum((first // 8) * 8, count * gene_tiles - SPAN)


def query_kernel(act_ref, w_ref, q_ref):
    q_ref[...] = jnp.dot(act_ref[...], w_ref[...], preferred_element_type=F32).astype(BF16)


def query_join_kernel(act_ref, w_ref, own_ref, q_ref):
    width = w_ref.shape[1]
    q_ref[:, :width] = own_ref[...]
    q_ref[:, width:] = jnp.dot(act_ref[...], w_ref[...], preferred_element_type=F32).astype(BF16)


def project_queries(act, own, other):
    rows, width = act.shape[0], own.shape[1]
    half = pl.pallas_call(
        query_kernel,
        in_specs=[VMEM] * 2,
        out_specs=VMEM,
        out_shape=jax.ShapeDtypeStruct((rows, width), BF16),
        cost_estimate=cost(2 * act.size * width, [act, own]),
        name="project_queries",
    )(act, own)
    return pl.pallas_call(
        query_join_kernel,
        in_specs=[VMEM] * 3,
        out_specs=VMEM,
        out_shape=jax.ShapeDtypeStruct((rows, 2 * width), BF16),
        cost_estimate=cost(8_000_000_000, [act, own]),
        compiler_params=PARAMS,
        name="join_queries",
    )(act, other, half)


def kv_kernel(
    gene_tiles, act_ref, wk1, wk2, wv1, wv2, mask_hbm, gene_hbm, peak_hbm,
    k_ref, v_ref, runs_ref, gene_ref, peak_ref, mask_ref, turned_ref, sems,
):
    me = lax.axis_index("peak")
    tiles = peak_ref.shape[0]
    origin = pl.multiple_of(window_origin(gene_tiles), 8)
    per_block = TILE // tiles
    columns = pl.multiple_of((me // per_block) * TILE, TILE)
    copies = [
        pltpu.make_async_copy(
            mask_hbm.at[pl.ds(origin, SPAN), pl.ds(columns, TILE)], mask_ref, sems.at[0]
        ),
        pltpu.make_async_copy(gene_hbm.at[pl.ds(origin, SPAN), :], gene_ref, sems.at[1]),
        pltpu.make_async_copy(
            peak_hbm.at[pl.ds(pl.multiple_of(me * tiles, 8), tiles), :], peak_ref, sems.at[2]
        ),
    ]
    for copy in copies:
        copy.start()
    width = wk1.shape[1]

    def block(i, carry):
        rows = pl.ds(pl.multiple_of(i * CHUNK, CHUNK), CHUNK)
        act = act_ref[rows, :]
        k_ref[rows, :width] = jnp.dot(act, wk1[...], preferred_element_type=F32).astype(BF16)
        v_ref[rows, :width] = jnp.dot(act, wv1[...], preferred_element_type=F32).astype(BF16)
        k_ref[rows, width:] = jnp.dot(act, wk2[...], preferred_element_type=F32).astype(BF16)
        v_ref[rows, width:] = jnp.dot(act, wv2[...], preferred_element_type=F32).astype(BF16)
        return carry

    lax.fori_loop(0, act_ref.shape[0] // CHUNK, block, 0)
    for copy in copies:
        copy.wait()
    blank = jnp.zeros((TILE - SPAN, TILE), I32)
    turned_ref[...] = jnp.concatenate([mask_ref[...], blank], 0).T
    allowed = turned_ref[pl.ds(pl.multiple_of((me % per_block) * tiles, 8), tiles), :]
    tags = jnp.concatenate([gene_ref[...], blank], 0).T
    peak = peak_ref[...]
    live = (
        (allowed > 0) & (tags[:1, :] <= peak[:, TILE - 1 :]) & (peak[:, :1] <= tags[TILE - 1 :, :])
    )
    place = lax.broadcasted_iota(I32, live.shape, 0)
    runs_ref[...] = jnp.zeros_like(runs_ref)
    runs_ref[0:1, :] = jnp.min(jnp.where(live, place, tiles), axis=0, keepdims=True)
    runs_ref[1:2, :] = jnp.max(jnp.where(live, place + 1, 0), axis=0, keepdims=True)


def project_kv(gene_tiles, act, wk, wv, mask, gene, peak):
    total, depth = act.shape
    width = 2 * wk[0].shape[1]
    tiles = total // TILE
    return pl.pallas_call(
        functools.partial(kv_kernel, gene_tiles),
        in_specs=[VMEM] * 5 + [ANY] * 3,
        out_specs=[VMEM] * 5,
        out_shape=[
            jax.ShapeDtypeStruct((total, width), BF16),
            jax.ShapeDtypeStruct((total, width), BF16),
            jax.ShapeDtypeStruct((8, TILE), I32),
            jax.ShapeDtypeStruct((SPAN, TILE), I32),
            jax.ShapeDtypeStruct((tiles, TILE), I32),
        ],
        scratch_shapes=[
            pltpu.VMEM((SPAN, TILE), I32),
            pltpu.VMEM((TILE, TILE), I32),
            pltpu.SemaphoreType.DMA((3,)),
        ],
        cost_estimate=cost(4 * total * depth * width, [act, act]),
        compiler_params=PARAMS,
        name="project_kv",
    )(act, *wk, *wv, mask, gene, peak)


def attend_kernel(
    by, heads, runs_ref, own_bias, other_bias, gene_ref, peak_ref, q_ref, k_ref, v_ref, o_ref, acc
):
    tiles = q_ref.shape[0] // TILE
    per_chunk = CHUNK // TILE
    dim = TILE
    scale = 0.5 / math.sqrt(dim)
    me, count = lax.axis_index("peak"), lax.axis_size("peak")
    source = me
    if by:
        kind = lax.axis_index("gene") % 2
        source = jnp.where((me // by) % 2 == kind, me + by, me - by)
    valid = (source >= 0) & (source < count)
    base = jnp.where(valid, source * tiles - window_origin(tiles), 0)
    lows = [runs_ref[0, base + i] for i in range(tiles)]
    highs = [runs_ref[1, base + i] for i in range(tiles)]
    low = functools.reduce(jnp.minimum, lows)
    high = functools.reduce(jnp.maximum, highs)
    first = low // per_chunk
    last = jnp.where(valid, (high + per_chunk - 1) // per_chunk, first)
    acc[...] = jnp.zeros_like(acc)
    tags = [
        jnp.broadcast_to(gene_ref[pl.ds(base + i, 1), :], (TILE, TILE)).T for i in range(tiles)
    ]
    local = own_bias.shape[0]

    def chunk(c, carry):
        rows = pl.ds(pl.multiple_of(c * CHUNK, CHUNK), CHUNK)
        peaks = [peak_ref[pl.ds(c * per_chunk + j, 1), :] for j in range(per_chunk)]
        inside = [
            [
                jnp.where((c * per_chunk + j >= lows[i]) & (c * per_chunk + j < highs[i]), peaks[j], -1)
                for j in range(per_chunk)
            ]
            for i in range(tiles)
        ]
        for h in range(heads):
            cols = slice(h * dim, (h + 1) * dim)
            bias = own_bias[h] if h < local else other_bias[h - local]
            scores = lax.dot_general(
                q_ref[:, cols], k_ref[rows, cols], (((1,), (1,)), ((), ())), preferred_element_type=F32
            )
            twice = jnp.tanh(scores * scale + 0.5 * bias) + 1.0
            bands = []
            for i in range(tiles):
                band = []
                for j in range(per_chunk):
                    part = twice[i * TILE : (i + 1) * TILE, j * TILE : (j + 1) * TILE]
                    band.append(jnp.where(tags[i] == inside[i][j], part, 0.0))
                bands.append(jnp.concatenate(band, 1))
            weights = jnp.concatenate(bands, 0).astype(BF16)
            acc[:, cols] += jnp.dot(weights, v_ref[rows, cols], preferred_element_type=F32)
        return carry

    lax.fori_loop(first, last, chunk, 0)
    o_ref[...] = (acc[...] * 0.5).astype(o_ref.dtype)


def attend(by, heads, tables, q, k, v, dtype):
    runs, own_bias, other_bias, gene, peak = tables
    shape = (q.shape[0], heads * TILE)
    return pl.pallas_call(
        functools.partial(attend_kernel, by, heads),
        in_specs=[SMEM] * 3 + [VMEM] * 5,
        out_specs=VMEM,
        out_shape=jax.ShapeDtypeStruct(shape, dtype),
        scratch_shapes=[pltpu.VMEM(shape, F32)],
        cost_estimate=cost(4 * q.shape[0] * k.shape[0] * heads * TILE, [q, k, v, q]),
        compiler_params=PARAMS,
    )(runs, own_bias, other_bias, gene, peak, q, k, v)


def mix_kernel(own_ref, near_ref, far_ref, w1, w2, send_ref, keep_ref):
    width = w1.shape[1] // 4
    depth = w1.shape[0]
    me = lax.axis_index("gene")
    mine = own_ref[...] + near_ref[:, :depth].astype(F32) + far_ref[:, :depth].astype(F32)
    theirs = near_ref[:, depth:].astype(F32) + far_ref[:, depth:].astype(F32)
    mine, theirs = mine.astype(BF16), theirs.astype(BF16)

    def share(block):
        cols = pl.ds(pl.multiple_of(block * width, width), width)
        return jnp.dot(mine, w1[:, cols], preferred_element_type=F32) + jnp.dot(
            theirs, w2[:, cols], preferred_element_type=F32
        )

    send_ref[:, :width] = share(me ^ 3).astype(BF16)
    send_ref[:, width:] = share(me ^ 1).astype(BF16)
    keep_ref[:, :width] = share(me ^ 2)
    keep_ref[:, width:] = share(me)


def mix(own, near, far, w1, w2):
    shape = (own.shape[0], w1.shape[1] // 2)
    return pl.pallas_call(
        mix_kernel,
        in_specs=[VMEM] * 5,
        out_specs=[VMEM, VMEM],
        out_shape=[jax.ShapeDtypeStruct(shape, BF16), jax.ShapeDtypeStruct(shape, F32)],
        cost_estimate=cost(4 * own.shape[0] * w1.size, [own, w1, w2, own, own]),
        compiler_params=PARAMS,
        name="mix",
    )(own, near, far, w1, w2)


def on_device(
    gene_act,
    peak_act,
    w_query,
    w_key,
    w_value,
    w_out,
    head_bias,
    block_mask,
    gene_chrom,
    peak_chrom,
):
    gene_tiles = gene_act.shape[0] // TILE
    local = head_bias.shape[0]
    count, genes = lax.axis_size("peak"), lax.axis_size("gene")

    def travel(x, by):
        return lax.ppermute(x, ("gene", "peak"), swap_pairs(genes, count, by))

    queries = project_queries(gene_act, w_query, core_swap(w_query))
    near, far = travel(queries, 1), travel(queries, 2)
    keys, values, runs, gene, peak = project_kv(
        gene_tiles,
        peak_act,
        (w_key, core_swap(w_key)),
        (w_value, core_swap(w_value)),
        block_mask,
        gene_chrom.reshape(-1, TILE),
        peak_chrom.reshape(-1, TILE),
    )
    tables = (runs, head_bias, core_swap(head_bias), gene, peak)
    near = travel(attend(1, 2 * local, tables, near, keys, values, BF16), 1)
    far = travel(attend(2, 2 * local, tables, far, keys, values, BF16), 2)
    own = attend(0, local, tables, queries, keys, values, F32)
    send, keep = mix(own, near, far, w_out, core_swap(w_out))
    width = send.shape[1] // 2
    half = keep + core_swap(send).astype(F32)
    other = lax.ppermute(half[:, :width].astype(BF16), "gene", [(0, 2), (2, 0), (1, 3), (3, 1)])
    return (half[:, width:] + other.astype(F32)).astype(BF16)


def solution(mesh):
    placed = (
        P("peak", None),
        P("peak", None),
        P(None, "gene"),
        P(None, "gene"),
        P(None, "gene"),
        P("gene", None),
        P("gene"),
        P(),
        P(),
        P(),
    )
    return jax.shard_map(
        on_device, mesh=mesh, in_specs=placed, out_specs=P("peak", "gene"), check_vma=False
    )
```

time: 89.6 us -> 83.6 us (0.933)
  the two profiles are of different devices: /device:TPU:3 before, /device:TPU:6 now
where the time goes in v1:
time: 83.6 us; the launch traced here: 83.3 us
  starting transfers between devices  29.9 us (36%)
  Pallas kernels  26.1 us (31%)
  waiting for transfers between devices  23.9 us (29%)
  local copies, waits for them, and re-layouts  2.25 us (3%)
  other arithmetic  0.94 us (1%)
    ppermute x4, starting transfers between devices, travel(): return lax.ppermute(x, ('gene', 'peak'), swap_pairs(genes, count, by))  17.2 us
    pallas_call x3, Pallas kernels, attend(): pl.pallas_call(functools.partial(attend_kernel, by, heads), in_specs=[SME...  17.2 us
    ppermute x1, waiting for transfers between devices, on_device(): lax.ppermute(half[:, :width].astype(BF16), 'gene', [(0, 2), (2, 0), (1, 3...  11.8 us
    ppermute x4, waiting for transfers between devices, travel(): return lax.ppermute(x, ('gene', 'peak'), swap_pairs(genes, count, by))  10.2 us
    ppermute x1, starting transfers between devices, on_device(): lax.ppermute(half[:, :width].astype(BF16), 'gene', [(0, 2), (2, 0), (1, 3...  7.37 us
    ppermute x6, starting transfers between devices, core_swap(): return lax.ppermute(x, 'gene', [(0, 1), (1, 0), (2, 3), (3, 2)])  5.36 us
    pallas_call x1, Pallas kernels, project_kv(): pl.pallas_call(functools.partial(kv_kernel, gene_tiles), in_specs=[VMEM]...  5.25 us
    pallas_call x1, Pallas kernels, project_queries(): pl.pallas_call(query_kernel, in_specs=[VMEM] * 2, out_specs=VMEM, out_sha...  2.5 us
  transfers between devices with their start and end apart: 11, of which 5 were waited for; matrix products, arithmetic and copies ran while one was open for 0% of the time, Pallas kernels for 30%

profile of v1, /device:TPU:6, one launch (start us, length us, event | category | flops | bytes accessed | tf_op | source)
XLA Modules:
  0.0 83.3 jit_solution(5656064772529858480)
XLA Ops:
  0.0 0.0 collective-permute-start.3
  0.0 0.5 collective-permute-start
  0.5 0.0 collective-permute-start.1
  0.5 2.5 %project_queries.1.own_ref = bf16[512,256]{1,0:T(8,128)(2,1)} custom-call(bf16[512,1024]{1,0:T(8,128)(2,1)} %act_ref.5, bf16[1024,256]{1,0:T(8,128)(2,1)} %w_ref.1), custom_call_target="tpu_custom_call" | custom-call | flops 268435456 | bytes 1572864 | tf_op jit(solution)/shard_map/project_queries/pallas_call | solution.py:63
  3.0 0.0 collective-permute-done.3.w_ref
  3.0 0.0 copy-start
  3.0 1.2 %copy-done = bf16[512,1024]{1,0:T(8,128)(2,1)S(1)} copy-done((bf16[512,1024]{1,0:T(8,128)(2,1)S(1)}, bf16[512,1024]{1,0:T(8,128)(2,1)}, u32[]{:S(2)}) %copy-start) | copy-done | bytes 1048600
  4.2 0.0 copy-start.2
  4.2 0.9 %copy-done.2 = bf16[512,256]{1,0:T(8,128)(2,1)S(1)} copy-done((bf16[512,256]{1,0:T(8,128)(2,1)S(1)}, bf16[512,256]{1,0:T(8,128)(2,1)}, u32[]{:S(2)}) %copy-start.2) | copy-done | bytes 262168
  5.2 0.0 copy-start.3
  5.2 0.0 copy-start.1
  5.2 0.0 copy-start.4
  5.2 0.0 copy-start.5
  5.2 0.0 copy-start.6
  5.2 0.0 copy-start.7
  5.2 0.0 copy-start.8
  5.2 0.0 copy-start.9
  5.3 0.4 join_queries.1.q_ref
  5.7 5.4 %collective-permute-start.6 = (bf16[512,512]{1,0:T(8,128)(2,1)S(1)}, bf16[512,512]{1,0:T(8,128)(2,1)S(1)}, u32[]{:S(2)}, u32[]{:S(2)}) collective-permute-start(bf16[512,512]{1,0:T(8,128)(2,1)S(1)} %join_queries.1.q_ref), channel_id=1, source_target_pairs={{0,2},{2,0},{1,3},{3,1},{4,6},{6,4},{5,7},{7,5},{8,10},{10,8},{9,1... | collective-permute-start | bytes 1572872 | tf_op jit(solution)/shard_map/ppermute | solution.py:278
  11.1 0.0 copy-done.3
  11.1 4.6 %collective-permute-start.2 = (f32[2]{0:T(128)S(1)}, f32[2]{0:T(128)S(1)}, u32[]{:S(2)}, u32[]{:S(2)}) collective-permute-start(f32[2]{0:T(128)S(1)} %copy-done.3), channel_id=1, source_target_pairs={{0,64},{64,0},{128,192},{192,128},{1,65},{65,1},{129,193},{193,129... | collective-permute-start | bytes 32 | tf_op jit(solution)/shard_map/ppermute | solution.py:36
  15.7 0.0 copy-done.1
  15.7 0.1 collective-permute-start.8
  15.8 0.0 collective-permute-done.wk2
  15.8 2.6 %collective-permute-start.4 = (bf16[512,512]{1,0:T(8,128)(2,1)S(1)}, bf16[512,512]{1,0:T(8,128)(2,1)S(1)}, u32[]{:S(2)}, u32[]{:S(2)}) collective-permute-start(bf16[512,512]{1,0:T(8,128)(2,1)S(1)} %join_queries.1.q_ref), channel_id=1, source_target_pairs={{0,1},{1,0},{2,3},{3,2},{4,5},{5,4},{6,7},{7,6},{8,9},{9,8},{10,11... | collective-permute-start | bytes 1572872 | tf_op jit(solution)/shard_map/ppermute | solution.py:278
  18.4 0.0 collective-permute-done.1.wv2
  18.4 0.0 copy-done.4
  18.4 0.0 copy-done.5
  18.5 0.0 copy-done.6
  18.5 0.0 copy-done.7
  18.5 0.0 copy-done.8
  18.5 0.0 copy-done.9
  18.5 5.2 %project_kv.1 = (bf16[2048,512]{1,0:T(8,128)(2,1)S(1)}, bf16[2048,512]{1,0:T(8,128)(2,1)S(1)}, s32[8,128]{1,0:T(8,128)S(1)}, s32[32,128]{1,0:T(8,128)S(1)}, s32[16,128]{1,0:T(8,128)S(1)}) custom-call(bf16[2048,1024]{1,0:T(8,128)(2,1)S(1)} %copy-done.4, bf16[1024,256]{1,0:T(8,128)(2,1)S(1)} %copy-done.6, bf16[1024,256]{1,0:T(8,128)(2,1)S(1)} %collective-permute-done.wk2, ...), custom_call_target="tpu_custom_call" | custom-call | flops 4294967296 | bytes 8388608 | tf_op jit(solution)/shard_map/project_kv/pallas_call | solution.py:134
  23.7 0.0 collective-permute-done.2.other_bias
  23.8 0.4 collective-permute-done.6.q_ref
  24.2 6.5 %shard_map.102 = bf16[512,512]{1,0:T(8,128)(2,1)S(1)} custom-call(s32[8,128]{1,0:T(8,128)S(1)} %get-tuple-element.12.runs_ref, f32[2]{0:T(128)S(1)} %copy-done.3, f32[2]{0:T(128)S(1)} %collective-permute-done.2.other_bias, s32[32,128]{1,0:T(8,128)S(1)} %get-tuple-element.13.gene_ref, s32[16,128]{1,0:T(8,128)S(1)} %get-tuple-element.14.peak_ref, ...), custom_call_target="tpu_custom_call" | custom-call | flops 2147483648 | bytes 5242880 | tf_op jit(solution)/shard_map/pallas_call | solution.py:217
  30.7 5.2 %collective-permute-start.7 = (bf16[512,512]{1,0:T(8,128)(2,1)S(1)}, bf16[512,512]{1,0:T(8,128)(2,1)S(1)}, u32[]{:S(2)}, u32[]{:S(2)}) collective-permute-start(bf16[512,512]{1,0:T(8,128)(2,1)S(1)} %shard_map.102), channel_id=1, source_target_pairs={{0,2},{2,0},{1,3},{3,1},{4,6},{6,4},{5,7},{7,5},{8,10},{10,8},{9,1... | collective-permute-start | bytes 1572872 | tf_op jit(solution)/shard_map/ppermute | solution.py:278
  35.9 5.4 %collective-permute-done.4.q_ref = bf16[512,512]{1,0:T(8,128)(2,1)S(1)} collective-permute-done((bf16[512,512]{1,0:T(8,128)(2,1)S(1)}, bf16[512,512]{1,0:T(8,128)(2,1)S(1)}, u32[]{:S(2)}, u32[]{:S(2)}) %collective-permute-start.4) | collective-permute-done | bytes 524320 | tf_op jit(solution)/shard_map/ppermute | solution.py:278
  41.3 6.5 %shard_map.101 = bf16[512,512]{1,0:T(8,128)(2,1)S(1)} custom-call(s32[8,128]{1,0:T(8,128)S(1)} %get-tuple-element.12.runs_ref, f32[2]{0:T(128)S(1)} %copy-done.3, f32[2]{0:T(128)S(1)} %collective-permute-done.2.other_bias, s32[32,128]{1,0:T(8,128)S(1)} %get-tuple-element.13.gene_ref, s32[16,128]{1,0:T(8,128)S(1)} %get-tuple-element.14.peak_ref, ...), custom_call_target="tpu_custom_call" | custom-call | flops 2147483648 | bytes 5242880 | tf_op jit(solution)/shard_map/pallas_call | solution.py:217
  47.8 4.1 %collective-permute-start.5 = (bf16[512,512]{1,0:T(8,128)(2,1)S(1)}, bf16[512,512]{1,0:T(8,128)(2,1)S(1)}, u32[]{:S(2)}, u32[]{:S(2)}) collective-permute-start(bf16[512,512]{1,0:T(8,128)(2,1)S(1)} %shard_map.101), channel_id=1, source_target_pairs={{0,1},{1,0},{2,3},{3,2},{4,5},{5,4},{6,7},{7,6},{8,9},{9,8},{10,11... | collective-permute-start | bytes 1572872 | tf_op jit(solution)/shard_map/ppermute | solution.py:278
  51.9 4.1 %shard_map.100.own_ref = f32[512,256]{1,0:T(8,128)S(1)} custom-call(s32[8,128]{1,0:T(8,128)S(1)} %get-tuple-element.12.runs_ref, f32[2]{0:T(128)S(1)} %copy-done.3, f32[2]{0:T(128)S(1)} %collective-permute-done.2.other_bias, s32[32,128]{1,0:T(8,128)S(1)} %get-tuple-element.13.gene_ref, s32[16,128]{1,0:T(8,128)S(1)} %get-tuple-element.14.peak_ref, ...), custom_call_target="tpu_custom_call" | custom-call | flops 1073741824 | bytes 5242880 | tf_op jit(solution)/shard_map/pallas_call | solution.py:217
  56.0 0.0 collective-permute-done.8.w2
  56.0 0.0 collective-permute-done.7.far_ref
  56.0 4.4 %collective-permute-done.5.near_ref = bf16[512,512]{1,0:T(8,128)(2,1)S(1)} collective-permute-done((bf16[512,512]{1,0:T(8,128)(2,1)S(1)}, bf16[512,512]{1,0:T(8,128)(2,1)S(1)}, u32[]{:S(2)}, u32[]{:S(2)}) %collective-permute-start.5) | collective-permute-done | bytes 524320 | tf_op jit(solution)/shard_map/ppermute | solution.py:278
  60.5 0.7 mix.1
  61.2 0.1 collective-permute-start.9
  61.3 1.9 %collective-permute-done.9 = bf16[512,512]{1,0:T(8,128)(2,1)S(1)} collective-permute-done((bf16[512,512]{1,0:T(8,128)(2,1)S(1)}, bf16[512,512]{1,0:T(8,128)(2,1)S(1)}, u32[]{:S(2)}, u32[]{:S(2)}) %collective-permute-start.9) | collective-permute-done | bytes 524320 | tf_op jit(solution)/shard_map/ppermute | solution.py:36
  63.2 0.2 convert_add_fusion
  63.4 7.4 %collective-permute-start.10 = (bf16[512,256]{1,0:T(8,128)(2,1)S(1)}, bf16[512,256]{1,0:T(8,128)(2,1)S(1)}, u32[]{:S(2)}, u32[]{:S(2)}) collective-permute-start(bf16[512,256]{1,0:T(8,128)(2,1)S(1)} %slice.15), channel_id=1, source_target_pairs={{0,128},{128,0},{64,192},{192,64},{1,129},{129,1},{65,193},{193,65... | collective-permute-start | bytes 786440 | tf_op jit(solution)/shard_map/ppermute | solution.py:298
  70.8 11.8 %collective-permute-done.10 = bf16[512,256]{1,0:T(8,128)(2,1)S(1)} collective-permute-done((bf16[512,256]{1,0:T(8,128)(2,1)S(1)}, bf16[512,256]{1,0:T(8,128)(2,1)S(1)}, u32[]{:S(2)}, u32[]{:S(2)}) %collective-permute-start.10) | collective-permute-done | bytes 262176 | tf_op jit(solution)/shard_map/ppermute | solution.py:298
  82.5 0.8 fusion
  (1 shorter events, 0.0 us)
Async XLA Ops:
  0.0 3.0 %collective-permute-start.3 = (bf16[1024,256]{1,0:T(8,128)(2,1)}, bf16[1024,256]{1,0:T(8,128)(2,1)S(1)}, u32[]{:S(2)}, u32[]{:S(2)}) collective-permute-start(bf16[1024,256]{1,0:T(8,128)(2,1)} %w_ref.1), channel_id=1, source_target_pairs={{0,64},{64,0},{128,192},{192,128},{1,65},{65,1},{129,193},{193,129... | collective-permute-start | bytes 1572872 | tf_op jit(solution)/shard_map/ppermute | solution.py:36
  0.0 15.8 %collective-permute-start = (bf16[1024,256]{1,0:T(8,128)(2,1)}, bf16[1024,256]{1,0:T(8,128)(2,1)S(1)}, u32[]{:S(2)}, u32[]{:S(2)}) collective-permute-start(bf16[1024,256]{1,0:T(8,128)(2,1)} %wk1.1), channel_id=1, source_target_pairs={{0,64},{64,0},{128,192},{192,128},{1,65},{65,1},{129,193},{193,129... | collective-permute-start | bytes 1572872 | tf_op jit(solution)/shard_map/ppermute | solution.py:36
  0.5 17.9 %collective-permute-start.1 = (bf16[1024,256]{1,0:T(8,128)(2,1)}, bf16[1024,256]{1,0:T(8,128)(2,1)S(1)}, u32[]{:S(2)}, u32[]{:S(2)}) collective-permute-start(bf16[1024,256]{1,0:T(8,128)(2,1)} %wv1.1), channel_id=1, source_target_pairs={{0,64},{64,0},{128,192},{192,128},{1,65},{65,1},{129,193},{193,129... | collective-permute-start | bytes 1572872 | tf_op jit(solution)/shard_map/ppermute | solution.py:36
  3.0 1.2 %copy-start = (bf16[512,1024]{1,0:T(8,128)(2,1)S(1)}, bf16[512,1024]{1,0:T(8,128)(2,1)}, u32[]{:S(2)}) copy-start(bf16[512,1024]{1,0:T(8,128)(2,1)} %act_ref.5) | copy-start | bytes 3145732
  4.2 0.9 %copy-start.2 = (bf16[512,256]{1,0:T(8,128)(2,1)S(1)}, bf16[512,256]{1,0:T(8,128)(2,1)}, u32[]{:S(2)}) copy-start(bf16[512,256]{1,0:T(8,128)(2,1)} %project_queries.1.own_ref) | copy-start | bytes 786436
  5.2 5.9 %copy-start.3 = (f32[2]{0:T(128)S(1)}, f32[2]{0:T(128)}, u32[]{:S(2)}) copy-start(f32[2]{0:T(128)} %own_bias.5) | copy-start | bytes 28
  5.2 10.5 %copy-start.1 = (bf16[256,1024]{1,0:T(8,128)(2,1)S(1)}, bf16[256,1024]{1,0:T(8,128)(2,1)}, u32[]{:S(2)}) copy-start(bf16[256,1024]{1,0:T(8,128)(2,1)} %w1.1) | copy-start | bytes 1572868
  5.2 13.2 %copy-start.4 = (bf16[2048,1024]{1,0:T(8,128)(2,1)S(1)}, bf16[2048,1024]{1,0:T(8,128)(2,1)}, u32[]{:S(2)}) copy-start(bf16[2048,1024]{1,0:T(8,128)(2,1)} %act_ref.3) | copy-start | bytes 12582916
  5.2 13.2 %copy-start.5 = (s32[256,1024]{1,0:T(8,128)S(1)}, s32[256,1024]{1,0:T(8,128)}, u32[]{:S(2)}) copy-start(s32[256,1024]{1,0:T(8,128)} %mask_hbm.1) | copy-start | bytes 3145732
  5.2 13.2 %copy-start.6 = (bf16[1024,256]{1,0:T(8,128)(2,1)S(1)}, bf16[1024,256]{1,0:T(8,128)(2,1)}, u32[]{:S(2)}) copy-start(bf16[1024,256]{1,0:T(8,128)(2,1)} %wk1.1) | copy-start | bytes 1572868
  5.2 13.2 %copy-start.7 = (bf16[1024,256]{1,0:T(8,128)(2,1)S(1)}, bf16[1024,256]{1,0:T(8,128)(2,1)}, u32[]{:S(2)}) copy-start(bf16[1024,256]{1,0:T(8,128)(2,1)} %wv1.1) | copy-start | bytes 1572868
  5.2 13.2 %copy-start.8 = (s32[131072]{0:T(1024)S(1)}, s32[131072]{0:T(1024)}, u32[]{:S(2)}) copy-start(s32[131072]{0:T(1024)} %param.19) | copy-start | bytes 1572868
  5.2 13.2 %copy-start.9 = (s32[32768]{0:T(1024)S(1)}, s32[32768]{0:T(1024)}, u32[]{:S(2)}) copy-start(s32[32768]{0:T(1024)} %param.18) | copy-start | bytes 393220
  5.7 18.5 %collective-permute-start.6 = (bf16[512,512]{1,0:T(8,128)(2,1)S(1)}, bf16[512,512]{1,0:T(8,128)(2,1)S(1)}, u32[]{:S(2)}, u32[]{:S(2)}) collective-permute-start(bf16[512,512]{1,0:T(8,128)(2,1)S(1)} %join_queries.1.q_ref), channel_id=1, source_target_pairs={{0,2},{2,0},{1,3},{3,1},{4,6},{6,4},{5,7},{7,5},{8,10},{10,8},{9,1... | collective-permute-start | bytes 1572872 | tf_op jit(solution)/shard_map/ppermute | solution.py:278
  11.1 12.7 %collective-permute-start.2 = (f32[2]{0:T(128)S(1)}, f32[2]{0:T(128)S(1)}, u32[]{:S(2)}, u32[]{:S(2)}) collective-permute-start(f32[2]{0:T(128)S(1)} %copy-done.3), channel_id=1, source_target_pairs={{0,64},{64,0},{128,192},{192,128},{1,65},{65,1},{129,193},{193,129... | collective-permute-start | bytes 32 | tf_op jit(solution)/shard_map/ppermute | solution.py:36
  15.7 40.3 %collective-permute-start.8 = (bf16[256,1024]{1,0:T(8,128)(2,1)S(1)}, bf16[256,1024]{1,0:T(8,128)(2,1)S(1)}, u32[]{:S(2)}, u32[]{:S(2)}) collective-permute-start(bf16[256,1024]{1,0:T(8,128)(2,1)S(1)} %copy-done.1), channel_id=1, source_target_pairs={{0,64},{64,0},{128,192},{192,128},{1,65},{65,1},{129,193},{193,129... | collective-permute-start | bytes 1572872 | tf_op jit(solution)/shard_map/ppermute | solution.py:36
  15.8 25.5 %collective-permute-start.4 = (bf16[512,512]{1,0:T(8,128)(2,1)S(1)}, bf16[512,512]{1,0:T(8,128)(2,1)S(1)}, u32[]{:S(2)}, u32[]{:S(2)}) collective-permute-start(bf16[512,512]{1,0:T(8,128)(2,1)S(1)} %join_queries.1.q_ref), channel_id=1, source_target_pairs={{0,1},{1,0},{2,3},{3,2},{4,5},{5,4},{6,7},{7,6},{8,9},{9,8},{10,11... | collective-permute-start | bytes 1572872 | tf_op jit(solution)/shard_map/ppermute | solution.py:278
  30.7 25.3 %collective-permute-start.7 = (bf16[512,512]{1,0:T(8,128)(2,1)S(1)}, bf16[512,512]{1,0:T(8,128)(2,1)S(1)}, u32[]{:S(2)}, u32[]{:S(2)}) collective-permute-start(bf16[512,512]{1,0:T(8,128)(2,1)S(1)} %shard_map.102), channel_id=1, source_target_pairs={{0,2},{2,0},{1,3},{3,1},{4,6},{6,4},{5,7},{7,5},{8,10},{10,8},{9,1... | collective-permute-start | bytes 1572872 | tf_op jit(solution)/shard_map/ppermute | solution.py:278
  47.8 12.6 %collective-permute-start.5 = (bf16[512,512]{1,0:T(8,128)(2,1)S(1)}, bf16[512,512]{1,0:T(8,128)(2,1)S(1)}, u32[]{:S(2)}, u32[]{:S(2)}) collective-permute-start(bf16[512,512]{1,0:T(8,128)(2,1)S(1)} %shard_map.101), channel_id=1, source_target_pairs={{0,1},{1,0},{2,3},{3,2},{4,5},{5,4},{6,7},{7,6},{8,9},{9,8},{10,11... | collective-permute-start | bytes 1572872 | tf_op jit(solution)/shard_map/ppermute | solution.py:278
  61.2 2.0 %collective-permute-start.9 = (bf16[512,512]{1,0:T(8,128)(2,1)S(1)}, bf16[512,512]{1,0:T(8,128)(2,1)S(1)}, u32[]{:S(2)}, u32[]{:S(2)}) collective-permute-start(bf16[512,512]{1,0:T(8,128)(2,1)S(1)} %get-tuple-element.18), channel_id=1, source_target_pairs={{0,64},{64,0},{128,192},{192,128},{1,65},{65,1},{129,193},{193,129... | collective-permute-start | bytes 1572872 | tf_op jit(solution)/shard_map/ppermute | solution.py:36
  63.4 19.1 %collective-permute-start.10 = (bf16[512,256]{1,0:T(8,128)(2,1)S(1)}, bf16[512,256]{1,0:T(8,128)(2,1)S(1)}, u32[]{:S(2)}, u32[]{:S(2)}) collective-permute-start(bf16[512,256]{1,0:T(8,128)(2,1)S(1)} %slice.15), channel_id=1, source_target_pairs={{0,128},{128,0},{64,192},{192,64},{1,129},{129,1},{65,193},{193,65... | collective-permute-start | bytes 786440 | tf_op jit(solution)/shard_map/ppermute | solution.py:298

commit v2 on v1

--- a/solution.py
+++ b/solution.py
@@ -13,20 +13,28 @@
 REACH = 2
 CHUNK = 512
 SPAN = 32
+BYS = (2, 1)
+CROSSED = True
 F32 = jnp.float32
 BF16 = jnp.bfloat16
 I32 = jnp.int32
 VMEM = pl.BlockSpec(memory_space=pltpu.VMEM)
 SMEM = pl.BlockSpec(memory_space=pltpu.SMEM)
-ANY = pl.BlockSpec(memory_space=pl.ANY)
+HBM = pl.BlockSpec(memory_space=pltpu.HBM)
 PARAMS = pltpu.CompilerParams(vmem_limit_bytes=20 << 20)
 
 
-def swap_pairs(genes, count, by):
+def partner_kind(core, turn):
+    by = BYS[turn]
+    return by, (core ^ (by - 1)) if CROSSED else core
+
+
+def swap_pairs(genes, count, turn):
     pairs = []
     for g in range(genes):
+        by, kind = partner_kind(g % 2, turn)
         for i in range(count - by):
-            if (i // by) % 2 == g % 2:
+            if (i // by) % 2 == kind:
                 a, b = g * count + i, g * count + i + by
                 pairs += [(a, b), (b, a)]
     return pairs
@@ -66,6 +74,7 @@
         out_specs=VMEM,
         out_shape=jax.ShapeDtypeStruct((rows, width), BF16),
         cost_estimate=cost(2 * act.size * width, [act, own]),
+        compiler_params=PARAMS,
         name="project_queries",
     )(act, own)
     return pl.pallas_call(
@@ -133,7 +142,7 @@
     tiles = total // TILE
     return pl.pallas_call(
         functools.partial(kv_kernel, gene_tiles),
-        in_specs=[VMEM] * 5 + [ANY] * 3,
+        in_specs=[VMEM] * 5 + [HBM] * 3,
         out_specs=[VMEM] * 5,
         out_shape=[
             jax.ShapeDtypeStruct((total, width), BF16),
@@ -154,7 +163,7 @@
 
 
 def attend_kernel(
-    by, heads, runs_ref, own_bias, other_bias, gene_ref, peak_ref, q_ref, k_ref, v_ref, o_ref, acc
+    turn, heads, runs_ref, own_bias, other_bias, gene_ref, peak_ref, q_ref, k_ref, v_ref, o_ref, acc
 ):
     tiles = q_ref.shape[0] // TILE
     per_chunk = CHUNK // TILE
@@ -162,8 +171,8 @@
     scale = 0.5 / math.sqrt(dim)
     me, count = lax.axis_index("peak"), lax.axis_size("peak")
     source = me
-    if by:
-        kind = lax.axis_index("gene") % 2
+    if turn is not None:
+        by, kind = partner_kind(lax.axis_index("gene") & 1, turn)
         source = jnp.where((me // by) % 2 == kind, me + by, me - by)
     valid = (source >= 0) & (source < count)
     base = jnp.where(valid, source * tiles - window_origin(tiles), 0)
@@ -211,11 +220,11 @@
     o_ref[...] = (acc[...] * 0.5).astype(o_ref.dtype)
 
 
-def attend(by, heads, tables, q, k, v, dtype):
+def attend(turn, heads, tables, q, k, v, dtype):
     runs, own_bias, other_bias, gene, peak = tables
     shape = (q.shape[0], heads * TILE)
     return pl.pallas_call(
-        functools.partial(attend_kernel, by, heads),
+        functools.partial(attend_kernel, turn, heads),
         in_specs=[SMEM] * 3 + [VMEM] * 5,
         out_specs=VMEM,
         out_shape=jax.ShapeDtypeStruct(shape, dtype),
@@ -225,12 +234,12 @@
     )(runs, own_bias, other_bias, gene, peak, q, k, v)
 
 
-def mix_kernel(own_ref, near_ref, far_ref, w1, w2, send_ref, keep_ref):
+def mix_kernel(own_ref, first_ref, second_ref, w1, w2, send_ref, keep_ref):
     width = w1.shape[1] // 4
     depth = w1.shape[0]
     me = lax.axis_index("gene")
-    mine = own_ref[...] + near_ref[:, :depth].astype(F32) + far_ref[:, :depth].astype(F32)
-    theirs = near_ref[:, depth:].astype(F32) + far_ref[:, depth:].astype(F32)
+    mine = own_ref[...] + first_ref[:, :depth].astype(F32) + second_ref[:, :depth].astype(F32)
+    theirs = first_ref[:, depth:].astype(F32) + second_ref[:, depth:].astype(F32)
     mine, theirs = mine.astype(BF16), theirs.astype(BF16)
 
     def share(block):
@@ -245,7 +254,7 @@
     keep_ref[:, width:] = share(me)
 
 
-def mix(own, near, far, w1, w2):
+def mix(own, first, second, w1, w2):
     shape = (own.shape[0], w1.shape[1] // 2)
     return pl.pallas_call(
         mix_kernel,
@@ -255,7 +264,7 @@
         cost_estimate=cost(4 * own.shape[0] * w1.size, [own, w1, w2, own, own]),
         compiler_params=PARAMS,
         name="mix",
-    )(own, near, far, w1, w2)
+    )(own, first, second, w1, w2)
 
 
 def on_device(
@@ -274,25 +283,23 @@
     local = head_bias.shape[0]
     count, genes = lax.axis_size("peak"), lax.axis_size("gene")
 
-    def travel(x, by):
-        return lax.ppermute(x, ("gene", "peak"), swap_pairs(genes, count, by))
+    def travel(x, turn):
+        return lax.ppermute(x, ("gene", "peak"), swap_pairs(genes, count, turn))
 
     queries = project_queries(gene_act, w_query, core_swap(w_query))
-    near, far = travel(queries, 1), travel(queries, 2)
+    first, second = travel(queries, 0), travel(queries, 1)
+    w_key = (w_key, core_swap(w_key))
+    w_value = (w_value, core_swap(w_value))
+    gene, peak = gene_chrom.reshape(-1, TILE), peak_chrom.reshape(-1, TILE)
     keys, values, runs, gene, peak = project_kv(
-        gene_tiles,
-        peak_act,
-        (w_key, core_swap(w_key)),
-        (w_value, core_swap(w_value)),
-        block_mask,
-        gene_chrom.reshape(-1, TILE),
-        peak_chrom.reshape(-1, TILE),
+        gene_tiles, peak_act, w_key, w_value, block_mask, gene, peak
     )
     tables = (runs, head_bias, core_swap(head_bias), gene, peak)
-    near = travel(attend(1, 2 * local, tables, near, keys, values, BF16), 1)
-    far = travel(attend(2, 2 * local, tables, far, keys, values, BF16), 2)
-    own = attend(0, local, tables, queries, keys, values, F32)
-    send, keep = mix(own, near, far, w_out, core_swap(w_out))
+    first = attend(0, 2 * local, tables, first, keys, values, BF16)
+    second = attend(1, 2 * local, tables, second, keys, values, BF16)
+    first, second = travel(first, 0), travel(second, 1)
+    own = attend(None, local, tables, queries, keys, values, F32)
+    send, keep = mix(own, first, second, w_out, core_swap(w_out))
     width = send.shape[1] // 2
     half = keep + core_swap(send).astype(F32)
     other = lax.ppermute(half[:, :width].astype(BF16), "gene", [(0, 2), (2, 0), (1, 3), (3, 1)])

time: 83.6 us -> 80.9 us (0.968)
  the two profiles are of different devices: /device:TPU:6 before, /device:TPU:3 now
where the time goes in v2:
time: 80.9 us; the launch traced here: 80.1 us
  starting transfers between devices  33.9 us (42%)
  waiting for transfers between devices  22.9 us (28%)
  Pallas kernels  19.7 us (24%)
  local copies, waits for them, and re-layouts  2.35 us (3%)
  other arithmetic  0.94 us (1%)
    ppermute x4, starting transfers between devices, travel(): return lax.ppermute(x, ('gene', 'peak'), swap_pairs(genes, count, turn))  28.1 us
    pallas_call x3, Pallas kernels, attend(): pl.pallas_call(functools.partial(attend_kernel, turn, heads), in_specs=[S...  12.9 us
    ppermute x1, waiting for transfers between devices, on_device(): lax.ppermute(half[:, :width].astype(BF16), 'gene', [(0, 2), (2, 0), (1, 3...  12.5 us
    ppermute x4, waiting for transfers between devices, travel(): return lax.ppermute(x, ('gene', 'peak'), swap_pairs(genes, count, turn))  8.5 us
    pallas_call x1, Pallas kernels, project_kv(): pl.pallas_call(functools.partial(kv_kernel, gene_tiles), in_specs=[VMEM]...  5.25 us
    ppermute x1, starting transfers between devices, on_device(): lax.ppermute(half[:, :width].astype(BF16), 'gene', [(0, 2), (2, 0), (1, 3...  3.99 us
    unnamed x20, local copies, waits for them, and re-layouts  2.32 us
    ppermute x6, waiting for transfers between devices, core_swap(): return lax.ppermute(x, 'gene', [(0, 1), (1, 0), (2, 3), (3, 2)])  1.91 us
  transfers between devices with their start and end apart: 11, of which 4 were waited for; matrix products, arithmetic and copies ran while one was open for 0% of the time, Pallas kernels for 24%

profile of v2, /device:TPU:3, one launch (start us, length us, event | category | flops | bytes accessed | tf_op | source)
XLA Modules:
  0.0 80.1 jit_solution(8297863811239702513)
XLA Ops:
  0.0 0.7 collective-permute-start.3
  0.7 0.0 collective-permute-start
  0.7 0.5 collective-permute-start.1
  1.2 0.0 copy-start
  1.2 1.2 %copy-done = bf16[512,1024]{1,0:T(8,128)(2,1)S(1)} copy-done((bf16[512,1024]{1,0:T(8,128)(2,1)S(1)}, bf16[512,1024]{1,0:T(8,128)(2,1)}, u32[]{:S(2)}) %copy-start) | copy-done | bytes 1048600
  2.4 0.0 copy-start.1
  2.4 1.0 %copy-done.1 = bf16[1024,256]{1,0:T(8,128)(2,1)S(1)} copy-done((bf16[1024,256]{1,0:T(8,128)(2,1)S(1)}, bf16[1024,256]{1,0:T(8,128)(2,1)}, u32[]{:S(2)}) %copy-start.1) | copy-done | bytes 524312
  3.5 0.4 project_queries.1.own_ref
  3.9 0.0 copy-start.3
  3.9 0.0 copy-start.2
  3.9 0.0 copy-start.4
  3.9 0.0 copy-start.5
  3.9 0.0 copy-start.6
  4.0 0.0 copy-start.7
  4.0 0.0 copy-start.8
  4.0 0.0 copy-start.9
  4.0 0.0 collective-permute-done.3.w_ref
  4.0 0.4 join_queries.1.q_ref
  4.4 8.9 %collective-permute-start.6 = (bf16[512,512]{1,0:T(8,128)(2,1)S(1)}, bf16[512,512]{1,0:T(8,128)(2,1)S(1)}, u32[]{:S(2)}, u32[]{:S(2)}) collective-permute-start(bf16[512,512]{1,0:T(8,128)(2,1)S(1)} %join_queries.1.q_ref), channel_id=1, source_target_pairs={{0,1},{1,0},{2,3},{3,2},{4,5},{5,4},{6,7},{7,6},{8,9},{9,8},{10,11... | collective-permute-start | bytes 1572872 | tf_op jit(solution)/shard_map/ppermute | solution.py:287
  13.4 0.0 copy-done.3
  13.4 0.1 collective-permute-start.2
  13.5 0.0 copy-done.2
  13.5 0.5 collective-permute-start.8
  14.0 0.0 collective-permute-done.wk2
  14.0 1.9 %collective-permute-start.4 = (bf16[512,512]{1,0:T(8,128)(2,1)S(1)}, bf16[512,512]{1,0:T(8,128)(2,1)S(1)}, u32[]{:S(2)}, u32[]{:S(2)}) collective-permute-start(bf16[512,512]{1,0:T(8,128)(2,1)S(1)} %join_queries.1.q_ref), channel_id=1, source_target_pairs={{2,4},{4,2},{3,5},{5,3},{6,8},{8,6},{7,9},{9,7},{10,12},{12,10},{1... | collective-permute-start | bytes 1572872 | tf_op jit(solution)/shard_map/ppermute | solution.py:287
  15.9 0.0 collective-permute-done.1.wv2
  15.9 0.0 copy-done.4
  15.9 0.0 copy-done.5
  16.0 0.0 copy-done.6
  16.0 0.0 copy-done.7
  16.0 0.0 copy-done.8
  16.0 0.0 copy-done.9
  16.0 5.2 %project_kv.1 = (bf16[2048,512]{1,0:T(8,128)(2,1)S(1)}, bf16[2048,512]{1,0:T(8,128)(2,1)S(1)}, s32[8,128]{1,0:T(8,128)S(1)}, s32[32,128]{1,0:T(8,128)S(1)}, s32[16,128]{1,0:T(8,128)S(1)}) custom-call(bf16[2048,1024]{1,0:T(8,128)(2,1)S(1)} %copy-done.4, bf16[1024,256]{1,0:T(8,128)(2,1)S(1)} %copy-done.6, bf16[1024,256]{1,0:T(8,128)(2,1)S(1)} %collective-permute-done.wk2, ...), custom_call_target="tpu_custom_call" | custom-call | flops 4294967296 | bytes 8388608 | tf_op jit(solution)/shard_map/project_kv/pallas_call | solution.py:143
  21.3 0.0 collective-permute-done.2.other_bias
  21.3 1.2 %collective-permute-done.6.q_ref = bf16[512,512]{1,0:T(8,128)(2,1)S(1)} collective-permute-done((bf16[512,512]{1,0:T(8,128)(2,1)S(1)}, bf16[512,512]{1,0:T(8,128)(2,1)S(1)}, u32[]{:S(2)}, u32[]{:S(2)}) %collective-permute-start.6) | collective-permute-done | bytes 524320 | tf_op jit(solution)/shard_map/ppermute | solution.py:287
  22.4 2.2 %shard_map.102 = bf16[512,512]{1,0:T(8,128)(2,1)S(1)} custom-call(s32[8,128]{1,0:T(8,128)S(1)} %get-tuple-element.12.runs_ref, f32[2]{0:T(128)S(1)} %copy-done.3, f32[2]{0:T(128)S(1)} %collective-permute-done.2.other_bias, s32[32,128]{1,0:T(8,128)S(1)} %get-tuple-element.13.gene_ref, s32[16,128]{1,0:T(8,128)S(1)} %get-tuple-element.14.peak_ref, ...), custom_call_target="tpu_custom_call" | custom-call | flops 2147483648 | bytes 5242880 | tf_op jit(solution)/shard_map/pallas_call | solution.py:226
  24.7 15.3 %collective-permute-start.7 = (bf16[512,512]{1,0:T(8,128)(2,1)S(1)}, bf16[512,512]{1,0:T(8,128)(2,1)S(1)}, u32[]{:S(2)}, u32[]{:S(2)}) collective-permute-start(bf16[512,512]{1,0:T(8,128)(2,1)S(1)} %shard_map.102), channel_id=1, source_target_pairs={{0,1},{1,0},{2,3},{3,2},{4,5},{5,4},{6,7},{7,6},{8,9},{9,8},{10,11... | collective-permute-start | bytes 1572872 | tf_op jit(solution)/shard_map/ppermute | solution.py:287
  40.0 0.0 collective-permute-done.4.q_ref
  40.0 6.5 %shard_map.101 = bf16[512,512]{1,0:T(8,128)(2,1)S(1)} custom-call(s32[8,128]{1,0:T(8,128)S(1)} %get-tuple-element.12.runs_ref, f32[2]{0:T(128)S(1)} %copy-done.3, f32[2]{0:T(128)S(1)} %collective-permute-done.2.other_bias, s32[32,128]{1,0:T(8,128)S(1)} %get-tuple-element.13.gene_ref, s32[16,128]{1,0:T(8,128)S(1)} %get-tuple-element.14.peak_ref, ...), custom_call_target="tpu_custom_call" | custom-call | flops 2147483648 | bytes 5242880 | tf_op jit(solution)/shard_map/pallas_call | solution.py:226
  46.5 1.9 %collective-permute-start.5 = (bf16[512,512]{1,0:T(8,128)(2,1)S(1)}, bf16[512,512]{1,0:T(8,128)(2,1)S(1)}, u32[]{:S(2)}, u32[]{:S(2)}) collective-permute-start(bf16[512,512]{1,0:T(8,128)(2,1)S(1)} %shard_map.101), channel_id=1, source_target_pairs={{2,4},{4,2},{3,5},{5,3},{6,8},{8,6},{7,9},{9,7},{10,12},{12,10},{1... | collective-permute-start | bytes 1572872 | tf_op jit(solution)/shard_map/ppermute | solution.py:287
  48.5 4.1 %shard_map.100.own_ref = f32[512,256]{1,0:T(8,128)S(1)} custom-call(s32[8,128]{1,0:T(8,128)S(1)} %get-tuple-element.12.runs_ref, f32[2]{0:T(128)S(1)} %copy-done.3, f32[2]{0:T(128)S(1)} %collective-permute-done.2.other_bias, s32[32,128]{1,0:T(8,128)S(1)} %get-tuple-element.13.gene_ref, s32[16,128]{1,0:T(8,128)S(1)} %get-tuple-element.14.peak_ref, ...), custom_call_target="tpu_custom_call" | custom-call | flops 1073741824 | bytes 5242880 | tf_op jit(solution)/shard_map/pallas_call | solution.py:226
  52.5 0.0 collective-permute-done.8.w2
  52.6 0.0 collective-permute-done.7.second_ref
  52.6 7.3 %collective-permute-done.5.first_ref = bf16[512,512]{1,0:T(8,128)(2,1)S(1)} collective-permute-done((bf16[512,512]{1,0:T(8,128)(2,1)S(1)}, bf16[512,512]{1,0:T(8,128)(2,1)S(1)}, u32[]{:S(2)}, u32[]{:S(2)}) %collective-permute-start.5) | collective-permute-done | bytes 524320 | tf_op jit(solution)/shard_map/ppermute | solution.py:287
  59.9 0.7 mix.1
  60.6 0.1 collective-permute-start.9
  60.7 1.9 %collective-permute-done.9 = bf16[512,512]{1,0:T(8,128)(2,1)S(1)} collective-permute-done((bf16[512,512]{1,0:T(8,128)(2,1)S(1)}, bf16[512,512]{1,0:T(8,128)(2,1)S(1)}, u32[]{:S(2)}, u32[]{:S(2)}) %collective-permute-start.9) | collective-permute-done | bytes 524320 | tf_op jit(solution)/shard_map/ppermute | solution.py:44
  62.6 0.2 convert_add_fusion
  62.9 4.0 %collective-permute-start.10 = (bf16[512,256]{1,0:T(8,128)(2,1)S(1)}, bf16[512,256]{1,0:T(8,128)(2,1)S(1)}, u32[]{:S(2)}, u32[]{:S(2)}) collective-permute-start(bf16[512,256]{1,0:T(8,128)(2,1)S(1)} %slice.15), channel_id=1, source_target_pairs={{0,128},{128,0},{64,192},{192,64},{1,129},{129,1},{65,193},{193,65... | collective-permute-start | bytes 786440 | tf_op jit(solution)/shard_map/ppermute | solution.py:305
  66.8 12.5 %collective-permute-done.10 = bf16[512,256]{1,0:T(8,128)(2,1)S(1)} collective-permute-done((bf16[512,256]{1,0:T(8,128)(2,1)S(1)}, bf16[512,256]{1,0:T(8,128)(2,1)S(1)}, u32[]{:S(2)}, u32[]{:S(2)}) %collective-permute-start.10) | collective-permute-done | bytes 262176 | tf_op jit(solution)/shard_map/ppermute | solution.py:305
  79.3 0.8 fusion
  (1 shorter events, 0.0 us)
Async XLA Ops:
  0.0 4.0 %collective-permute-start.3 = (bf16[1024,256]{1,0:T(8,128)(2,1)}, bf16[1024,256]{1,0:T(8,128)(2,1)S(1)}, u32[]{:S(2)}, u32[]{:S(2)}) collective-permute-start(bf16[1024,256]{1,0:T(8,128)(2,1)} %w_ref.1), channel_id=1, source_target_pairs={{0,64},{64,0},{128,192},{192,128},{1,65},{65,1},{129,193},{193,129... | collective-permute-start | bytes 1572872 | tf_op jit(solution)/shard_map/ppermute | solution.py:44
  0.7 13.3 %collective-permute-start = (bf16[1024,256]{1,0:T(8,128)(2,1)}, bf16[1024,256]{1,0:T(8,128)(2,1)S(1)}, u32[]{:S(2)}, u32[]{:S(2)}) collective-permute-start(bf16[1024,256]{1,0:T(8,128)(2,1)} %wk1.1), channel_id=1, source_target_pairs={{0,64},{64,0},{128,192},{192,128},{1,65},{65,1},{129,193},{193,129... | collective-permute-start | bytes 1572872 | tf_op jit(solution)/shard_map/ppermute | solution.py:44
  0.7 15.3 %collective-permute-start.1 = (bf16[1024,256]{1,0:T(8,128)(2,1)}, bf16[1024,256]{1,0:T(8,128)(2,1)S(1)}, u32[]{:S(2)}, u32[]{:S(2)}) collective-permute-start(bf16[1024,256]{1,0:T(8,128)(2,1)} %wv1.1), channel_id=1, source_target_pairs={{0,64},{64,0},{128,192},{192,128},{1,65},{65,1},{129,193},{193,129... | collective-permute-start | bytes 1572872 | tf_op jit(solution)/shard_map/ppermute | solution.py:44
  1.2 1.2 %copy-start = (bf16[512,1024]{1,0:T(8,128)(2,1)S(1)}, bf16[512,1024]{1,0:T(8,128)(2,1)}, u32[]{:S(2)}) copy-start(bf16[512,1024]{1,0:T(8,128)(2,1)} %act_ref.5) | copy-start | bytes 3145732
  2.4 1.0 %copy-start.1 = (bf16[1024,256]{1,0:T(8,128)(2,1)S(1)}, bf16[1024,256]{1,0:T(8,128)(2,1)}, u32[]{:S(2)}) copy-start(bf16[1024,256]{1,0:T(8,128)(2,1)} %w_ref.1) | copy-start | bytes 1572868
  3.9 9.5 %copy-start.3 = (f32[2]{0:T(128)S(1)}, f32[2]{0:T(128)}, u32[]{:S(2)}) copy-start(f32[2]{0:T(128)} %own_bias.5) | copy-start | bytes 28
  3.9 9.6 %copy-start.2 = (bf16[256,1024]{1,0:T(8,128)(2,1)S(1)}, bf16[256,1024]{1,0:T(8,128)(2,1)}, u32[]{:S(2)}) copy-start(bf16[256,1024]{1,0:T(8,128)(2,1)} %w1.1) | copy-start | bytes 1572868
  3.9 12.0 %copy-start.4 = (bf16[2048,1024]{1,0:T(8,128)(2,1)S(1)}, bf16[2048,1024]{1,0:T(8,128)(2,1)}, u32[]{:S(2)}) copy-start(bf16[2048,1024]{1,0:T(8,128)(2,1)} %act_ref.3) | copy-start | bytes 12582916
  3.9 12.0 %copy-start.5 = (s32[256,1024]{1,0:T(8,128)S(1)}, s32[256,1024]{1,0:T(8,128)}, u32[]{:S(2)}) copy-start(s32[256,1024]{1,0:T(8,128)} %mask_hbm.1) | copy-start | bytes 3145732
  3.9 12.0 %copy-start.6 = (bf16[1024,256]{1,0:T(8,128)(2,1)S(1)}, bf16[1024,256]{1,0:T(8,128)(2,1)}, u32[]{:S(2)}) copy-start(bf16[1024,256]{1,0:T(8,128)(2,1)} %wk1.1) | copy-start | bytes 1572868
  4.0 12.0 %copy-start.7 = (bf16[1024,256]{1,0:T(8,128)(2,1)S(1)}, bf16[1024,256]{1,0:T(8,128)(2,1)}, u32[]{:S(2)}) copy-start(bf16[1024,256]{1,0:T(8,128)(2,1)} %wv1.1) | copy-start | bytes 1572868
  4.0 12.0 %copy-start.8 = (s32[131072]{0:T(1024)S(1)}, s32[131072]{0:T(1024)}, u32[]{:S(2)}) copy-start(s32[131072]{0:T(1024)} %param.19) | copy-start | bytes 1572868
  4.0 12.0 %copy-start.9 = (s32[32768]{0:T(1024)S(1)}, s32[32768]{0:T(1024)}, u32[]{:S(2)}) copy-start(s32[32768]{0:T(1024)} %param.18) | copy-start | bytes 393220
  4.4 18.0 %collective-permute-start.6 = (bf16[512,512]{1,0:T(8,128)(2,1)S(1)}, bf16[512,512]{1,0:T(8,128)(2,1)S(1)}, u32[]{:S(2)}, u32[]{:S(2)}) collective-permute-start(bf16[512,512]{1,0:T(8,128)(2,1)S(1)} %join_queries.1.q_ref), channel_id=1, source_target_pairs={{0,1},{1,0},{2,3},{3,2},{4,5},{5,4},{6,7},{7,6},{8,9},{9,8},{10,11... | collective-permute-start | bytes 1572872 | tf_op jit(solution)/shard_map/ppermute | solution.py:287
  13.4 7.8 %collective-permute-start.2 = (f32[2]{0:T(128)S(1)}, f32[2]{0:T(128)S(1)}, u32[]{:S(2)}, u32[]{:S(2)}) collective-permute-start(f32[2]{0:T(128)S(1)} %copy-done.3), channel_id=1, source_target_pairs={{0,64},{64,0},{128,192},{192,128},{1,65},{65,1},{129,193},{193,129... | collective-permute-start | bytes 32 | tf_op jit(solution)/shard_map/ppermute | solution.py:44
  13.5 39.0 %collective-permute-start.8 = (bf16[256,1024]{1,0:T(8,128)(2,1)S(1)}, bf16[256,1024]{1,0:T(8,128)(2,1)S(1)}, u32[]{:S(2)}, u32[]{:S(2)}) collective-permute-start(bf16[256,1024]{1,0:T(8,128)(2,1)S(1)} %copy-done.2), channel_id=1, source_target_pairs={{0,64},{64,0},{128,192},{192,128},{1,65},{65,1},{129,193},{193,129... | collective-permute-start | bytes 1572872 | tf_op jit(solution)/shard_map/ppermute | solution.py:44
  14.0 26.0 %collective-permute-start.4 = (bf16[512,512]{1,0:T(8,128)(2,1)S(1)}, bf16[512,512]{1,0:T(8,128)(2,1)S(1)}, u32[]{:S(2)}, u32[]{:S(2)}) collective-permute-start(bf16[512,512]{1,0:T(8,128)(2,1)S(1)} %join_queries.1.q_ref), channel_id=1, source_target_pairs={{2,4},{4,2},{3,5},{5,3},{6,8},{8,6},{7,9},{9,7},{10,12},{12,10},{1... | collective-permute-start | bytes 1572872 | tf_op jit(solution)/shard_map/ppermute | solution.py:287
  24.7 27.9 %collective-permute-start.7 = (bf16[512,512]{1,0:T(8,128)(2,1)S(1)}, bf16[512,512]{1,0:T(8,128)(2,1)S(1)}, u32[]{:S(2)}, u32[]{:S(2)}) collective-permute-start(bf16[512,512]{1,0:T(8,128)(2,1)S(1)} %shard_map.102), channel_id=1, source_target_pairs={{0,1},{1,0},{2,3},{3,2},{4,5},{5,4},{6,7},{7,6},{8,9},{9,8},{10,11... | collective-permute-start | bytes 1572872 | tf_op jit(solution)/shard_map/ppermute | solution.py:287
  46.5 13.4 %collective-permute-start.5 = (bf16[512,512]{1,0:T(8,128)(2,1)S(1)}, bf16[512,512]{1,0:T(8,128)(2,1)S(1)}, u32[]{:S(2)}, u32[]{:S(2)}) collective-permute-start(bf16[512,512]{1,0:T(8,128)(2,1)S(1)} %shard_map.101), channel_id=1, source_target_pairs={{2,4},{4,2},{3,5},{5,3},{6,8},{8,6},{7,9},{9,7},{10,12},{12,10},{1... | collective-permute-start | bytes 1572872 | tf_op jit(solution)/shard_map/ppermute | solution.py:287
  60.6 2.0 %collective-permute-start.9 = (bf16[512,512]{1,0:T(8,128)(2,1)S(1)}, bf16[512,512]{1,0:T(8,128)(2,1)S(1)}, u32[]{:S(2)}, u32[]{:S(2)}) collective-permute-start(bf16[512,512]{1,0:T(8,128)(2,1)S(1)} %get-tuple-element.18), channel_id=1, source_target_pairs={{0,64},{64,0},{128,192},{192,128},{1,65},{65,1},{129,193},{193,129... | collective-permute-start | bytes 1572872 | tf_op jit(solution)/shard_map/ppermute | solution.py:44
  62.9 16.5 %collective-permute-start.10 = (bf16[512,256]{1,0:T(8,128)(2,1)S(1)}, bf16[512,256]{1,0:T(8,128)(2,1)S(1)}, u32[]{:S(2)}, u32[]{:S(2)}) collective-permute-start(bf16[512,256]{1,0:T(8,128)(2,1)S(1)} %slice.15), channel_id=1, source_target_pairs={{0,128},{128,0},{64,192},{192,64},{1,129},{129,1},{65,193},{193,65... | collective-permute-start | bytes 786440 | tf_op jit(solution)/shard_map/ppermute | solution.py:305

commit v3 on v2

--- a/solution.py
+++ b/solution.py
@@ -15,6 +15,7 @@
 SPAN = 32
 BYS = (2, 1)
 CROSSED = True
+PARTS = 2
 F32 = jnp.float32
 BF16 = jnp.bfloat16
 I32 = jnp.int32
@@ -163,9 +164,10 @@
 
 
 def attend_kernel(
-    turn, heads, runs_ref, own_bias, other_bias, gene_ref, peak_ref, q_ref, k_ref, v_ref, o_ref, acc
+    turn, heads, part, runs_ref, own_bias, other_bias, gene_ref, peak_ref, q_ref, k_ref, v_ref, o_ref, acc
 ):
-    tiles = q_ref.shape[0] // TILE
+    tiles = o_ref.shape[0] // TILE
+    taken = slice(part * tiles * TILE, (part + 1) * tiles * TILE)
     per_chunk = CHUNK // TILE
     dim = TILE
     scale = 0.5 / math.sqrt(dim)
@@ -175,7 +177,8 @@
         by, kind = partner_kind(lax.axis_index("gene") & 1, turn)
         source = jnp.where((me // by) % 2 == kind, me + by, me - by)
     valid = (source >= 0) & (source < count)
-    base = jnp.where(valid, source * tiles - window_origin(tiles), 0)
+    gene_tiles = q_ref.shape[0] // TILE
+    base = jnp.where(valid, source * gene_tiles - window_origin(gene_tiles), 0) + part * tiles
     lows = [runs_ref[0, base + i] for i in range(tiles)]
     highs = [runs_ref[1, base + i] for i in range(tiles)]
     low = functools.reduce(jnp.minimum, lows)
@@ -202,7 +205,7 @@
             cols = slice(h * dim, (h + 1) * dim)
             bias = own_bias[h] if h < local else other_bias[h - local]
             scores = lax.dot_general(
-                q_ref[:, cols], k_ref[rows, cols], (((1,), (1,)), ((), ())), preferred_element_type=F32
+                q_ref[taken, cols], k_ref[rows, cols], (((1,), (1,)), ((), ())), preferred_element_type=F32
             )
             twice = jnp.tanh(scores * scale + 0.5 * bias) + 1.0
             bands = []
@@ -220,26 +223,28 @@
     o_ref[...] = (acc[...] * 0.5).astype(o_ref.dtype)
 
 
-def attend(turn, heads, tables, q, k, v, dtype):
+def attend(turn, heads, tables, q, k, v, dtype, part=0, parts=1):
     runs, own_bias, other_bias, gene, peak = tables
-    shape = (q.shape[0], heads * TILE)
-    return pl.pallas_call(
-        functools.partial(attend_kernel, turn, heads),
+    shape = (q.shape[0] // parts, heads * TILE)
+    return pl.pallas_call(
+        functools.partial(attend_kernel, turn, heads, part),
         in_specs=[SMEM] * 3 + [VMEM] * 5,
         out_specs=VMEM,
         out_shape=jax.ShapeDtypeStruct(shape, dtype),
         scratch_shapes=[pltpu.VMEM(shape, F32)],
-        cost_estimate=cost(4 * q.shape[0] * k.shape[0] * heads * TILE, [q, k, v, q]),
+        cost_estimate=cost(4 * shape[0] * k.shape[0] * heads * TILE, [q, k, v, q]),
         compiler_params=PARAMS,
     )(runs, own_bias, other_bias, gene, peak, q, k, v)
 
 
-def mix_kernel(own_ref, first_ref, second_ref, w1, w2, send_ref, keep_ref):
+def mix_kernel(part, own_ref, first_ref, second_ref, w1, w2, send_ref, keep_ref):
+    rows = slice(part * send_ref.shape[0], (part + 1) * send_ref.shape[0])
     width = w1.shape[1] // 4
     depth = w1.shape[0]
     me = lax.axis_index("gene")
-    mine = own_ref[...] + first_ref[:, :depth].astype(F32) + second_ref[:, :depth].astype(F32)
-    theirs = first_ref[:, depth:].astype(F32) + second_ref[:, depth:].astype(F32)
+    first, second = first_ref[rows, :].astype(F32), second_ref[...].astype(F32)
+    mine = own_ref[rows, :] + first[:, :depth] + second[:, :depth]
+    theirs = first[:, depth:] + second[:, depth:]
     mine, theirs = mine.astype(BF16), theirs.astype(BF16)
 
     def share(block):
@@ -254,17 +259,39 @@
     keep_ref[:, width:] = share(me)
 
 
-def mix(own, first, second, w1, w2):
-    shape = (own.shape[0], w1.shape[1] // 2)
-    return pl.pallas_call(
-        mix_kernel,
+def mix(part, own, first, second, w1, w2):
+    shape = (second.shape[0], w1.shape[1] // 2)
+    return pl.pallas_call(
+        functools.partial(mix_kernel, part),
         in_specs=[VMEM] * 5,
         out_specs=[VMEM, VMEM],
         out_shape=[jax.ShapeDtypeStruct(shape, BF16), jax.ShapeDtypeStruct(shape, F32)],
-        cost_estimate=cost(4 * own.shape[0] * w1.size, [own, w1, w2, own, own]),
-        compiler_params=PARAMS,
-        name="mix",
+        cost_estimate=cost(4 * shape[0] * w1.size, [own, w1, w2, own, own]),
+        compiler_params=PARAMS,
     )(own, first, second, w1, w2)
+
+
+def finish_kernel(*refs):
+    out_ref = refs[-1]
+    parts = (len(refs) - 1) // 2
+    rows, width = refs[parts].shape
+    for part in range(parts):
+        total = refs[part][:, width:] + refs[parts + part][...].astype(F32)
+        out_ref[part * rows : (part + 1) * rows, :] = total.astype(BF16)
+
+
+def finish(halves, others):
+    rows, width = others[0].shape
+    shape = (len(others) * rows, width)
+    return pl.pallas_call(
+        finish_kernel,
+        in_specs=[VMEM] * (2 * len(others)),
+        out_specs=VMEM,
+        out_shape=jax.ShapeDtypeStruct(shape, BF16),
+        cost_estimate=cost(2 * rows * width, halves + others),
+        compiler_params=PARAMS,
+        name="finish",
+    )(*halves, *others)
 
 
 def on_device(
@@ -296,14 +323,22 @@
     )
     tables = (runs, head_bias, core_swap(head_bias), gene, peak)
     first = attend(0, 2 * local, tables, first, keys, values, BF16)
-    second = attend(1, 2 * local, tables, second, keys, values, BF16)
-    first, second = travel(first, 0), travel(second, 1)
+    first = travel(first, 0)
+    seconds = []
+    for part in range(PARTS):
+        rows = attend(1, 2 * local, tables, second, keys, values, BF16, part, PARTS)
+        seconds.append(travel(rows, 1))
     own = attend(None, local, tables, queries, keys, values, F32)
-    send, keep = mix(own, first, second, w_out, core_swap(w_out))
-    width = send.shape[1] // 2
-    half = keep + core_swap(send).astype(F32)
-    other = lax.ppermute(half[:, :width].astype(BF16), "gene", [(0, 2), (2, 0), (1, 3), (3, 1)])
-    return (half[:, width:] + other.astype(F32)).astype(BF16)
+    w_other = core_swap(w_out)
+    halves, others = [], []
+    for part in range(PARTS):
+        send, keep = mix(part, own, first, seconds[part], w_out, w_other)
+        width = send.shape[1] // 2
+        half = keep + core_swap(send).astype(F32)
+        pairs = [(0, 2), (2, 0), (1, 3), (3, 1)]
+        others.append(lax.ppermute(half[:, :width].astype(BF16), "gene", pairs))
+        halves.append(half)
+    return finish(halves, others)
 
 
 def solution(mesh):

time: 80.9 us -> 81.9 us (1.012)
  waiting for transfers between devices: 22.9 us -> 14.1 us
  starting transfers between devices: 33.9 us -> 41.4 us
  Pallas kernels: 19.7 us -> 22.1 us
    ppermute x4 -> x5, waiting for transfers between devices: 8.5 us -> 2.24 us  [travel(): return lax.ppermute(x, ('gene', 'peak'), swap_pairs(genes, count, turn))]
    ppermute x6 -> x7, starting transfers between devices: 1.86 us -> 6.34 us  [core_swap(): return lax.ppermute(x, 'gene', [(0, 1), (1, 0), (2, 3), (3, 2)])]
    ppermute x1 -> x2, starting transfers between devices: 3.99 us -> 8.46 us  [on_device(): others.append(lax.ppermute(half[:, :width].astype(BF16), 'gene', pairs))]
    pallas_call x4 -> x7, Pallas kernels: 13.6 us -> 16 us  [the longest x4 14.3 us: attend(): pl.pallas_call(functools.partial(attend_kernel, turn, heads, part), in_sp...]
    ppermute x4 -> x5, starting transfers between devices: 28.1 us -> 26.6 us  [travel(): return lax.ppermute(x, ('gene', 'peak'), swap_pairs(genes, count, turn))]
    ppermute x6 -> x7, waiting for transfers between devices: 1.91 us -> 0.5 us  [core_swap(): return lax.ppermute(x, 'gene', [(0, 1), (1, 0), (2, 3), (3, 2)])]
    ppermute x1 -> x2, waiting for transfers between devices: 12.5 us -> 11.3 us  [on_device(): others.append(lax.ppermute(half[:, :width].astype(BF16), 'gene', pairs))]
  transfers between devices with their start and end apart: 11 -> 14, of which waited for: 4 -> 4; matrix products, arithmetic and copies ran while one was open for 0% -> 0% of each run, Pallas kernels for 24% -> 27%
where the time goes in v3:
time: 81.9 us; the launch traced here: 80.4 us
  starting transfers between devices  41.4 us (51%)
  Pallas kernels  22.1 us (27%)
  waiting for transfers between devices  14.1 us (17%)
  local copies, waits for them, and re-layouts  2.36 us (3%)
    ppermute x5, starting transfers between devices, travel(): return lax.ppermute(x, ('gene', 'peak'), swap_pairs(genes, count, turn))  26.6 us
    pallas_call x4, Pallas kernels, attend(): pl.pallas_call(functools.partial(attend_kernel, turn, heads, part), in_sp...  14.3 us
    ppermute x2, waiting for transfers between devices, on_device(): others.append(lax.ppermute(half[:, :width].astype(BF16), 'gene', pairs))  11.3 us
    ppermute x2, starting transfers between devices, on_device(): others.append(lax.ppermute(half[:, :width].astype(BF16), 'gene', pairs))  8.46 us
    ppermute x7, starting transfers between devices, core_swap(): return lax.ppermute(x, 'gene', [(0, 1), (1, 0), (2, 3), (3, 2)])  6.34 us
    pallas_call x1, Pallas kernels, project_kv(): pl.pallas_call(functools.partial(kv_kernel, gene_tiles), in_specs=[VMEM]...  5.25 us
    unnamed x20, local copies, waits for them, and re-layouts  2.32 us
    ppermute x5, waiting for transfers between devices, travel(): return lax.ppermute(x, ('gene', 'peak'), swap_pairs(genes, count, turn))  2.24 us
  transfers between devices with their start and end apart: 14, of which 4 were waited for; matrix products, arithmetic and copies ran while one was open for 0% of the time, Pallas kernels for 27%

profile of v3, /device:TPU:3, one launch (start us, length us, event | category | flops | bytes accessed | tf_op | source)
XLA Modules:
  0.0 80.4 jit_solution(912825036690273811)
XLA Ops:
  0.0 0.7 collective-permute-start.3
  0.7 0.0 collective-permute-start
  0.7 0.5 collective-permute-start.1
  1.2 0.0 copy-start.1
  1.2 1.2 %copy-done.1 = bf16[512,1024]{1,0:T(8,128)(2,1)S(1)} copy-done((bf16[512,1024]{1,0:T(8,128)(2,1)S(1)}, bf16[512,1024]{1,0:T(8,128)(2,1)}, u32[]{:S(2)}) %copy-start.1) | copy-done | bytes 1048600
  2.4 0.0 copy-start.2
  2.4 1.0 %copy-done.2 = bf16[1024,256]{1,0:T(8,128)(2,1)S(1)} copy-done((bf16[1024,256]{1,0:T(8,128)(2,1)S(1)}, bf16[1024,256]{1,0:T(8,128)(2,1)}, u32[]{:S(2)}) %copy-start.2) | copy-done | bytes 524312
  3.5 0.4 project_queries.1.own_ref
  3.9 0.0 copy-start.3
  3.9 0.0 copy-start
  3.9 0.0 copy-start.4
  3.9 0.0 copy-start.5
  3.9 0.0 copy-start.6
  4.0 0.0 copy-start.7
  4.0 0.0 copy-start.8
  4.0 0.0 copy-start.9
  4.0 0.0 collective-permute-done.3.w_ref
  4.0 0.4 join_queries.1.q_ref
  4.4 5.1 %collective-permute-start.4 = (bf16[512,512]{1,0:T(8,128)(2,1)S(1)}, bf16[512,512]{1,0:T(8,128)(2,1)S(1)}, u32[]{:S(2)}, u32[]{:S(2)}) collective-permute-start(bf16[512,512]{1,0:T(8,128)(2,1)S(1)} %join_queries.1.q_ref), channel_id=1, source_target_pairs={{2,4},{4,2},{3,5},{5,3},{6,8},{8,6},{7,9},{9,7},{10,12},{12,10},{1... | collective-permute-start | bytes 1572872 | tf_op jit(solution)/shard_map/ppermute | solution.py:314
  9.5 0.0 copy-done.3
  9.6 4.4 %collective-permute-start.2 = (f32[2]{0:T(128)S(1)}, f32[2]{0:T(128)S(1)}, u32[]{:S(2)}, u32[]{:S(2)}) collective-permute-start(f32[2]{0:T(128)S(1)} %copy-done.3), channel_id=1, source_target_pairs={{0,64},{64,0},{128,192},{192,128},{1,65},{65,1},{129,193},{193,129... | collective-permute-start | bytes 32 | tf_op jit(solution)/shard_map/ppermute | solution.py:45
  14.0 0.0 copy-done
  14.0 0.1 collective-permute-start.8
  14.1 0.0 collective-permute-done.wk2
  14.1 2.8 %collective-permute-start.6 = (bf16[512,512]{1,0:T(8,128)(2,1)S(1)}, bf16[512,512]{1,0:T(8,128)(2,1)S(1)}, u32[]{:S(2)}, u32[]{:S(2)}) collective-permute-start(bf16[512,512]{1,0:T(8,128)(2,1)S(1)} %join_queries.1.q_ref), channel_id=1, source_target_pairs={{0,1},{1,0},{2,3},{3,2},{4,5},{5,4},{6,7},{7,6},{8,9},{9,8},{10,11... | collective-permute-start | bytes 1572872 | tf_op jit(solution)/shard_map/ppermute | solution.py:314
  16.9 0.0 collective-permute-done.1.wv2
  16.9 0.0 copy-done.4
  16.9 0.0 copy-done.5
  16.9 0.0 copy-done.6
  16.9 0.0 copy-done.7
  16.9 0.0 copy-done.8
  16.9 0.0 copy-done.9
  16.9 5.2 %project_kv.1 = (bf16[2048,512]{1,0:T(8,128)(2,1)S(1)}, bf16[2048,512]{1,0:T(8,128)(2,1)S(1)}, s32[8,128]{1,0:T(8,128)S(1)}, s32[32,128]{1,0:T(8,128)S(1)}, s32[16,128]{1,0:T(8,128)S(1)}) custom-call(bf16[2048,1024]{1,0:T(8,128)(2,1)S(1)} %copy-done.4, bf16[1024,256]{1,0:T(8,128)(2,1)S(1)} %copy-done.6, bf16[1024,256]{1,0:T(8,128)(2,1)S(1)} %collective-permute-done.wk2, ...), custom_call_target="tpu_custom_call" | custom-call | flops 4294967296 | bytes 8388608 | tf_op jit(solution)/shard_map/project_kv/pallas_call | solution.py:144
  22.2 0.0 collective-permute-done.2.other_bias
  22.2 2.2 %collective-permute-done.4.q_ref = bf16[512,512]{1,0:T(8,128)(2,1)S(1)} collective-permute-done((bf16[512,512]{1,0:T(8,128)(2,1)S(1)}, bf16[512,512]{1,0:T(8,128)(2,1)S(1)}, u32[]{:S(2)}, u32[]{:S(2)}) %collective-permute-start.4) | collective-permute-done | bytes 524320 | tf_op jit(solution)/shard_map/ppermute | solution.py:314
  24.4 6.5 %shard_map.101 = bf16[512,512]{1,0:T(8,128)(2,1)S(1)} custom-call(s32[8,128]{1,0:T(8,128)S(1)} %get-tuple-element.14.runs_ref, f32[2]{0:T(128)S(1)} %copy-done.3, f32[2]{0:T(128)S(1)} %collective-permute-done.2.other_bias, s32[32,128]{1,0:T(8,128)S(1)} %get-tuple-element.15.gene_ref, s32[16,128]{1,0:T(8,128)S(1)} %get-tuple-element.16.peak_ref, ...), custom_call_target="tpu_custom_call" | custom-call | flops 2147483648 | bytes 5242880 | tf_op jit(solution)/shard_map/pallas_call | solution.py:229
  31.0 5.3 %collective-permute-start.5 = (bf16[512,512]{1,0:T(8,128)(2,1)S(1)}, bf16[512,512]{1,0:T(8,128)(2,1)S(1)}, u32[]{:S(2)}, u32[]{:S(2)}) collective-permute-start(bf16[512,512]{1,0:T(8,128)(2,1)S(1)} %shard_map.101), channel_id=1, source_target_pairs={{2,4},{4,2},{3,5},{5,3},{6,8},{8,6},{7,9},{9,7},{10,12},{12,10},{1... | collective-permute-start | bytes 1572872 | tf_op jit(solution)/shard_map/ppermute | solution.py:314
  36.3 0.0 collective-permute-done.6.q_ref
  36.3 1.9 %shard_map.104 = bf16[256,512]{1,0:T(8,128)(2,1)S(1)} custom-call(s32[8,128]{1,0:T(8,128)S(1)} %get-tuple-element.14.runs_ref, f32[2]{0:T(128)S(1)} %copy-done.3, f32[2]{0:T(128)S(1)} %collective-permute-done.2.other_bias, s32[32,128]{1,0:T(8,128)S(1)} %get-tuple-element.15.gene_ref, s32[16,128]{1,0:T(8,128)S(1)} %get-tuple-element.16.peak_ref, ...), custom_call_target="tpu_custom_call" | custom-call | flops 1073741824 | bytes 5242880 | tf_op jit(solution)/shard_map/pallas_call | solution.py:229
  38.2 1.9 %collective-permute-start.10 = (bf16[256,512]{1,0:T(8,128)(2,1)S(1)}, bf16[256,512]{1,0:T(8,128)(2,1)S(1)}, u32[]{:S(2)}, u32[]{:S(2)}) collective-permute-start(bf16[256,512]{1,0:T(8,128)(2,1)S(1)} %shard_map.104), channel_id=1, source_target_pairs={{0,1},{1,0},{2,3},{3,2},{4,5},{5,4},{6,7},{7,6},{8,9},{9,8},{10,11... | collective-permute-start | bytes 786440 | tf_op jit(solution)/shard_map/ppermute | solution.py:314
  40.1 1.8 %shard_map.102 = bf16[256,512]{1,0:T(8,128)(2,1)S(1)} custom-call(s32[8,128]{1,0:T(8,128)S(1)} %get-tuple-element.14.runs_ref, f32[2]{0:T(128)S(1)} %copy-done.3, f32[2]{0:T(128)S(1)} %collective-permute-done.2.other_bias, s32[32,128]{1,0:T(8,128)S(1)} %get-tuple-element.15.gene_ref, s32[16,128]{1,0:T(8,128)S(1)} %get-tuple-element.16.peak_ref, ...), custom_call_target="tpu_custom_call" | custom-call | flops 1073741824 | bytes 5242880 | tf_op jit(solution)/shard_map/pallas_call | solution.py:229
  42.0 11.4 %collective-permute-start.7 = (bf16[256,512]{1,0:T(8,128)(2,1)S(1)}, bf16[256,512]{1,0:T(8,128)(2,1)S(1)}, u32[]{:S(2)}, u32[]{:S(2)}) collective-permute-start(bf16[256,512]{1,0:T(8,128)(2,1)S(1)} %shard_map.102), channel_id=1, source_target_pairs={{0,1},{1,0},{2,3},{3,2},{4,5},{5,4},{6,7},{7,6},{8,9},{9,8},{10,11... | collective-permute-start | bytes 786440 | tf_op jit(solution)/shard_map/ppermute | solution.py:314
  53.4 4.1 %shard_map.100.own_ref = f32[512,256]{1,0:T(8,128)S(1)} custom-call(s32[8,128]{1,0:T(8,128)S(1)} %get-tuple-element.14.runs_ref, f32[2]{0:T(128)S(1)} %copy-done.3, f32[2]{0:T(128)S(1)} %collective-permute-done.2.other_bias, s32[32,128]{1,0:T(8,128)S(1)} %get-tuple-element.15.gene_ref, s32[16,128]{1,0:T(8,128)S(1)} %get-tuple-element.16.peak_ref, ...), custom_call_target="tpu_custom_call" | custom-call | flops 1073741824 | bytes 5242880 | tf_op jit(solution)/shard_map/pallas_call | solution.py:229
  57.5 0.0 collective-permute-done.8.w2
  57.5 0.0 collective-permute-done.10.second_ref
  57.5 0.0 collective-permute-done.5.first_ref
  57.5 0.5 shard_map.105
  58.0 0.1 collective-permute-start.11
  58.1 0.0 collective-permute-done.7.second_ref
  58.1 0.5 shard_map.103
  58.6 0.6 collective-permute-start.9
  59.1 0.5 collective-permute-done.11
  59.6 0.1 convert_add_fusion.refs_1_
  59.7 7.9 %collective-permute-start.13 = (bf16[256,256]{1,0:T(8,128)(2,1)S(1)}, bf16[256,256]{1,0:T(8,128)(2,1)S(1)}, u32[]{:S(2)}, u32[]{:S(2)}) collective-permute-start(bf16[256,256]{1,0:T(8,128)(2,1)S(1)} %slice.14), channel_id=1, source_target_pairs={{0,128},{128,0},{64,192},{192,64},{1,129},{129,1},{65,193},{193,65... | collective-permute-start | bytes 393224 | tf_op jit(solution)/shard_map/ppermute | solution.py:339
  67.6 0.0 collective-permute-done.9
  67.6 0.1 convert_add_fusion.1.refs_0_
  67.7 0.6 collective-permute-start.12
  68.3 8.5 %collective-permute-done.13.refs_3_ = bf16[256,256]{1,0:T(8,128)(2,1)S(1)} collective-permute-done((bf16[256,256]{1,0:T(8,128)(2,1)S(1)}, bf16[256,256]{1,0:T(8,128)(2,1)S(1)}, u32[]{:S(2)}, u32[]{:S(2)}) %collective-permute-start.13) | collective-permute-done | bytes 131104 | tf_op jit(solution)/shard_map/ppermute | solution.py:339
  76.8 2.8 %collective-permute-done.12.refs_2_ = bf16[256,256]{1,0:T(8,128)(2,1)S(1)} collective-permute-done((bf16[256,256]{1,0:T(8,128)(2,1)S(1)}, bf16[256,256]{1,0:T(8,128)(2,1)S(1)}, u32[]{:S(2)}, u32[]{:S(2)}) %collective-permute-start.12) | collective-permute-done | bytes 131104 | tf_op jit(solution)/shard_map/ppermute | solution.py:339
  79.6 0.7 finish.1
  (2 shorter events, 0.0 us)
Async XLA Ops:
  0.0 4.0 %collective-permute-start.3 = (bf16[1024,256]{1,0:T(8,128)(2,1)}, bf16[1024,256]{1,0:T(8,128)(2,1)S(1)}, u32[]{:S(2)}, u32[]{:S(2)}) collective-permute-start(bf16[1024,256]{1,0:T(8,128)(2,1)} %w_ref.1), channel_id=1, source_target_pairs={{0,64},{64,0},{128,192},{192,128},{1,65},{65,1},{129,193},{193,129... | collective-permute-start | bytes 1572872 | tf_op jit(solution)/shard_map/ppermute | solution.py:45
  0.7 13.4 %collective-permute-start = (bf16[1024,256]{1,0:T(8,128)(2,1)}, bf16[1024,256]{1,0:T(8,128)(2,1)S(1)}, u32[]{:S(2)}, u32[]{:S(2)}) collective-permute-start(bf16[1024,256]{1,0:T(8,128)(2,1)} %wk1.1), channel_id=1, source_target_pairs={{0,64},{64,0},{128,192},{192,128},{1,65},{65,1},{129,193},{193,129... | collective-permute-start | bytes 1572872 | tf_op jit(solution)/shard_map/ppermute | solution.py:45
  0.7 16.2 %collective-permute-start.1 = (bf16[1024,256]{1,0:T(8,128)(2,1)}, bf16[1024,256]{1,0:T(8,128)(2,1)S(1)}, u32[]{:S(2)}, u32[]{:S(2)}) collective-permute-start(bf16[1024,256]{1,0:T(8,128)(2,1)} %wv1.1), channel_id=1, source_target_pairs={{0,64},{64,0},{128,192},{192,128},{1,65},{65,1},{129,193},{193,129... | collective-permute-start | bytes 1572872 | tf_op jit(solution)/shard_map/ppermute | solution.py:45
  1.2 1.2 %copy-start.1 = (bf16[512,1024]{1,0:T(8,128)(2,1)S(1)}, bf16[512,1024]{1,0:T(8,128)(2,1)}, u32[]{:S(2)}) copy-start(bf16[512,1024]{1,0:T(8,128)(2,1)} %act_ref.5) | copy-start | bytes 3145732
  2.4 1.0 %copy-start.2 = (bf16[1024,256]{1,0:T(8,128)(2,1)S(1)}, bf16[1024,256]{1,0:T(8,128)(2,1)}, u32[]{:S(2)}) copy-start(bf16[1024,256]{1,0:T(8,128)(2,1)} %w_ref.1) | copy-start | bytes 1572868
  3.9 5.7 %copy-start.3 = (f32[2]{0:T(128)S(1)}, f32[2]{0:T(128)}, u32[]{:S(2)}) copy-start(f32[2]{0:T(128)} %own_bias.7) | copy-start | bytes 28
  3.9 10.1 %copy-start = (bf16[256,1024]{1,0:T(8,128)(2,1)S(1)}, bf16[256,1024]{1,0:T(8,128)(2,1)}, u32[]{:S(2)}) copy-start(bf16[256,1024]{1,0:T(8,128)(2,1)} %w1.3) | copy-start | bytes 1572868
  3.9 13.0 %copy-start.4 = (bf16[2048,1024]{1,0:T(8,128)(2,1)S(1)}, bf16[2048,1024]{1,0:T(8,128)(2,1)}, u32[]{:S(2)}) copy-start(bf16[2048,1024]{1,0:T(8,128)(2,1)} %act_ref.3) | copy-start | bytes 12582916
  3.9 13.0 %copy-start.5 = (s32[256,1024]{1,0:T(8,128)S(1)}, s32[256,1024]{1,0:T(8,128)}, u32[]{:S(2)}) copy-start(s32[256,1024]{1,0:T(8,128)} %mask_hbm.1) | copy-start | bytes 3145732
  3.9 13.0 %copy-start.6 = (bf16[1024,256]{1,0:T(8,128)(2,1)S(1)}, bf16[1024,256]{1,0:T(8,128)(2,1)}, u32[]{:S(2)}) copy-start(bf16[1024,256]{1,0:T(8,128)(2,1)} %wk1.1) | copy-start | bytes 1572868
  4.0 13.0 %copy-start.7 = (bf16[1024,256]{1,0:T(8,128)(2,1)S(1)}, bf16[1024,256]{1,0:T(8,128)(2,1)}, u32[]{:S(2)}) copy-start(bf16[1024,256]{1,0:T(8,128)(2,1)} %wv1.1) | copy-start | bytes 1572868
  4.0 13.0 %copy-start.8 = (s32[131072]{0:T(1024)S(1)}, s32[131072]{0:T(1024)}, u32[]{:S(2)}) copy-start(s32[131072]{0:T(1024)} %param.19) | copy-start | bytes 1572868
  4.0 13.0 %copy-start.9 = (s32[32768]{0:T(1024)S(1)}, s32[32768]{0:T(1024)}, u32[]{:S(2)}) copy-start(s32[32768]{0:T(1024)} %param.18) | copy-start | bytes 393220
  4.4 20.0 %collective-permute-start.4 = (bf16[512,512]{1,0:T(8,128)(2,1)S(1)}, bf16[512,512]{1,0:T(8,128)(2,1)S(1)}, u32[]{:S(2)}, u32[]{:S(2)}) collective-permute-start(bf16[512,512]{1,0:T(8,128)(2,1)S(1)} %join_queries.1.q_ref), channel_id=1, source_target_pairs={{2,4},{4,2},{3,5},{5,3},{6,8},{8,6},{7,9},{9,7},{10,12},{12,10},{1... | collective-permute-start | bytes 1572872 | tf_op jit(solution)/shard_map/ppermute | solution.py:314
  9.6 12.6 %collective-permute-start.2 = (f32[2]{0:T(128)S(1)}, f32[2]{0:T(128)S(1)}, u32[]{:S(2)}, u32[]{:S(2)}) collective-permute-start(f32[2]{0:T(128)S(1)} %copy-done.3), channel_id=1, source_target_pairs={{0,64},{64,0},{128,192},{192,128},{1,65},{65,1},{129,193},{193,129... | collective-permute-start | bytes 32 | tf_op jit(solution)/shard_map/ppermute | solution.py:45
  14.0 43.5 %collective-permute-start.8 = (bf16[256,1024]{1,0:T(8,128)(2,1)S(1)}, bf16[256,1024]{1,0:T(8,128)(2,1)S(1)}, u32[]{:S(2)}, u32[]{:S(2)}) collective-permute-start(bf16[256,1024]{1,0:T(8,128)(2,1)S(1)} %copy-done), channel_id=1, source_target_pairs={{0,64},{64,0},{128,192},{192,128},{1,65},{65,1},{129,193},{193,129... | collective-permute-start | bytes 1572872 | tf_op jit(solution)/shard_map/ppermute | solution.py:45
  14.1 22.2 %collective-permute-start.6 = (bf16[512,512]{1,0:T(8,128)(2,1)S(1)}, bf16[512,512]{1,0:T(8,128)(2,1)S(1)}, u32[]{:S(2)}, u32[]{:S(2)}) collective-permute-start(bf16[512,512]{1,0:T(8,128)(2,1)S(1)} %join_queries.1.q_ref), channel_id=1, source_target_pairs={{0,1},{1,0},{2,3},{3,2},{4,5},{5,4},{6,7},{7,6},{8,9},{9,8},{10,11... | collective-permute-start | bytes 1572872 | tf_op jit(solution)/shard_map/ppermute | solution.py:314
  31.0 26.5 %collective-permute-start.5 = (bf16[512,512]{1,0:T(8,128)(2,1)S(1)}, bf16[512,512]{1,0:T(8,128)(2,1)S(1)}, u32[]{:S(2)}, u32[]{:S(2)}) collective-permute-start(bf16[512,512]{1,0:T(8,128)(2,1)S(1)} %shard_map.101), channel_id=1, source_target_pairs={{2,4},{4,2},{3,5},{5,3},{6,8},{8,6},{7,9},{9,7},{10,12},{12,10},{1... | collective-permute-start | bytes 1572872 | tf_op jit(solution)/shard_map/ppermute | solution.py:314
  38.2 19.3 %collective-permute-start.10 = (bf16[256,512]{1,0:T(8,128)(2,1)S(1)}, bf16[256,512]{1,0:T(8,128)(2,1)S(1)}, u32[]{:S(2)}, u32[]{:S(2)}) collective-permute-start(bf16[256,512]{1,0:T(8,128)(2,1)S(1)} %shard_map.104), channel_id=1, source_target_pairs={{0,1},{1,0},{2,3},{3,2},{4,5},{5,4},{6,7},{7,6},{8,9},{9,8},{10,11... | collective-permute-start | bytes 786440 | tf_op jit(solution)/shard_map/ppermute | solution.py:314
  42.0 16.1 %collective-permute-start.7 = (bf16[256,512]{1,0:T(8,128)(2,1)S(1)}, bf16[256,512]{1,0:T(8,128)(2,1)S(1)}, u32[]{:S(2)}, u32[]{:S(2)}) collective-permute-start(bf16[256,512]{1,0:T(8,128)(2,1)S(1)} %shard_map.102), channel_id=1, source_target_pairs={{0,1},{1,0},{2,3},{3,2},{4,5},{5,4},{6,7},{7,6},{8,9},{9,8},{10,11... | collective-permute-start | bytes 786440 | tf_op jit(solution)/shard_map/ppermute | solution.py:314
  58.0 1.6 %collective-permute-start.11 = (bf16[256,512]{1,0:T(8,128)(2,1)S(1)}, bf16[256,512]{1,0:T(8,128)(2,1)S(1)}, u32[]{:S(2)}, u32[]{:S(2)}) collective-permute-start(bf16[256,512]{1,0:T(8,128)(2,1)S(1)} %get-tuple-element.22), channel_id=1, source_target_pairs={{0,64},{64,0},{128,192},{192,128},{1,65},{65,1},{129,193},{193,129... | collective-permute-start | bytes 786440 | tf_op jit(solution)/shard_map/ppermute | solution.py:45
  58.6 9.0 %collective-permute-start.9 = (bf16[256,512]{1,0:T(8,128)(2,1)S(1)}, bf16[256,512]{1,0:T(8,128)(2,1)S(1)}, u32[]{:S(2)}, u32[]{:S(2)}) collective-permute-start(bf16[256,512]{1,0:T(8,128)(2,1)S(1)} %get-tuple-element.20), channel_id=1, source_target_pairs={{0,64},{64,0},{128,192},{192,128},{1,65},{65,1},{129,193},{193,129... | collective-permute-start | bytes 786440 | tf_op jit(solution)/shard_map/ppermute | solution.py:45
  59.7 17.1 %collective-permute-start.13 = (bf16[256,256]{1,0:T(8,128)(2,1)S(1)}, bf16[256,256]{1,0:T(8,128)(2,1)S(1)}, u32[]{:S(2)}, u32[]{:S(2)}) collective-permute-start(bf16[256,256]{1,0:T(8,128)(2,1)S(1)} %slice.14), channel_id=1, source_target_pairs={{0,128},{128,0},{64,192},{192,64},{1,129},{129,1},{65,193},{193,65... | collective-permute-start | bytes 393224 | tf_op jit(solution)/shard_map/ppermute | solution.py:339
  67.7 11.9 %collective-permute-start.12 = (bf16[256,256]{1,0:T(8,128)(2,1)S(1)}, bf16[256,256]{1,0:T(8,128)(2,1)S(1)}, u32[]{:S(2)}, u32[]{:S(2)}) collective-permute-start(bf16[256,256]{1,0:T(8,128)(2,1)S(1)} %slice.15), channel_id=1, source_target_pairs={{0,128},{128,0},{64,192},{192,64},{1,129},{129,1},{65,193},{193,65... | collective-permute-start | bytes 393224 | tf_op jit(solution)/shard_map/ppermute | solution.py:339

commit v4 on v3

--- a/solution.py
+++ b/solution.py
@@ -11,11 +11,12 @@
 
 TILE = 128
 REACH = 2
-CHUNK = 512
+CHUNK = 1024
+BLOCK = 512
 SPAN = 32
 BYS = (2, 1)
 CROSSED = True
-PARTS = 2
+PARTS = 1
 F32 = jnp.float32
 BF16 = jnp.bfloat16
 I32 = jnp.int32
@@ -112,7 +113,7 @@
     width = wk1.shape[1]
 
     def block(i, carry):
-        rows = pl.ds(pl.multiple_of(i * CHUNK, CHUNK), CHUNK)
+        rows = pl.ds(pl.multiple_of(i * BLOCK, BLOCK), BLOCK)
         act = act_ref[rows, :]
         k_ref[rows, :width] = jnp.dot(act, wk1[...], preferred_element_type=F32).astype(BF16)
         v_ref[rows, :width] = jnp.dot(act, wv1[...], preferred_element_type=F32).astype(BF16)
@@ -120,7 +121,7 @@
         v_ref[rows, width:] = jnp.dot(act, wv2[...], preferred_element_type=F32).astype(BF16)
         return carry
 
-    lax.fori_loop(0, act_ref.shape[0] // CHUNK, block, 0)
+    lax.fori_loop(0, act_ref.shape[0] // BLOCK, block, 0)
     for copy in copies:
         copy.wait()
     blank = jnp.zeros((TILE - SPAN, TILE), I32)
@@ -164,10 +165,10 @@
 
 
 def attend_kernel(
-    turn, heads, part, runs_ref, own_bias, other_bias, gene_ref, peak_ref, q_ref, k_ref, v_ref, o_ref, acc
+    turn, heads, runs_ref, own_bias, other_bias, gene_ref, peak_ref, q_ref, k_ref, v_ref, *rest
 ):
-    tiles = o_ref.shape[0] // TILE
-    taken = slice(part * tiles * TILE, (part + 1) * tiles * TILE)
+    *o_refs, acc = rest
+    tiles = q_ref.shape[0] // TILE
     per_chunk = CHUNK // TILE
     dim = TILE
     scale = 0.5 / math.sqrt(dim)
@@ -177,8 +178,7 @@
         by, kind = partner_kind(lax.axis_index("gene") & 1, turn)
         source = jnp.where((me // by) % 2 == kind, me + by, me - by)
     valid = (source >= 0) & (source < count)
-    gene_tiles = q_ref.shape[0] // TILE
-    base = jnp.where(valid, source * gene_tiles - window_origin(gene_tiles), 0) + part * tiles
+    base = jnp.where(valid, source * tiles - window_origin(tiles), 0)
     lows = [runs_ref[0, base + i] for i in range(tiles)]
     highs = [runs_ref[1, base + i] for i in range(tiles)]
     low = functools.reduce(jnp.minimum, lows)
@@ -205,7 +205,7 @@
             cols = slice(h * dim, (h + 1) * dim)
             bias = own_bias[h] if h < local else other_bias[h - local]
             scores = lax.dot_general(
-                q_ref[taken, cols], k_ref[rows, cols], (((1,), (1,)), ((), ())), preferred_element_type=F32
+                q_ref[:, cols], k_ref[rows, cols], (((1,), (1,)), ((), ())), preferred_element_type=F32
             )
             twice = jnp.tanh(scores * scale + 0.5 * bias) + 1.0
             bands = []
@@ -220,19 +220,21 @@
         return carry
 
     lax.fori_loop(first, last, chunk, 0)
-    o_ref[...] = (acc[...] * 0.5).astype(o_ref.dtype)
-
-
-def attend(turn, heads, tables, q, k, v, dtype, part=0, parts=1):
+    size = o_refs[0].shape[0]
+    for i, o_ref in enumerate(o_refs):
+        o_ref[...] = (acc[i * size : (i + 1) * size, :] * 0.5).astype(o_ref.dtype)
+
+
+def attend(turn, heads, tables, q, k, v, dtype, parts=1):
     runs, own_bias, other_bias, gene, peak = tables
-    shape = (q.shape[0] // parts, heads * TILE)
-    return pl.pallas_call(
-        functools.partial(attend_kernel, turn, heads, part),
+    rows, width = q.shape[0], heads * TILE
+    return pl.pallas_call(
+        functools.partial(attend_kernel, turn, heads),
         in_specs=[SMEM] * 3 + [VMEM] * 5,
-        out_specs=VMEM,
-        out_shape=jax.ShapeDtypeStruct(shape, dtype),
-        scratch_shapes=[pltpu.VMEM(shape, F32)],
-        cost_estimate=cost(4 * shape[0] * k.shape[0] * heads * TILE, [q, k, v, q]),
+        out_specs=[VMEM] * parts,
+        out_shape=[jax.ShapeDtypeStruct((rows // parts, width), dtype)] * parts,
+        scratch_shapes=[pltpu.VMEM((rows, width), F32)],
+        cost_estimate=cost(4 * rows * k.shape[0] * width, [q, k, v, q]),
         compiler_params=PARAMS,
     )(runs, own_bias, other_bias, gene, peak, q, k, v)
 
@@ -322,13 +324,11 @@
         gene_tiles, peak_act, w_key, w_value, block_mask, gene, peak
     )
     tables = (runs, head_bias, core_swap(head_bias), gene, peak)
-    first = attend(0, 2 * local, tables, first, keys, values, BF16)
+    (first,) = attend(0, 2 * local, tables, first, keys, values, BF16)
     first = travel(first, 0)
-    seconds = []
-    for part in range(PARTS):
-        rows = attend(1, 2 * local, tables, second, keys, values, BF16, part, PARTS)
-        seconds.append(travel(rows, 1))
-    own = attend(None, local, tables, queries, keys, values, F32)
+    seconds = attend(1, 2 * local, tables, second, keys, values, BF16, PARTS)
+    seconds = [travel(rows, 1) for rows in seconds]
+    (own,) = attend(None, local, tables, queries, keys, values, F32)
     w_other = core_swap(w_out)
     halves, others = [], []
     for part in range(PARTS):

time: 81.9 us -> 80.5 us (0.983); the launches traced: 80.4 us -> 80.3 us
  waiting for transfers between devices: 14.1 us -> 22.8 us
  starting transfers between devices: 41.4 us -> 33.6 us
  Pallas kernels: 22.1 us -> 21.1 us
    ppermute x5 -> x4, waiting for transfers between devices: 2.24 us -> 9.02 us  [travel(): return lax.ppermute(x, ('gene', 'peak'), swap_pairs(genes, count, turn))]
    ppermute x7 -> x6, starting transfers between devices: 6.34 us -> 1.86 us  [core_swap(): return lax.ppermute(x, 'gene', [(0, 1), (1, 0), (2, 3), (3, 2)])]
    ppermute x2 -> x1, starting transfers between devices: 8.46 us -> 5.33 us  [on_device(): others.append(lax.ppermute(half[:, :width].astype(BF16), 'gene', pairs))]
    ppermute x7 -> x6, waiting for transfers between devices: 0.5 us -> 1.91 us  [core_swap(): return lax.ppermute(x, 'gene', [(0, 1), (1, 0), (2, 3), (3, 2)])]
    pallas_call x4 -> x3, Pallas kernels: 14.3 us -> 13.5 us  [attend(): pl.pallas_call(functools.partial(attend_kernel, turn, heads), in_specs=[S...]
    ppermute x2 -> x1, waiting for transfers between devices: 11.3 us -> 11.8 us  [on_device(): others.append(lax.ppermute(half[:, :width].astype(BF16), 'gene', pairs))]
    ppermute x5 -> x4, starting transfers between devices: 26.6 us -> 26.4 us  [travel(): return lax.ppermute(x, ('gene', 'peak'), swap_pairs(genes, count, turn))]
  transfers between devices with their start and end apart: 14 -> 11, of which waited for: 4 -> 4; matrix products, arithmetic and copies ran while one was open for 0% -> 0% of each run, Pallas kernels for 27% -> 24%
where the time goes in v4:
time: 80.5 us; the launch traced here: 80.3 us
  starting transfers between devices  33.6 us (42%)
  waiting for transfers between devices  22.8 us (28%)
  Pallas kernels  21.1 us (26%)
  local copies, waits for them, and re-layouts  2.35 us (3%)
    ppermute x4, starting transfers between devices, travel(): return lax.ppermute(x, ('gene', 'peak'), swap_pairs(genes, count, turn))  26.4 us
    pallas_call x3, Pallas kernels, attend(): pl.pallas_call(functools.partial(attend_kernel, turn, heads), in_specs=[S...  13.5 us
    ppermute x1, waiting for transfers between devices, on_device(): others.append(lax.ppermute(half[:, :width].astype(BF16), 'gene', pairs))  11.8 us
    ppermute x4, waiting for transfers between devices, travel(): return lax.ppermute(x, ('gene', 'peak'), swap_pairs(genes, count, turn))  9.02 us
    ppermute x1, starting transfers between devices, on_device(): others.append(lax.ppermute(half[:, :width].astype(BF16), 'gene', pairs))  5.33 us
    pallas_call x1, Pallas kernels, project_kv(): pl.pallas_call(functools.partial(kv_kernel, gene_tiles), in_specs=[VMEM]...  5.25 us
    unnamed x20, local copies, waits for them, and re-layouts  2.32 us
    ppermute x6, waiting for transfers between devices, core_swap(): return lax.ppermute(x, 'gene', [(0, 1), (1, 0), (2, 3), (3, 2)])  1.91 us
  transfers between devices with their start and end apart: 11, of which 4 were waited for; matrix products, arithmetic and copies ran while one was open for 0% of the time, Pallas kernels for 24%

profile of v4, /device:TPU:3, one launch (start us, length us, event | category | flops | bytes accessed | tf_op | source)
XLA Modules:
  0.0 80.3 jit_solution(4249811093043180671)
XLA Ops:
  0.0 0.7 collective-permute-start.3
  0.7 0.0 collective-permute-start
  0.7 0.5 collective-permute-start.1
  1.2 0.0 copy-start
  1.2 1.2 %copy-done = bf16[512,1024]{1,0:T(8,128)(2,1)S(1)} copy-done((bf16[512,1024]{1,0:T(8,128)(2,1)S(1)}, bf16[512,1024]{1,0:T(8,128)(2,1)}, u32[]{:S(2)}) %copy-start) | copy-done | bytes 1048600
  2.4 0.0 copy-start.1
  2.4 1.0 %copy-done.1 = bf16[1024,256]{1,0:T(8,128)(2,1)S(1)} copy-done((bf16[1024,256]{1,0:T(8,128)(2,1)S(1)}, bf16[1024,256]{1,0:T(8,128)(2,1)}, u32[]{:S(2)}) %copy-start.1) | copy-done | bytes 524312
  3.5 0.4 project_queries.1.own_ref
  3.9 0.0 copy-start.3
  3.9 0.0 copy-start.2
  3.9 0.0 copy-start.4
  3.9 0.0 copy-start.5
  3.9 0.0 copy-start.6
  4.0 0.0 copy-start.7
  4.0 0.0 copy-start.8
  4.0 0.0 copy-start.9
  4.0 0.0 collective-permute-done.3.w_ref
  4.0 0.4 join_queries.1.q_ref
  4.4 8.9 %collective-permute-start.6 = (bf16[512,512]{1,0:T(8,128)(2,1)S(1)}, bf16[512,512]{1,0:T(8,128)(2,1)S(1)}, u32[]{:S(2)}, u32[]{:S(2)}) collective-permute-start(bf16[512,512]{1,0:T(8,128)(2,1)S(1)} %join_queries.1.q_ref), channel_id=1, source_target_pairs={{0,1},{1,0},{2,3},{3,2},{4,5},{5,4},{6,7},{7,6},{8,9},{9,8},{10,11... | collective-permute-start | bytes 1572872 | tf_op jit(solution)/shard_map/ppermute | solution.py:316
  13.4 0.0 copy-done.3
  13.4 0.1 collective-permute-start.2
  13.5 0.0 copy-done.2
  13.5 0.5 collective-permute-start.8
  14.0 0.0 collective-permute-done.wk2
  14.0 1.9 %collective-permute-start.4 = (bf16[512,512]{1,0:T(8,128)(2,1)S(1)}, bf16[512,512]{1,0:T(8,128)(2,1)S(1)}, u32[]{:S(2)}, u32[]{:S(2)}) collective-permute-start(bf16[512,512]{1,0:T(8,128)(2,1)S(1)} %join_queries.1.q_ref), channel_id=1, source_target_pairs={{2,4},{4,2},{3,5},{5,3},{6,8},{8,6},{7,9},{9,7},{10,12},{12,10},{1... | collective-permute-start | bytes 1572872 | tf_op jit(solution)/shard_map/ppermute | solution.py:316
  15.9 0.0 collective-permute-done.1.wv2
  15.9 0.0 copy-done.4
  15.9 0.0 copy-done.5
  16.0 0.0 copy-done.6
  16.0 0.0 copy-done.7
  16.0 0.0 copy-done.8
  16.0 0.0 copy-done.9
  16.0 5.2 %project_kv.1 = (bf16[2048,512]{1,0:T(8,128)(2,1)S(1)}, bf16[2048,512]{1,0:T(8,128)(2,1)S(1)}, s32[8,128]{1,0:T(8,128)S(1)}, s32[32,128]{1,0:T(8,128)S(1)}, s32[16,128]{1,0:T(8,128)S(1)}) custom-call(bf16[2048,1024]{1,0:T(8,128)(2,1)S(1)} %copy-done.4, bf16[1024,256]{1,0:T(8,128)(2,1)S(1)} %copy-done.6, bf16[1024,256]{1,0:T(8,128)(2,1)S(1)} %collective-permute-done.wk2, ...), custom_call_target="tpu_custom_call" | custom-call | flops 4294967296 | bytes 8388608 | tf_op jit(solution)/shard_map/project_kv/pallas_call | solution.py:145
  21.3 0.0 collective-permute-done.2.other_bias
  21.3 1.2 %collective-permute-done.6.q_ref = bf16[512,512]{1,0:T(8,128)(2,1)S(1)} collective-permute-done((bf16[512,512]{1,0:T(8,128)(2,1)S(1)}, bf16[512,512]{1,0:T(8,128)(2,1)S(1)}, u32[]{:S(2)}, u32[]{:S(2)}) %collective-permute-start.6) | collective-permute-done | bytes 524320 | tf_op jit(solution)/shard_map/ppermute | solution.py:316
  22.4 3.5 %shard_map.102 = bf16[512,512]{1,0:T(8,128)(2,1)S(1)} custom-call(s32[8,128]{1,0:T(8,128)S(1)} %get-tuple-element.12.runs_ref, f32[2]{0:T(128)S(1)} %copy-done.3, f32[2]{0:T(128)S(1)} %collective-permute-done.2.other_bias, s32[32,128]{1,0:T(8,128)S(1)} %get-tuple-element.13.gene_ref, s32[16,128]{1,0:T(8,128)S(1)} %get-tuple-element.14.peak_ref, ...), custom_call_target="tpu_custom_call" | custom-call | flops 2147483648 | bytes 5242880 | tf_op jit(solution)/shard_map/pallas_call | solution.py:231
  25.9 13.7 %collective-permute-start.7 = (bf16[512,512]{1,0:T(8,128)(2,1)S(1)}, bf16[512,512]{1,0:T(8,128)(2,1)S(1)}, u32[]{:S(2)}, u32[]{:S(2)}) collective-permute-start(bf16[512,512]{1,0:T(8,128)(2,1)S(1)} %shard_map.102), channel_id=1, source_target_pairs={{0,1},{1,0},{2,3},{3,2},{4,5},{5,4},{6,7},{7,6},{8,9},{9,8},{10,11... | collective-permute-start | bytes 1572872 | tf_op jit(solution)/shard_map/ppermute | solution.py:316
  39.6 0.0 collective-permute-done.4.q_ref
  39.6 6.1 %shard_map.101 = bf16[512,512]{1,0:T(8,128)(2,1)S(1)} custom-call(s32[8,128]{1,0:T(8,128)S(1)} %get-tuple-element.12.runs_ref, f32[2]{0:T(128)S(1)} %copy-done.3, f32[2]{0:T(128)S(1)} %collective-permute-done.2.other_bias, s32[32,128]{1,0:T(8,128)S(1)} %get-tuple-element.13.gene_ref, s32[16,128]{1,0:T(8,128)S(1)} %get-tuple-element.14.peak_ref, ...), custom_call_target="tpu_custom_call" | custom-call | flops 2147483648 | bytes 5242880 | tf_op jit(solution)/shard_map/pallas_call | solution.py:231
  45.7 1.9 %collective-permute-start.5 = (bf16[512,512]{1,0:T(8,128)(2,1)S(1)}, bf16[512,512]{1,0:T(8,128)(2,1)S(1)}, u32[]{:S(2)}, u32[]{:S(2)}) collective-permute-start(bf16[512,512]{1,0:T(8,128)(2,1)S(1)} %shard_map.101), channel_id=1, source_target_pairs={{2,4},{4,2},{3,5},{5,3},{6,8},{8,6},{7,9},{9,7},{10,12},{12,10},{1... | collective-permute-start | bytes 1572872 | tf_op jit(solution)/shard_map/ppermute | solution.py:316
  47.7 3.9 %shard_map.100.own_ref = f32[512,256]{1,0:T(8,128)S(1)} custom-call(s32[8,128]{1,0:T(8,128)S(1)} %get-tuple-element.12.runs_ref, f32[2]{0:T(128)S(1)} %copy-done.3, f32[2]{0:T(128)S(1)} %collective-permute-done.2.other_bias, s32[32,128]{1,0:T(8,128)S(1)} %get-tuple-element.13.gene_ref, s32[16,128]{1,0:T(8,128)S(1)} %get-tuple-element.14.peak_ref, ...), custom_call_target="tpu_custom_call" | custom-call | flops 1073741824 | bytes 5242880 | tf_op jit(solution)/shard_map/pallas_call | solution.py:231
  51.5 0.0 collective-permute-done.8.w2
  51.5 0.0 collective-permute-done.7.second_ref
  51.5 7.9 %collective-permute-done.5.first_ref = bf16[512,512]{1,0:T(8,128)(2,1)S(1)} collective-permute-done((bf16[512,512]{1,0:T(8,128)(2,1)S(1)}, bf16[512,512]{1,0:T(8,128)(2,1)S(1)}, u32[]{:S(2)}, u32[]{:S(2)}) %collective-permute-start.5) | collective-permute-done | bytes 524320 | tf_op jit(solution)/shard_map/ppermute | solution.py:316
  59.4 0.7 shard_map.103
  60.1 0.1 collective-permute-start.9
  60.2 1.9 %collective-permute-done.9 = bf16[512,512]{1,0:T(8,128)(2,1)S(1)} collective-permute-done((bf16[512,512]{1,0:T(8,128)(2,1)S(1)}, bf16[512,512]{1,0:T(8,128)(2,1)S(1)}, u32[]{:S(2)}, u32[]{:S(2)}) %collective-permute-start.9) | collective-permute-done | bytes 524320 | tf_op jit(solution)/shard_map/ppermute | solution.py:46
  62.1 0.2 convert_add_fusion.refs_0_
  62.4 5.3 %collective-permute-start.10 = (bf16[512,256]{1,0:T(8,128)(2,1)S(1)}, bf16[512,256]{1,0:T(8,128)(2,1)S(1)}, u32[]{:S(2)}, u32[]{:S(2)}) collective-permute-start(bf16[512,256]{1,0:T(8,128)(2,1)S(1)} %slice.7), channel_id=1, source_target_pairs={{0,128},{128,0},{64,192},{192,64},{1,129},{129,1},{65,193},{193,65... | collective-permute-start | bytes 786440 | tf_op jit(solution)/shard_map/ppermute | solution.py:339
  67.7 11.8 %collective-permute-done.10.refs_1_ = bf16[512,256]{1,0:T(8,128)(2,1)S(1)} collective-permute-done((bf16[512,256]{1,0:T(8,128)(2,1)S(1)}, bf16[512,256]{1,0:T(8,128)(2,1)S(1)}, u32[]{:S(2)}, u32[]{:S(2)}) %collective-permute-start.10) | collective-permute-done | bytes 262176 | tf_op jit(solution)/shard_map/ppermute | solution.py:339
  79.5 0.7 finish.1
  (1 shorter events, 0.0 us)
Async XLA Ops:
  0.0 4.0 %collective-permute-start.3 = (bf16[1024,256]{1,0:T(8,128)(2,1)}, bf16[1024,256]{1,0:T(8,128)(2,1)S(1)}, u32[]{:S(2)}, u32[]{:S(2)}) collective-permute-start(bf16[1024,256]{1,0:T(8,128)(2,1)} %w_ref.1), channel_id=1, source_target_pairs={{0,64},{64,0},{128,192},{192,128},{1,65},{65,1},{129,193},{193,129... | collective-permute-start | bytes 1572872 | tf_op jit(solution)/shard_map/ppermute | solution.py:46
  0.7 13.3 %collective-permute-start = (bf16[1024,256]{1,0:T(8,128)(2,1)}, bf16[1024,256]{1,0:T(8,128)(2,1)S(1)}, u32[]{:S(2)}, u32[]{:S(2)}) collective-permute-start(bf16[1024,256]{1,0:T(8,128)(2,1)} %wk1.1), channel_id=1, source_target_pairs={{0,64},{64,0},{128,192},{192,128},{1,65},{65,1},{129,193},{193,129... | collective-permute-start | bytes 1572872 | tf_op jit(solution)/shard_map/ppermute | solution.py:46
  0.7 15.2 %collective-permute-start.1 = (bf16[1024,256]{1,0:T(8,128)(2,1)}, bf16[1024,256]{1,0:T(8,128)(2,1)S(1)}, u32[]{:S(2)}, u32[]{:S(2)}) collective-permute-start(bf16[1024,256]{1,0:T(8,128)(2,1)} %wv1.1), channel_id=1, source_target_pairs={{0,64},{64,0},{128,192},{192,128},{1,65},{65,1},{129,193},{193,129... | collective-permute-start | bytes 1572872 | tf_op jit(solution)/shard_map/ppermute | solution.py:46
  1.2 1.2 %copy-start = (bf16[512,1024]{1,0:T(8,128)(2,1)S(1)}, bf16[512,1024]{1,0:T(8,128)(2,1)}, u32[]{:S(2)}) copy-start(bf16[512,1024]{1,0:T(8,128)(2,1)} %act_ref.5) | copy-start | bytes 3145732
  2.4 1.0 %copy-start.1 = (bf16[1024,256]{1,0:T(8,128)(2,1)S(1)}, bf16[1024,256]{1,0:T(8,128)(2,1)}, u32[]{:S(2)}) copy-start(bf16[1024,256]{1,0:T(8,128)(2,1)} %w_ref.1) | copy-start | bytes 1572868
  3.9 9.5 %copy-start.3 = (f32[2]{0:T(128)S(1)}, f32[2]{0:T(128)}, u32[]{:S(2)}) copy-start(f32[2]{0:T(128)} %own_bias.5) | copy-start | bytes 28
  3.9 9.6 %copy-start.2 = (bf16[256,1024]{1,0:T(8,128)(2,1)S(1)}, bf16[256,1024]{1,0:T(8,128)(2,1)}, u32[]{:S(2)}) copy-start(bf16[256,1024]{1,0:T(8,128)(2,1)} %w1.1) | copy-start | bytes 1572868
  3.9 12.0 %copy-start.4 = (bf16[2048,1024]{1,0:T(8,128)(2,1)S(1)}, bf16[2048,1024]{1,0:T(8,128)(2,1)}, u32[]{:S(2)}) copy-start(bf16[2048,1024]{1,0:T(8,128)(2,1)} %act_ref.3) | copy-start | bytes 12582916
  3.9 12.0 %copy-start.5 = (s32[256,1024]{1,0:T(8,128)S(1)}, s32[256,1024]{1,0:T(8,128)}, u32[]{:S(2)}) copy-start(s32[256,1024]{1,0:T(8,128)} %mask_hbm.1) | copy-start | bytes 3145732
  3.9 12.0 %copy-start.6 = (bf16[1024,256]{1,0:T(8,128)(2,1)S(1)}, bf16[1024,256]{1,0:T(8,128)(2,1)}, u32[]{:S(2)}) copy-start(bf16[1024,256]{1,0:T(8,128)(2,1)} %wk1.1) | copy-start | bytes 1572868
  4.0 12.0 %copy-start.7 = (bf16[1024,256]{1,0:T(8,128)(2,1)S(1)}, bf16[1024,256]{1,0:T(8,128)(2,1)}, u32[]{:S(2)}) copy-start(bf16[1024,256]{1,0:T(8,128)(2,1)} %wv1.1) | copy-start | bytes 1572868
  4.0 12.0 %copy-start.8 = (s32[131072]{0:T(1024)S(1)}, s32[131072]{0:T(1024)}, u32[]{:S(2)}) copy-start(s32[131072]{0:T(1024)} %param.19) | copy-start | bytes 1572868
  4.0 12.0 %copy-start.9 = (s32[32768]{0:T(1024)S(1)}, s32[32768]{0:T(1024)}, u32[]{:S(2)}) copy-start(s32[32768]{0:T(1024)} %param.18) | copy-start | bytes 393220
  4.4 18.0 %collective-permute-start.6 = (bf16[512,512]{1,0:T(8,128)(2,1)S(1)}, bf16[512,512]{1,0:T(8,128)(2,1)S(1)}, u32[]{:S(2)}, u32[]{:S(2)}) collective-permute-start(bf16[512,512]{1,0:T(8,128)(2,1)S(1)} %join_queries.1.q_ref), channel_id=1, source_target_pairs={{0,1},{1,0},{2,3},{3,2},{4,5},{5,4},{6,7},{7,6},{8,9},{9,8},{10,11... | collective-permute-start | bytes 1572872 | tf_op jit(solution)/shard_map/ppermute | solution.py:316
  13.4 7.8 %collective-permute-start.2 = (f32[2]{0:T(128)S(1)}, f32[2]{0:T(128)S(1)}, u32[]{:S(2)}, u32[]{:S(2)}) collective-permute-start(f32[2]{0:T(128)S(1)} %copy-done.3), channel_id=1, source_target_pairs={{0,64},{64,0},{128,192},{192,128},{1,65},{65,1},{129,193},{193,129... | collective-permute-start | bytes 32 | tf_op jit(solution)/shard_map/ppermute | solution.py:46
  13.5 38.0 %collective-permute-start.8 = (bf16[256,1024]{1,0:T(8,128)(2,1)S(1)}, bf16[256,1024]{1,0:T(8,128)(2,1)S(1)}, u32[]{:S(2)}, u32[]{:S(2)}) collective-permute-start(bf16[256,1024]{1,0:T(8,128)(2,1)S(1)} %copy-done.2), channel_id=1, source_target_pairs={{0,64},{64,0},{128,192},{192,128},{1,65},{65,1},{129,193},{193,129... | collective-permute-start | bytes 1572872 | tf_op jit(solution)/shard_map/ppermute | solution.py:46
  14.0 25.6 %collective-permute-start.4 = (bf16[512,512]{1,0:T(8,128)(2,1)S(1)}, bf16[512,512]{1,0:T(8,128)(2,1)S(1)}, u32[]{:S(2)}, u32[]{:S(2)}) collective-permute-start(bf16[512,512]{1,0:T(8,128)(2,1)S(1)} %join_queries.1.q_ref), channel_id=1, source_target_pairs={{2,4},{4,2},{3,5},{5,3},{6,8},{8,6},{7,9},{9,7},{10,12},{12,10},{1... | collective-permute-start | bytes 1572872 | tf_op jit(solution)/shard_map/ppermute | solution.py:316
  25.9 25.6 %collective-permute-start.7 = (bf16[512,512]{1,0:T(8,128)(2,1)S(1)}, bf16[512,512]{1,0:T(8,128)(2,1)S(1)}, u32[]{:S(2)}, u32[]{:S(2)}) collective-permute-start(bf16[512,512]{1,0:T(8,128)(2,1)S(1)} %shard_map.102), channel_id=1, source_target_pairs={{0,1},{1,0},{2,3},{3,2},{4,5},{5,4},{6,7},{7,6},{8,9},{9,8},{10,11... | collective-permute-start | bytes 1572872 | tf_op jit(solution)/shard_map/ppermute | solution.py:316
  45.7 13.7 %collective-permute-start.5 = (bf16[512,512]{1,0:T(8,128)(2,1)S(1)}, bf16[512,512]{1,0:T(8,128)(2,1)S(1)}, u32[]{:S(2)}, u32[]{:S(2)}) collective-permute-start(bf16[512,512]{1,0:T(8,128)(2,1)S(1)} %shard_map.101), channel_id=1, source_target_pairs={{2,4},{4,2},{3,5},{5,3},{6,8},{8,6},{7,9},{9,7},{10,12},{12,10},{1... | collective-permute-start | bytes 1572872 | tf_op jit(solution)/shard_map/ppermute | solution.py:316
  60.1 2.0 %collective-permute-start.9 = (bf16[512,512]{1,0:T(8,128)(2,1)S(1)}, bf16[512,512]{1,0:T(8,128)(2,1)S(1)}, u32[]{:S(2)}, u32[]{:S(2)}) collective-permute-start(bf16[512,512]{1,0:T(8,128)(2,1)S(1)} %get-tuple-element.18), channel_id=1, source_target_pairs={{0,64},{64,0},{128,192},{192,128},{1,65},{65,1},{129,193},{193,129... | collective-permute-start | bytes 1572872 | tf_op jit(solution)/shard_map/ppermute | solution.py:46
  62.4 17.2 %collective-permute-start.10 = (bf16[512,256]{1,0:T(8,128)(2,1)S(1)}, bf16[512,256]{1,0:T(8,128)(2,1)S(1)}, u32[]{:S(2)}, u32[]{:S(2)}) collective-permute-start(bf16[512,256]{1,0:T(8,128)(2,1)S(1)} %slice.7), channel_id=1, source_target_pairs={{0,128},{128,0},{64,192},{192,64},{1,129},{129,1},{65,193},{193,65... | collective-permute-start | bytes 786440 | tf_op jit(solution)/shard_map/ppermute | solution.py:339

commit v5 on v4

--- a/solution.py
+++ b/solution.py
@@ -239,15 +239,13 @@
     )(runs, own_bias, other_bias, gene, peak, q, k, v)
 
 
-def mix_kernel(part, own_ref, first_ref, second_ref, w1, w2, send_ref, keep_ref):
-    rows = slice(part * send_ref.shape[0], (part + 1) * send_ref.shape[0])
+def mix_kernel(across, own_ref, first_ref, second_ref, w1, w2, send_ref, keep_ref):
     width = w1.shape[1] // 4
     depth = w1.shape[0]
     me = lax.axis_index("gene")
-    first, second = first_ref[rows, :].astype(F32), second_ref[...].astype(F32)
-    mine = own_ref[rows, :] + first[:, :depth] + second[:, :depth]
-    theirs = first[:, depth:] + second[:, depth:]
-    mine, theirs = mine.astype(BF16), theirs.astype(BF16)
+    first, second = first_ref[...].astype(F32), second_ref[...].astype(F32)
+    mine = (own_ref[...] + first[:, :depth] + second[:, :depth]).astype(BF16)
+    theirs = (first[:, depth:] + second[:, depth:]).astype(BF16)
 
     def share(block):
         cols = pl.ds(pl.multiple_of(block * width, width), width)
@@ -255,45 +253,38 @@
             theirs, w2[:, cols], preferred_element_type=F32
         )
 
-    send_ref[:, :width] = share(me ^ 3).astype(BF16)
-    send_ref[:, width:] = share(me ^ 1).astype(BF16)
-    keep_ref[:, :width] = share(me ^ 2)
-    keep_ref[:, width:] = share(me)
-
-
-def mix(part, own, first, second, w1, w2):
-    shape = (second.shape[0], w1.shape[1] // 2)
-    return pl.pallas_call(
-        functools.partial(mix_kernel, part),
+    send_ref[...] = share(me ^ (1 + across)).astype(BF16)
+    keep_ref[...] = share(me ^ across)
+
+
+def mix(across, own, first, second, w1, w2):
+    shape = (own.shape[0], w1.shape[1] // 4)
+    return pl.pallas_call(
+        functools.partial(mix_kernel, across),
         in_specs=[VMEM] * 5,
         out_specs=[VMEM, VMEM],
         out_shape=[jax.ShapeDtypeStruct(shape, BF16), jax.ShapeDtypeStruct(shape, F32)],
-        cost_estimate=cost(4 * shape[0] * w1.size, [own, w1, w2, own, own]),
-        compiler_params=PARAMS,
+        cost_estimate=cost(2 * own.shape[0] * w1.size, [own, w1, w2, own, own]),
+        compiler_params=PARAMS,
+        name="mix_across" if across else "mix_here",
     )(own, first, second, w1, w2)
 
 
-def finish_kernel(*refs):
-    out_ref = refs[-1]
-    parts = (len(refs) - 1) // 2
-    rows, width = refs[parts].shape
-    for part in range(parts):
-        total = refs[part][:, width:] + refs[parts + part][...].astype(F32)
-        out_ref[part * rows : (part + 1) * rows, :] = total.astype(BF16)
-
-
-def finish(halves, others):
-    rows, width = others[0].shape
-    shape = (len(others) * rows, width)
+def finish_kernel(keep_ref, core_ref, z_ref, out_ref):
+    total = keep_ref[...] + core_ref[...].astype(F32) + z_ref[...].astype(F32)
+    out_ref[...] = total.astype(BF16)
+
+
+def finish(keep, core, z):
     return pl.pallas_call(
         finish_kernel,
-        in_specs=[VMEM] * (2 * len(others)),
+        in_specs=[VMEM] * 3,
         out_specs=VMEM,
-        out_shape=jax.ShapeDtypeStruct(shape, BF16),
-        cost_estimate=cost(2 * rows * width, halves + others),
+        out_shape=jax.ShapeDtypeStruct(keep.shape, BF16),
+        cost_estimate=cost(2 * keep.size, [keep, core, z]),
         compiler_params=PARAMS,
         name="finish",
-    )(*halves, *others)
+    )(keep, core, z)
 
 
 def on_device(
@@ -330,15 +321,13 @@
     seconds = [travel(rows, 1) for rows in seconds]
     (own,) = attend(None, local, tables, queries, keys, values, F32)
     w_other = core_swap(w_out)
-    halves, others = [], []
-    for part in range(PARTS):
-        send, keep = mix(part, own, first, seconds[part], w_out, w_other)
-        width = send.shape[1] // 2
-        half = keep + core_swap(send).astype(F32)
-        pairs = [(0, 2), (2, 0), (1, 3), (3, 1)]
-        others.append(lax.ppermute(half[:, :width].astype(BF16), "gene", pairs))
-        halves.append(half)
-    return finish(halves, others)
+    total = (own, first, seconds[0], w_out, w_other)
+    send, keep = mix(2, *total)
+    half = keep + core_swap(send).astype(F32)
+    pairs = [(0, 2), (2, 0), (1, 3), (3, 1)]
+    other = lax.ppermute(half.astype(BF16), "gene", pairs)
+    send, keep = mix(0, *total)
+    return finish(keep, core_swap(send), other)
 
 
 def solution(mesh):

time: 80.5 us -> 79.7 us (0.990)
  waiting for transfers between devices: 22.8 us -> 21.3 us
    ppermute x6 -> x7, waiting for transfers between devices: 1.91 us -> 0.5 us  [core_swap(): return lax.ppermute(x, 'gene', [(0, 1), (1, 0), (2, 3), (3, 2)])]
    ppermute x6 -> x7, starting transfers between devices: 1.86 us -> 2.43 us  [core_swap(): return lax.ppermute(x, 'gene', [(0, 1), (1, 0), (2, 3), (3, 2)])]
    pallas_call x2 -> x3, Pallas kernels: 1.49 us -> 1.69 us  [the longest x2 0.91 us: mix(): pl.pallas_call(functools.partial(mix_kernel, across), in_specs=[VMEM] * 5...]
  transfers between devices with their start and end apart: 11 -> 12, of which waited for: 4 -> 4; matrix products, arithmetic and copies ran while one was open for 0% -> 0% of each run, Pallas kernels for 24% -> 25%
where the time goes in v5:
time: 79.7 us; the launch traced here: 79.5 us
  starting transfers between devices  34.2 us (43%)
  Pallas kernels  21.3 us (27%)
  waiting for transfers between devices  21.3 us (27%)
  local copies, waits for them, and re-layouts  2.32 us (3%)
    ppermute x4, starting transfers between devices, travel(): return lax.ppermute(x, ('gene', 'peak'), swap_pairs(genes, count, turn))  26.4 us
    pallas_call x3, Pallas kernels, attend(): pl.pallas_call(functools.partial(attend_kernel, turn, heads), in_specs=[S...  13.5 us
    ppermute x1, waiting for transfers between devices, on_device(): other = lax.ppermute(half.astype(BF16), 'gene', pairs)  11.8 us
    ppermute x4, waiting for transfers between devices, travel(): return lax.ppermute(x, ('gene', 'peak'), swap_pairs(genes, count, turn))  9.02 us
    ppermute x1, starting transfers between devices, on_device(): other = lax.ppermute(half.astype(BF16), 'gene', pairs)  5.35 us
    pallas_call x1, Pallas kernels, project_kv(): pl.pallas_call(functools.partial(kv_kernel, gene_tiles), in_specs=[VMEM]...  5.25 us
    ppermute x7, starting transfers between devices, core_swap(): return lax.ppermute(x, 'gene', [(0, 1), (1, 0), (2, 3), (3, 2)])  2.43 us
    unnamed x20, local copies, waits for them, and re-layouts  2.32 us
  transfers between devices with their start and end apart: 12, of which 4 were waited for; matrix products, arithmetic and copies ran while one was open for 0% of the time, Pallas kernels for 25%

profile of v5, /device:TPU:3, one launch (start us, length us, event | category | flops | bytes accessed | tf_op | source)
XLA Modules:
  0.0 79.5 jit_solution(10459191089825773418)
XLA Ops:
  0.0 0.7 collective-permute-start.3
  0.7 0.0 collective-permute-start
  0.7 0.5 collective-permute-start.1
  1.2 0.0 copy-start.1
  1.2 1.2 %copy-done.1 = bf16[512,1024]{1,0:T(8,128)(2,1)S(1)} copy-done((bf16[512,1024]{1,0:T(8,128)(2,1)S(1)}, bf16[512,1024]{1,0:T(8,128)(2,1)}, u32[]{:S(2)}) %copy-start.1) | copy-done | bytes 1048600
  2.4 0.0 copy-start.2
  2.4 1.0 %copy-done.2 = bf16[1024,256]{1,0:T(8,128)(2,1)S(1)} copy-done((bf16[1024,256]{1,0:T(8,128)(2,1)S(1)}, bf16[1024,256]{1,0:T(8,128)(2,1)}, u32[]{:S(2)}) %copy-start.2) | copy-done | bytes 524312
  3.5 0.4 project_queries.1.own_ref
  3.9 0.0 copy-start.3
  3.9 0.0 copy-start
  3.9 0.0 copy-start.4
  3.9 0.0 copy-start.5
  3.9 0.0 copy-start.6
  4.0 0.0 copy-start.7
  4.0 0.0 copy-start.8
  4.0 0.0 copy-start.9
  4.0 0.0 collective-permute-done.3.w_ref
  4.0 0.4 join_queries.1.q_ref
  4.4 8.9 %collective-permute-start.6 = (bf16[512,512]{1,0:T(8,128)(2,1)S(1)}, bf16[512,512]{1,0:T(8,128)(2,1)S(1)}, u32[]{:S(2)}, u32[]{:S(2)}) collective-permute-start(bf16[512,512]{1,0:T(8,128)(2,1)S(1)} %join_queries.1.q_ref), channel_id=1, source_target_pairs={{0,1},{1,0},{2,3},{3,2},{4,5},{5,4},{6,7},{7,6},{8,9},{9,8},{10,11... | collective-permute-start | bytes 1572872 | tf_op jit(solution)/shard_map/ppermute | solution.py:307
  13.4 0.0 copy-done.3
  13.4 0.1 collective-permute-start.2
  13.5 0.0 copy-done
  13.5 0.5 collective-permute-start.8
  14.0 0.0 collective-permute-done.wk2
  14.0 1.9 %collective-permute-start.4 = (bf16[512,512]{1,0:T(8,128)(2,1)S(1)}, bf16[512,512]{1,0:T(8,128)(2,1)S(1)}, u32[]{:S(2)}, u32[]{:S(2)}) collective-permute-start(bf16[512,512]{1,0:T(8,128)(2,1)S(1)} %join_queries.1.q_ref), channel_id=1, source_target_pairs={{2,4},{4,2},{3,5},{5,3},{6,8},{8,6},{7,9},{9,7},{10,12},{12,10},{1... | collective-permute-start | bytes 1572872 | tf_op jit(solution)/shard_map/ppermute | solution.py:307
  15.9 0.0 collective-permute-done.1.wv2
  15.9 0.0 copy-done.4
  15.9 0.0 copy-done.5
  16.0 0.0 copy-done.6
  16.0 0.0 copy-done.7
  16.0 0.0 copy-done.8
  16.0 0.0 copy-done.9
  16.0 5.2 %project_kv.1 = (bf16[2048,512]{1,0:T(8,128)(2,1)S(1)}, bf16[2048,512]{1,0:T(8,128)(2,1)S(1)}, s32[8,128]{1,0:T(8,128)S(1)}, s32[32,128]{1,0:T(8,128)S(1)}, s32[16,128]{1,0:T(8,128)S(1)}) custom-call(bf16[2048,1024]{1,0:T(8,128)(2,1)S(1)} %copy-done.4, bf16[1024,256]{1,0:T(8,128)(2,1)S(1)} %copy-done.6, bf16[1024,256]{1,0:T(8,128)(2,1)S(1)} %collective-permute-done.wk2, ...), custom_call_target="tpu_custom_call" | custom-call | flops 4294967296 | bytes 8388608 | tf_op jit(solution)/shard_map/project_kv/pallas_call | solution.py:145
  21.3 0.0 collective-permute-done.2.other_bias
  21.3 1.2 %collective-permute-done.6.q_ref = bf16[512,512]{1,0:T(8,128)(2,1)S(1)} collective-permute-done((bf16[512,512]{1,0:T(8,128)(2,1)S(1)}, bf16[512,512]{1,0:T(8,128)(2,1)S(1)}, u32[]{:S(2)}, u32[]{:S(2)}) %collective-permute-start.6) | collective-permute-done | bytes 524320 | tf_op jit(solution)/shard_map/ppermute | solution.py:307
  22.4 3.5 %shard_map.102 = bf16[512,512]{1,0:T(8,128)(2,1)S(1)} custom-call(s32[8,128]{1,0:T(8,128)S(1)} %get-tuple-element.14.runs_ref, f32[2]{0:T(128)S(1)} %copy-done.3, f32[2]{0:T(128)S(1)} %collective-permute-done.2.other_bias, s32[32,128]{1,0:T(8,128)S(1)} %get-tuple-element.15.gene_ref, s32[16,128]{1,0:T(8,128)S(1)} %get-tuple-element.16.peak_ref, ...), custom_call_target="tpu_custom_call" | custom-call | flops 2147483648 | bytes 5242880 | tf_op jit(solution)/shard_map/pallas_call | solution.py:231
  25.9 13.7 %collective-permute-start.7 = (bf16[512,512]{1,0:T(8,128)(2,1)S(1)}, bf16[512,512]{1,0:T(8,128)(2,1)S(1)}, u32[]{:S(2)}, u32[]{:S(2)}) collective-permute-start(bf16[512,512]{1,0:T(8,128)(2,1)S(1)} %shard_map.102), channel_id=1, source_target_pairs={{0,1},{1,0},{2,3},{3,2},{4,5},{5,4},{6,7},{7,6},{8,9},{9,8},{10,11... | collective-permute-start | bytes 1572872 | tf_op jit(solution)/shard_map/ppermute | solution.py:307
  39.6 0.0 collective-permute-done.4.q_ref
  39.6 6.1 %shard_map.101 = bf16[512,512]{1,0:T(8,128)(2,1)S(1)} custom-call(s32[8,128]{1,0:T(8,128)S(1)} %get-tuple-element.14.runs_ref, f32[2]{0:T(128)S(1)} %copy-done.3, f32[2]{0:T(128)S(1)} %collective-permute-done.2.other_bias, s32[32,128]{1,0:T(8,128)S(1)} %get-tuple-element.15.gene_ref, s32[16,128]{1,0:T(8,128)S(1)} %get-tuple-element.16.peak_ref, ...), custom_call_target="tpu_custom_call" | custom-call | flops 2147483648 | bytes 5242880 | tf_op jit(solution)/shard_map/pallas_call | solution.py:231
  45.7 1.9 %collective-permute-start.5 = (bf16[512,512]{1,0:T(8,128)(2,1)S(1)}, bf16[512,512]{1,0:T(8,128)(2,1)S(1)}, u32[]{:S(2)}, u32[]{:S(2)}) collective-permute-start(bf16[512,512]{1,0:T(8,128)(2,1)S(1)} %shard_map.101), channel_id=1, source_target_pairs={{2,4},{4,2},{3,5},{5,3},{6,8},{8,6},{7,9},{9,7},{10,12},{12,10},{1... | collective-permute-start | bytes 1572872 | tf_op jit(solution)/shard_map/ppermute | solution.py:307
  47.7 3.9 %shard_map.100.own_ref = f32[512,256]{1,0:T(8,128)S(1)} custom-call(s32[8,128]{1,0:T(8,128)S(1)} %get-tuple-element.14.runs_ref, f32[2]{0:T(128)S(1)} %copy-done.3, f32[2]{0:T(128)S(1)} %collective-permute-done.2.other_bias, s32[32,128]{1,0:T(8,128)S(1)} %get-tuple-element.15.gene_ref, s32[16,128]{1,0:T(8,128)S(1)} %get-tuple-element.16.peak_ref, ...), custom_call_target="tpu_custom_call" | custom-call | flops 1073741824 | bytes 5242880 | tf_op jit(solution)/shard_map/pallas_call | solution.py:231
  51.5 0.0 collective-permute-done.8.w2
  51.5 0.0 collective-permute-done.7.second_ref
  51.5 7.9 %collective-permute-done.5.first_ref = bf16[512,512]{1,0:T(8,128)(2,1)S(1)} collective-permute-done((bf16[512,512]{1,0:T(8,128)(2,1)S(1)}, bf16[512,512]{1,0:T(8,128)(2,1)S(1)}, u32[]{:S(2)}, u32[]{:S(2)}) %collective-permute-start.5) | collective-permute-done | bytes 524320 | tf_op jit(solution)/shard_map/ppermute | solution.py:307
  59.4 0.4 mix_across.1
  59.9 0.1 collective-permute-start.10
  60.0 0.5 mix_here.1
  60.4 0.6 collective-permute-start.9
  61.0 0.5 collective-permute-done.10
  61.5 0.1 add_convert_fusion
  61.5 5.3 %collective-permute-start.11 = (bf16[512,256]{1,0:T(8,128)(2,1)S(1)}, bf16[512,256]{1,0:T(8,128)(2,1)S(1)}, u32[]{:S(2)}, u32[]{:S(2)}) collective-permute-start(bf16[512,256]{1,0:T(8,128)(2,1)S(1)} %add_convert_fusion), channel_id=1, source_target_pairs={{0,128},{128,0},{64,192},{192,64},{1,129},{129,1},{65,193},{193,65... | collective-permute-start | bytes 786440 | tf_op jit(solution)/shard_map/ppermute | solution.py:328
  66.9 0.0 collective-permute-done.9.core_ref
  66.9 11.8 %collective-permute-done.11.z_ref = bf16[512,256]{1,0:T(8,128)(2,1)S(1)} collective-permute-done((bf16[512,256]{1,0:T(8,128)(2,1)S(1)}, bf16[512,256]{1,0:T(8,128)(2,1)S(1)}, u32[]{:S(2)}, u32[]{:S(2)}) %collective-permute-start.11) | collective-permute-done | bytes 262176 | tf_op jit(solution)/shard_map/ppermute | solution.py:328
  78.7 0.8 finish.1
Async XLA Ops:
  0.0 4.0 %collective-permute-start.3 = (bf16[1024,256]{1,0:T(8,128)(2,1)}, bf16[1024,256]{1,0:T(8,128)(2,1)S(1)}, u32[]{:S(2)}, u32[]{:S(2)}) collective-permute-start(bf16[1024,256]{1,0:T(8,128)(2,1)} %w_ref.1), channel_id=1, source_target_pairs={{0,64},{64,0},{128,192},{192,128},{1,65},{65,1},{129,193},{193,129... | collective-permute-start | bytes 1572872 | tf_op jit(solution)/shard_map/ppermute | solution.py:46
  0.7 13.3 %collective-permute-start = (bf16[1024,256]{1,0:T(8,128)(2,1)}, bf16[1024,256]{1,0:T(8,128)(2,1)S(1)}, u32[]{:S(2)}, u32[]{:S(2)}) collective-permute-start(bf16[1024,256]{1,0:T(8,128)(2,1)} %wk1.1), channel_id=1, source_target_pairs={{0,64},{64,0},{128,192},{192,128},{1,65},{65,1},{129,193},{193,129... | collective-permute-start | bytes 1572872 | tf_op jit(solution)/shard_map/ppermute | solution.py:46
  0.7 15.2 %collective-permute-start.1 = (bf16[1024,256]{1,0:T(8,128)(2,1)}, bf16[1024,256]{1,0:T(8,128)(2,1)S(1)}, u32[]{:S(2)}, u32[]{:S(2)}) collective-permute-start(bf16[1024,256]{1,0:T(8,128)(2,1)} %wv1.1), channel_id=1, source_target_pairs={{0,64},{64,0},{128,192},{192,128},{1,65},{65,1},{129,193},{193,129... | collective-permute-start | bytes 1572872 | tf_op jit(solution)/shard_map/ppermute | solution.py:46
  1.2 1.2 %copy-start.1 = (bf16[512,1024]{1,0:T(8,128)(2,1)S(1)}, bf16[512,1024]{1,0:T(8,128)(2,1)}, u32[]{:S(2)}) copy-start(bf16[512,1024]{1,0:T(8,128)(2,1)} %act_ref.5) | copy-start | bytes 3145732
  2.4 1.0 %copy-start.2 = (bf16[1024,256]{1,0:T(8,128)(2,1)S(1)}, bf16[1024,256]{1,0:T(8,128)(2,1)}, u32[]{:S(2)}) copy-start(bf16[1024,256]{1,0:T(8,128)(2,1)} %w_ref.1) | copy-start | bytes 1572868
  3.9 9.5 %copy-start.3 = (f32[2]{0:T(128)S(1)}, f32[2]{0:T(128)}, u32[]{:S(2)}) copy-start(f32[2]{0:T(128)} %own_bias.5) | copy-start | bytes 28
  3.9 9.6 %copy-start = (bf16[256,1024]{1,0:T(8,128)(2,1)S(1)}, bf16[256,1024]{1,0:T(8,128)(2,1)}, u32[]{:S(2)}) copy-start(bf16[256,1024]{1,0:T(8,128)(2,1)} %w1.3) | copy-start | bytes 1572868
  3.9 12.0 %copy-start.4 = (bf16[2048,1024]{1,0:T(8,128)(2,1)S(1)}, bf16[2048,1024]{1,0:T(8,128)(2,1)}, u32[]{:S(2)}) copy-start(bf16[2048,1024]{1,0:T(8,128)(2,1)} %act_ref.3) | copy-start | bytes 12582916
  3.9 12.0 %copy-start.5 = (s32[256,1024]{1,0:T(8,128)S(1)}, s32[256,1024]{1,0:T(8,128)}, u32[]{:S(2)}) copy-start(s32[256,1024]{1,0:T(8,128)} %mask_hbm.1) | copy-start | bytes 3145732
  3.9 12.0 %copy-start.6 = (bf16[1024,256]{1,0:T(8,128)(2,1)S(1)}, bf16[1024,256]{1,0:T(8,128)(2,1)}, u32[]{:S(2)}) copy-start(bf16[1024,256]{1,0:T(8,128)(2,1)} %wk1.1) | copy-start | bytes 1572868
  4.0 12.0 %copy-start.7 = (bf16[1024,256]{1,0:T(8,128)(2,1)S(1)}, bf16[1024,256]{1,0:T(8,128)(2,1)}, u32[]{:S(2)}) copy-start(bf16[1024,256]{1,0:T(8,128)(2,1)} %wv1.1) | copy-start | bytes 1572868
  4.0 12.0 %copy-start.8 = (s32[131072]{0:T(1024)S(1)}, s32[131072]{0:T(1024)}, u32[]{:S(2)}) copy-start(s32[131072]{0:T(1024)} %param.19) | copy-start | bytes 1572868
  4.0 12.0 %copy-start.9 = (s32[32768]{0:T(1024)S(1)}, s32[32768]{0:T(1024)}, u32[]{:S(2)}) copy-start(s32[32768]{0:T(1024)} %param.18) | copy-start | bytes 393220
  4.4 18.0 %collective-permute-start.6 = (bf16[512,512]{1,0:T(8,128)(2,1)S(1)}, bf16[512,512]{1,0:T(8,128)(2,1)S(1)}, u32[]{:S(2)}, u32[]{:S(2)}) collective-permute-start(bf16[512,512]{1,0:T(8,128)(2,1)S(1)} %join_queries.1.q_ref), channel_id=1, source_target_pairs={{0,1},{1,0},{2,3},{3,2},{4,5},{5,4},{6,7},{7,6},{8,9},{9,8},{10,11... | collective-permute-start | bytes 1572872 | tf_op jit(solution)/shard_map/ppermute | solution.py:307
  13.4 7.8 %collective-permute-start.2 = (f32[2]{0:T(128)S(1)}, f32[2]{0:T(128)S(1)}, u32[]{:S(2)}, u32[]{:S(2)}) collective-permute-start(f32[2]{0:T(128)S(1)} %copy-done.3), channel_id=1, source_target_pairs={{0,64},{64,0},{128,192},{192,128},{1,65},{65,1},{129,193},{193,129... | collective-permute-start | bytes 32 | tf_op jit(solution)/shard_map/ppermute | solution.py:46
  13.5 38.0 %collective-permute-start.8 = (bf16[256,1024]{1,0:T(8,128)(2,1)S(1)}, bf16[256,1024]{1,0:T(8,128)(2,1)S(1)}, u32[]{:S(2)}, u32[]{:S(2)}) collective-permute-start(bf16[256,1024]{1,0:T(8,128)(2,1)S(1)} %copy-done), channel_id=1, source_target_pairs={{0,64},{64,0},{128,192},{192,128},{1,65},{65,1},{129,193},{193,129... | collective-permute-start | bytes 1572872 | tf_op jit(solution)/shard_map/ppermute | solution.py:46
  14.0 25.6 %collective-permute-start.4 = (bf16[512,512]{1,0:T(8,128)(2,1)S(1)}, bf16[512,512]{1,0:T(8,128)(2,1)S(1)}, u32[]{:S(2)}, u32[]{:S(2)}) collective-permute-start(bf16[512,512]{1,0:T(8,128)(2,1)S(1)} %join_queries.1.q_ref), channel_id=1, source_target_pairs={{2,4},{4,2},{3,5},{5,3},{6,8},{8,6},{7,9},{9,7},{10,12},{12,10},{1... | collective-permute-start | bytes 1572872 | tf_op jit(solution)/shard_map/ppermute | solution.py:307
  25.9 25.6 %collective-permute-start.7 = (bf16[512,512]{1,0:T(8,128)(2,1)S(1)}, bf16[512,512]{1,0:T(8,128)(2,1)S(1)}, u32[]{:S(2)}, u32[]{:S(2)}) collective-permute-start(bf16[512,512]{1,0:T(8,128)(2,1)S(1)} %shard_map.102), channel_id=1, source_target_pairs={{0,1},{1,0},{2,3},{3,2},{4,5},{5,4},{6,7},{7,6},{8,9},{9,8},{10,11... | collective-permute-start | bytes 1572872 | tf_op jit(solution)/shard_map/ppermute | solution.py:307
  45.7 13.7 %collective-permute-start.5 = (bf16[512,512]{1,0:T(8,128)(2,1)S(1)}, bf16[512,512]{1,0:T(8,128)(2,1)S(1)}, u32[]{:S(2)}, u32[]{:S(2)}) collective-permute-start(bf16[512,512]{1,0:T(8,128)(2,1)S(1)} %shard_map.101), channel_id=1, source_target_pairs={{2,4},{4,2},{3,5},{5,3},{6,8},{8,6},{7,9},{9,7},{10,12},{12,10},{1... | collective-permute-start | bytes 1572872 | tf_op jit(solution)/shard_map/ppermute | solution.py:307
  59.9 1.6 %collective-permute-start.10 = (bf16[512,256]{1,0:T(8,128)(2,1)S(1)}, bf16[512,256]{1,0:T(8,128)(2,1)S(1)}, u32[]{:S(2)}, u32[]{:S(2)}) collective-permute-start(bf16[512,256]{1,0:T(8,128)(2,1)S(1)} %get-tuple-element.22), channel_id=1, source_target_pairs={{0,64},{64,0},{128,192},{192,128},{1,65},{65,1},{129,193},{193,129... | collective-permute-start | bytes 786440 | tf_op jit(solution)/shard_map/ppermute | solution.py:46
  60.4 6.5 %collective-permute-start.9 = (bf16[512,256]{1,0:T(8,128)(2,1)S(1)}, bf16[512,256]{1,0:T(8,128)(2,1)S(1)}, u32[]{:S(2)}, u32[]{:S(2)}) collective-permute-start(bf16[512,256]{1,0:T(8,128)(2,1)S(1)} %get-tuple-element.20), channel_id=1, source_target_pairs={{0,64},{64,0},{128,192},{192,128},{1,65},{65,1},{129,193},{193,129... | collective-permute-start | bytes 786440 | tf_op jit(solution)/shard_map/ppermute | solution.py:46
  61.5 17.2 %collective-permute-start.11 = (bf16[512,256]{1,0:T(8,128)(2,1)S(1)}, bf16[512,256]{1,0:T(8,128)(2,1)S(1)}, u32[]{:S(2)}, u32[]{:S(2)}) collective-permute-start(bf16[512,256]{1,0:T(8,128)(2,1)S(1)} %add_convert_fusion), channel_id=1, source_target_pairs={{0,128},{128,0},{64,192},{192,64},{1,129},{129,1},{65,193},{193,65... | collective-permute-start | bytes 786440 | tf_op jit(solution)/shard_map/ppermute | solution.py:328

commit v6 on v5

--- a/solution.py
+++ b/solution.py
@@ -11,7 +11,7 @@
 
 TILE = 128
 REACH = 2
-CHUNK = 1024
+STEPS = {None: 2048, 0: 1024, 1: 2048}
 BLOCK = 512
 SPAN = 32
 BYS = (2, 1)
@@ -169,7 +169,8 @@
 ):
     *o_refs, acc = rest
     tiles = q_ref.shape[0] // TILE
-    per_chunk = CHUNK // TILE
+    step = STEPS[turn]
+    per_chunk = step // TILE
     dim = TILE
     scale = 0.5 / math.sqrt(dim)
     me, count = lax.axis_index("peak"), lax.axis_size("peak")
@@ -192,7 +193,7 @@
     local = own_bias.shape[0]
 
     def chunk(c, carry):
-        rows = pl.ds(pl.multiple_of(c * CHUNK, CHUNK), CHUNK)
+        rows = pl.ds(pl.multiple_of(c * step, step), step)
         peaks = [peak_ref[pl.ds(c * per_chunk + j, 1), :] for j in range(per_chunk)]
         inside = [
             [

time: 79.7 us -> 79.5 us (level)
  starting transfers between devices: 34.2 us -> 31.7 us
  Pallas kernels: 21.3 us -> 23.5 us
    ppermute x4, starting transfers between devices: 26.4 us -> 23.8 us  [travel(): return lax.ppermute(x, ('gene', 'peak'), swap_pairs(genes, count, turn))]
    pallas_call x3, Pallas kernels: 13.5 us -> 15.6 us  [attend(): pl.pallas_call(functools.partial(attend_kernel, turn, heads), in_specs=[S...]
  transfers between devices with their start and end apart: 12 -> 12, of which waited for: 4 -> 4; matrix products, arithmetic and copies ran while one was open for 0% -> 0% of each run, Pallas kernels for 25% -> 28%
where the time goes in v6:
time: 79.5 us; the launch traced here: 79.2 us
  starting transfers between devices  31.7 us (40%)
  Pallas kernels  23.5 us (30%)
  waiting for transfers between devices  21.4 us (27%)
  local copies, waits for them, and re-layouts  2.32 us (3%)
    ppermute x4, starting transfers between devices, travel(): return lax.ppermute(x, ('gene', 'peak'), swap_pairs(genes, count, turn))  23.8 us
    pallas_call x3, Pallas kernels, attend(): pl.pallas_call(functools.partial(attend_kernel, turn, heads), in_specs=[S...  15.6 us
    ppermute x1, waiting for transfers between devices, on_device(): other = lax.ppermute(half.astype(BF16), 'gene', pairs)  11.7 us
    ppermute x4, waiting for transfers between devices, travel(): return lax.ppermute(x, ('gene', 'peak'), swap_pairs(genes, count, turn))  9.22 us
    ppermute x1, starting transfers between devices, on_device(): other = lax.ppermute(half.astype(BF16), 'gene', pairs)  5.52 us
    pallas_call x1, Pallas kernels, project_kv(): pl.pallas_call(functools.partial(kv_kernel, gene_tiles), in_specs=[VMEM]...  5.25 us
    ppermute x7, starting transfers between devices, core_swap(): return lax.ppermute(x, 'gene', [(0, 1), (1, 0), (2, 3), (3, 2)])  2.43 us
    unnamed x20, local copies, waits for them, and re-layouts  2.32 us
  transfers between devices with their start and end apart: 12, of which 4 were waited for; matrix products, arithmetic and copies ran while one was open for 0% of the time, Pallas kernels for 28%

profile of v6, /device:TPU:3, one launch (start us, length us, event | category | flops | bytes accessed | tf_op | source)
XLA Modules:
  0.0 79.2 jit_solution(11749026983293302767)
XLA Ops:
  0.0 0.7 collective-permute-start.3
  0.7 0.0 collective-permute-start
  0.7 0.5 collective-permute-start.1
  1.2 0.0 copy-start.1
  1.2 1.2 %copy-done.1 = bf16[512,1024]{1,0:T(8,128)(2,1)S(1)} copy-done((bf16[512,1024]{1,0:T(8,128)(2,1)S(1)}, bf16[512,1024]{1,0:T(8,128)(2,1)}, u32[]{:S(2)}) %copy-start.1) | copy-done | bytes 1048600
  2.4 0.0 copy-start.2
  2.4 1.0 %copy-done.2 = bf16[1024,256]{1,0:T(8,128)(2,1)S(1)} copy-done((bf16[1024,256]{1,0:T(8,128)(2,1)S(1)}, bf16[1024,256]{1,0:T(8,128)(2,1)}, u32[]{:S(2)}) %copy-start.2) | copy-done | bytes 524312
  3.5 0.4 project_queries.1.own_ref
  3.9 0.0 copy-start.3
  3.9 0.0 copy-start
  3.9 0.0 copy-start.4
  3.9 0.0 copy-start.5
  3.9 0.0 copy-start.6
  4.0 0.0 copy-start.7
  4.0 0.0 copy-start.8
  4.0 0.0 copy-start.9
  4.0 0.0 collective-permute-done.3.w_ref
  4.0 0.4 join_queries.1.q_ref
  4.4 8.9 %collective-permute-start.6 = (bf16[512,512]{1,0:T(8,128)(2,1)S(1)}, bf16[512,512]{1,0:T(8,128)(2,1)S(1)}, u32[]{:S(2)}, u32[]{:S(2)}) collective-permute-start(bf16[512,512]{1,0:T(8,128)(2,1)S(1)} %join_queries.1.q_ref), channel_id=1, source_target_pairs={{0,1},{1,0},{2,3},{3,2},{4,5},{5,4},{6,7},{7,6},{8,9},{9,8},{10,11... | collective-permute-start | bytes 1572872 | tf_op jit(solution)/shard_map/ppermute | solution.py:308
  13.4 0.0 copy-done.3
  13.4 0.1 collective-permute-start.2
  13.5 0.0 copy-done
  13.5 0.5 collective-permute-start.8
  14.0 0.0 collective-permute-done.wk2
  14.0 1.9 %collective-permute-start.4 = (bf16[512,512]{1,0:T(8,128)(2,1)S(1)}, bf16[512,512]{1,0:T(8,128)(2,1)S(1)}, u32[]{:S(2)}, u32[]{:S(2)}) collective-permute-start(bf16[512,512]{1,0:T(8,128)(2,1)S(1)} %join_queries.1.q_ref), channel_id=1, source_target_pairs={{2,4},{4,2},{3,5},{5,3},{6,8},{8,6},{7,9},{9,7},{10,12},{12,10},{1... | collective-permute-start | bytes 1572872 | tf_op jit(solution)/shard_map/ppermute | solution.py:308
  15.9 0.0 collective-permute-done.1.wv2
  15.9 0.0 copy-done.4
  15.9 0.0 copy-done.5
  16.0 0.0 copy-done.6
  16.0 0.0 copy-done.7
  16.0 0.0 copy-done.8
  16.0 0.0 copy-done.9
  16.0 5.2 %project_kv.1 = (bf16[2048,512]{1,0:T(8,128)(2,1)S(1)}, bf16[2048,512]{1,0:T(8,128)(2,1)S(1)}, s32[8,128]{1,0:T(8,128)S(1)}, s32[32,128]{1,0:T(8,128)S(1)}, s32[16,128]{1,0:T(8,128)S(1)}) custom-call(bf16[2048,1024]{1,0:T(8,128)(2,1)S(1)} %copy-done.4, bf16[1024,256]{1,0:T(8,128)(2,1)S(1)} %copy-done.6, bf16[1024,256]{1,0:T(8,128)(2,1)S(1)} %collective-permute-done.wk2, ...), custom_call_target="tpu_custom_call" | custom-call | flops 4294967296 | bytes 8388608 | tf_op jit(solution)/shard_map/project_kv/pallas_call | solution.py:145
  21.3 0.0 collective-permute-done.2.other_bias
  21.3 1.2 %collective-permute-done.6.q_ref = bf16[512,512]{1,0:T(8,128)(2,1)S(1)} collective-permute-done((bf16[512,512]{1,0:T(8,128)(2,1)S(1)}, bf16[512,512]{1,0:T(8,128)(2,1)S(1)}, u32[]{:S(2)}, u32[]{:S(2)}) %collective-permute-start.6) | collective-permute-done | bytes 524320 | tf_op jit(solution)/shard_map/ppermute | solution.py:308
  22.4 5.8 %shard_map.102 = bf16[512,512]{1,0:T(8,128)(2,1)S(1)} custom-call(s32[8,128]{1,0:T(8,128)S(1)} %get-tuple-element.14.runs_ref, f32[2]{0:T(128)S(1)} %copy-done.3, f32[2]{0:T(128)S(1)} %collective-permute-done.2.other_bias, s32[32,128]{1,0:T(8,128)S(1)} %get-tuple-element.15.gene_ref, s32[16,128]{1,0:T(8,128)S(1)} %get-tuple-element.16.peak_ref, ...), custom_call_target="tpu_custom_call" | custom-call | flops 2147483648 | bytes 5242880 | tf_op jit(solution)/shard_map/pallas_call | solution.py:232
  28.3 11.0 %collective-permute-start.7 = (bf16[512,512]{1,0:T(8,128)(2,1)S(1)}, bf16[512,512]{1,0:T(8,128)(2,1)S(1)}, u32[]{:S(2)}, u32[]{:S(2)}) collective-permute-start(bf16[512,512]{1,0:T(8,128)(2,1)S(1)} %shard_map.102), channel_id=1, source_target_pairs={{0,1},{1,0},{2,3},{3,2},{4,5},{5,4},{6,7},{7,6},{8,9},{9,8},{10,11... | collective-permute-start | bytes 1572872 | tf_op jit(solution)/shard_map/ppermute | solution.py:308
  39.3 0.0 collective-permute-done.4.q_ref
  39.3 6.3 %shard_map.101 = bf16[512,512]{1,0:T(8,128)(2,1)S(1)} custom-call(s32[8,128]{1,0:T(8,128)S(1)} %get-tuple-element.14.runs_ref, f32[2]{0:T(128)S(1)} %copy-done.3, f32[2]{0:T(128)S(1)} %collective-permute-done.2.other_bias, s32[32,128]{1,0:T(8,128)S(1)} %get-tuple-element.15.gene_ref, s32[16,128]{1,0:T(8,128)S(1)} %get-tuple-element.16.peak_ref, ...), custom_call_target="tpu_custom_call" | custom-call | flops 2147483648 | bytes 5242880 | tf_op jit(solution)/shard_map/pallas_call | solution.py:232
  45.6 1.9 %collective-permute-start.5 = (bf16[512,512]{1,0:T(8,128)(2,1)S(1)}, bf16[512,512]{1,0:T(8,128)(2,1)S(1)}, u32[]{:S(2)}, u32[]{:S(2)}) collective-permute-start(bf16[512,512]{1,0:T(8,128)(2,1)S(1)} %shard_map.101), channel_id=1, source_target_pairs={{2,4},{4,2},{3,5},{5,3},{6,8},{8,6},{7,9},{9,7},{10,12},{12,10},{1... | collective-permute-start | bytes 1572872 | tf_op jit(solution)/shard_map/ppermute | solution.py:308
  47.6 3.5 %shard_map.100.own_ref = f32[512,256]{1,0:T(8,128)S(1)} custom-call(s32[8,128]{1,0:T(8,128)S(1)} %get-tuple-element.14.runs_ref, f32[2]{0:T(128)S(1)} %copy-done.3, f32[2]{0:T(128)S(1)} %collective-permute-done.2.other_bias, s32[32,128]{1,0:T(8,128)S(1)} %get-tuple-element.15.gene_ref, s32[16,128]{1,0:T(8,128)S(1)} %get-tuple-element.16.peak_ref, ...), custom_call_target="tpu_custom_call" | custom-call | flops 1073741824 | bytes 5242880 | tf_op jit(solution)/shard_map/pallas_call | solution.py:232
  51.0 0.0 collective-permute-done.8.w2
  51.0 0.0 collective-permute-done.7.second_ref
  51.1 8.1 %collective-permute-done.5.first_ref = bf16[512,512]{1,0:T(8,128)(2,1)S(1)} collective-permute-done((bf16[512,512]{1,0:T(8,128)(2,1)S(1)}, bf16[512,512]{1,0:T(8,128)(2,1)S(1)}, u32[]{:S(2)}, u32[]{:S(2)}) %collective-permute-start.5) | collective-permute-done | bytes 524320 | tf_op jit(solution)/shard_map/ppermute | solution.py:308
  59.1 0.4 mix_across.1
  59.6 0.1 collective-permute-start.10
  59.7 0.5 mix_here.1
  60.1 0.6 collective-permute-start.9
  60.7 0.5 collective-permute-done.10
  61.2 0.1 add_convert_fusion
  61.3 5.5 %collective-permute-start.11 = (bf16[512,256]{1,0:T(8,128)(2,1)S(1)}, bf16[512,256]{1,0:T(8,128)(2,1)S(1)}, u32[]{:S(2)}, u32[]{:S(2)}) collective-permute-start(bf16[512,256]{1,0:T(8,128)(2,1)S(1)} %add_convert_fusion), channel_id=1, source_target_pairs={{0,128},{128,0},{64,192},{192,64},{1,129},{129,1},{65,193},{193,65... | collective-permute-start | bytes 786440 | tf_op jit(solution)/shard_map/ppermute | solution.py:329
  66.8 0.0 collective-permute-done.9.core_ref
  66.8 11.7 %collective-permute-done.11.z_ref = bf16[512,256]{1,0:T(8,128)(2,1)S(1)} collective-permute-done((bf16[512,256]{1,0:T(8,128)(2,1)S(1)}, bf16[512,256]{1,0:T(8,128)(2,1)S(1)}, u32[]{:S(2)}, u32[]{:S(2)}) %collective-permute-start.11) | collective-permute-done | bytes 262176 | tf_op jit(solution)/shard_map/ppermute | solution.py:329
  78.4 0.8 finish.1
Async XLA Ops:
  0.0 4.0 %collective-permute-start.3 = (bf16[1024,256]{1,0:T(8,128)(2,1)}, bf16[1024,256]{1,0:T(8,128)(2,1)S(1)}, u32[]{:S(2)}, u32[]{:S(2)}) collective-permute-start(bf16[1024,256]{1,0:T(8,128)(2,1)} %w_ref.1), channel_id=1, source_target_pairs={{0,64},{64,0},{128,192},{192,128},{1,65},{65,1},{129,193},{193,129... | collective-permute-start | bytes 1572872 | tf_op jit(solution)/shard_map/ppermute | solution.py:46
  0.7 13.3 %collective-permute-start = (bf16[1024,256]{1,0:T(8,128)(2,1)}, bf16[1024,256]{1,0:T(8,128)(2,1)S(1)}, u32[]{:S(2)}, u32[]{:S(2)}) collective-permute-start(bf16[1024,256]{1,0:T(8,128)(2,1)} %wk1.1), channel_id=1, source_target_pairs={{0,64},{64,0},{128,192},{192,128},{1,65},{65,1},{129,193},{193,129... | collective-permute-start | bytes 1572872 | tf_op jit(solution)/shard_map/ppermute | solution.py:46
  0.7 15.2 %collective-permute-start.1 = (bf16[1024,256]{1,0:T(8,128)(2,1)}, bf16[1024,256]{1,0:T(8,128)(2,1)S(1)}, u32[]{:S(2)}, u32[]{:S(2)}) collective-permute-start(bf16[1024,256]{1,0:T(8,128)(2,1)} %wv1.1), channel_id=1, source_target_pairs={{0,64},{64,0},{128,192},{192,128},{1,65},{65,1},{129,193},{193,129... | collective-permute-start | bytes 1572872 | tf_op jit(solution)/shard_map/ppermute | solution.py:46
  1.2 1.2 %copy-start.1 = (bf16[512,1024]{1,0:T(8,128)(2,1)S(1)}, bf16[512,1024]{1,0:T(8,128)(2,1)}, u32[]{:S(2)}) copy-start(bf16[512,1024]{1,0:T(8,128)(2,1)} %act_ref.5) | copy-start | bytes 3145732
  2.4 1.0 %copy-start.2 = (bf16[1024,256]{1,0:T(8,128)(2,1)S(1)}, bf16[1024,256]{1,0:T(8,128)(2,1)}, u32[]{:S(2)}) copy-start(bf16[1024,256]{1,0:T(8,128)(2,1)} %w_ref.1) | copy-start | bytes 1572868
  3.9 9.5 %copy-start.3 = (f32[2]{0:T(128)S(1)}, f32[2]{0:T(128)}, u32[]{:S(2)}) copy-start(f32[2]{0:T(128)} %own_bias.5) | copy-start | bytes 28
  3.9 9.6 %copy-start = (bf16[256,1024]{1,0:T(8,128)(2,1)S(1)}, bf16[256,1024]{1,0:T(8,128)(2,1)}, u32[]{:S(2)}) copy-start(bf16[256,1024]{1,0:T(8,128)(2,1)} %w1.3) | copy-start | bytes 1572868
  3.9 12.0 %copy-start.4 = (bf16[2048,1024]{1,0:T(8,128)(2,1)S(1)}, bf16[2048,1024]{1,0:T(8,128)(2,1)}, u32[]{:S(2)}) copy-start(bf16[2048,1024]{1,0:T(8,128)(2,1)} %act_ref.3) | copy-start | bytes 12582916
  3.9 12.0 %copy-start.5 = (s32[256,1024]{1,0:T(8,128)S(1)}, s32[256,1024]{1,0:T(8,128)}, u32[]{:S(2)}) copy-start(s32[256,1024]{1,0:T(8,128)} %mask_hbm.1) | copy-start | bytes 3145732
  3.9 12.0 %copy-start.6 = (bf16[1024,256]{1,0:T(8,128)(2,1)S(1)}, bf16[1024,256]{1,0:T(8,128)(2,1)}, u32[]{:S(2)}) copy-start(bf16[1024,256]{1,0:T(8,128)(2,1)} %wk1.1) | copy-start | bytes 1572868
  4.0 12.0 %copy-start.7 = (bf16[1024,256]{1,0:T(8,128)(2,1)S(1)}, bf16[1024,256]{1,0:T(8,128)(2,1)}, u32[]{:S(2)}) copy-start(bf16[1024,256]{1,0:T(8,128)(2,1)} %wv1.1) | copy-start | bytes 1572868
  4.0 12.0 %copy-start.8 = (s32[131072]{0:T(1024)S(1)}, s32[131072]{0:T(1024)}, u32[]{:S(2)}) copy-start(s32[131072]{0:T(1024)} %param.19) | copy-start | bytes 1572868
  4.0 12.0 %copy-start.9 = (s32[32768]{0:T(1024)S(1)}, s32[32768]{0:T(1024)}, u32[]{:S(2)}) copy-start(s32[32768]{0:T(1024)} %param.18) | copy-start | bytes 393220
  4.4 18.0 %collective-permute-start.6 = (bf16[512,512]{1,0:T(8,128)(2,1)S(1)}, bf16[512,512]{1,0:T(8,128)(2,1)S(1)}, u32[]{:S(2)}, u32[]{:S(2)}) collective-permute-start(bf16[512,512]{1,0:T(8,128)(2,1)S(1)} %join_queries.1.q_ref), channel_id=1, source_target_pairs={{0,1},{1,0},{2,3},{3,2},{4,5},{5,4},{6,7},{7,6},{8,9},{9,8},{10,11... | collective-permute-start | bytes 1572872 | tf_op jit(solution)/shard_map/ppermute | solution.py:308
  13.4 7.8 %collective-permute-start.2 = (f32[2]{0:T(128)S(1)}, f32[2]{0:T(128)S(1)}, u32[]{:S(2)}, u32[]{:S(2)}) collective-permute-start(f32[2]{0:T(128)S(1)} %copy-done.3), channel_id=1, source_target_pairs={{0,64},{64,0},{128,192},{192,128},{1,65},{65,1},{129,193},{193,129... | collective-permute-start | bytes 32 | tf_op jit(solution)/shard_map/ppermute | solution.py:46
  13.5 37.5 %collective-permute-start.8 = (bf16[256,1024]{1,0:T(8,128)(2,1)S(1)}, bf16[256,1024]{1,0:T(8,128)(2,1)S(1)}, u32[]{:S(2)}, u32[]{:S(2)}) collective-permute-start(bf16[256,1024]{1,0:T(8,128)(2,1)S(1)} %copy-done), channel_id=1, source_target_pairs={{0,64},{64,0},{128,192},{192,128},{1,65},{65,1},{129,193},{193,129... | collective-permute-start | bytes 1572872 | tf_op jit(solution)/shard_map/ppermute | solution.py:46
  14.0 25.3 %collective-permute-start.4 = (bf16[512,512]{1,0:T(8,128)(2,1)S(1)}, bf16[512,512]{1,0:T(8,128)(2,1)S(1)}, u32[]{:S(2)}, u32[]{:S(2)}) collective-permute-start(bf16[512,512]{1,0:T(8,128)(2,1)S(1)} %join_queries.1.q_ref), channel_id=1, source_target_pairs={{2,4},{4,2},{3,5},{5,3},{6,8},{8,6},{7,9},{9,7},{10,12},{12,10},{1... | collective-permute-start | bytes 1572872 | tf_op jit(solution)/shard_map/ppermute | solution.py:308
  28.3 22.8 %collective-permute-start.7 = (bf16[512,512]{1,0:T(8,128)(2,1)S(1)}, bf16[512,512]{1,0:T(8,128)(2,1)S(1)}, u32[]{:S(2)}, u32[]{:S(2)}) collective-permute-start(bf16[512,512]{1,0:T(8,128)(2,1)S(1)} %shard_map.102), channel_id=1, source_target_pairs={{0,1},{1,0},{2,3},{3,2},{4,5},{5,4},{6,7},{7,6},{8,9},{9,8},{10,11... | collective-permute-start | bytes 1572872 | tf_op jit(solution)/shard_map/ppermute | solution.py:308
  45.6 13.5 %collective-permute-start.5 = (bf16[512,512]{1,0:T(8,128)(2,1)S(1)}, bf16[512,512]{1,0:T(8,128)(2,1)S(1)}, u32[]{:S(2)}, u32[]{:S(2)}) collective-permute-start(bf16[512,512]{1,0:T(8,128)(2,1)S(1)} %shard_map.101), channel_id=1, source_target_pairs={{2,4},{4,2},{3,5},{5,3},{6,8},{8,6},{7,9},{9,7},{10,12},{12,10},{1... | collective-permute-start | bytes 1572872 | tf_op jit(solution)/shard_map/ppermute | solution.py:308
  59.6 1.6 %collective-permute-start.10 = (bf16[512,256]{1,0:T(8,128)(2,1)S(1)}, bf16[512,256]{1,0:T(8,128)(2,1)S(1)}, u32[]{:S(2)}, u32[]{:S(2)}) collective-permute-start(bf16[512,256]{1,0:T(8,128)(2,1)S(1)} %get-tuple-element.22), channel_id=1, source_target_pairs={{0,64},{64,0},{128,192},{192,128},{1,65},{65,1},{129,193},{193,129... | collective-permute-start | bytes 786440 | tf_op jit(solution)/shard_map/ppermute | solution.py:46
  60.1 6.6 %collective-permute-start.9 = (bf16[512,256]{1,0:T(8,128)(2,1)S(1)}, bf16[512,256]{1,0:T(8,128)(2,1)S(1)}, u32[]{:S(2)}, u32[]{:S(2)}) collective-permute-start(bf16[512,256]{1,0:T(8,128)(2,1)S(1)} %get-tuple-element.20), channel_id=1, source_target_pairs={{0,64},{64,0},{128,192},{192,128},{1,65},{65,1},{129,193},{193,129... | collective-permute-start | bytes 786440 | tf_op jit(solution)/shard_map/ppermute | solution.py:46
  61.3 17.2 %collective-permute-start.11 = (bf16[512,256]{1,0:T(8,128)(2,1)S(1)}, bf16[512,256]{1,0:T(8,128)(2,1)S(1)}, u32[]{:S(2)}, u32[]{:S(2)}) collective-permute-start(bf16[512,256]{1,0:T(8,128)(2,1)S(1)} %add_convert_fusion), channel_id=1, source_target_pairs={{0,128},{128,0},{64,192},{192,64},{1,129},{129,1},{65,193},{193,65... | collective-permute-start | bytes 786440 | tf_op jit(solution)/shard_map/ppermute | solution.py:329

commit v7 on v6

--- a/solution.py
+++ b/solution.py
@@ -186,14 +186,14 @@
     high = functools.reduce(jnp.maximum, highs)
     first = low // per_chunk
     last = jnp.where(valid, (high + per_chunk - 1) // per_chunk, first)
-    acc[...] = jnp.zeros_like(acc)
+    whole = step == k_ref.shape[0]
     tags = [
         jnp.broadcast_to(gene_ref[pl.ds(base + i, 1), :], (TILE, TILE)).T for i in range(tiles)
     ]
     local = own_bias.shape[0]
 
     def chunk(c, carry):
-        rows = pl.ds(pl.multiple_of(c * step, step), step)
+        rows = slice(None) if whole else pl.ds(pl.multiple_of(c * step, step), step)
         peaks = [peak_ref[pl.ds(c * per_chunk + j, 1), :] for j in range(per_chunk)]
         inside = [
             [
@@ -217,9 +217,25 @@
                     band.append(jnp.where(tags[i] == inside[i][j], part, 0.0))
                 bands.append(jnp.concatenate(band, 1))
             weights = jnp.concatenate(bands, 0).astype(BF16)
-            acc[:, cols] += jnp.dot(weights, v_ref[rows, cols], preferred_element_type=F32)
+            part = jnp.dot(weights, v_ref[rows, cols], preferred_element_type=F32)
+            if whole:
+                o_refs[0][:, cols] = (part * 0.5).astype(o_refs[0].dtype)
+            else:
+                acc[:, cols] += part
         return carry
 
+    if whole:
+
+        @pl.when(last > first)
+        def _():
+            chunk(0, 0)
+
+        @pl.when(last <= first)
+        def _():
+            o_refs[0][...] = jnp.zeros_like(o_refs[0])
+
+        return
+    acc[...] = jnp.zeros_like(acc)
     lax.fori_loop(first, last, chunk, 0)
     size = o_refs[0].shape[0]
     for i, o_ref in enumerate(o_refs):

time: 79.5 us -> 79 us (level)
  transfers between devices with their start and end apart: 12 -> 12, of which waited for: 4 -> 4; matrix products, arithmetic and copies ran while one was open for 0% -> 0% of each run, Pallas kernels for 28% -> 27%
where the time goes in v7:
time: 79 us; the launch traced here: 78.8 us
  starting transfers between devices  31.7 us (40%)
  Pallas kernels  22.8 us (29%)
  waiting for transfers between devices  21.6 us (27%)
  local copies, waits for them, and re-layouts  2.32 us (3%)
    ppermute x4, starting transfers between devices, travel(): return lax.ppermute(x, ('gene', 'peak'), swap_pairs(genes, count, turn))  23.8 us
    pallas_call x3, Pallas kernels, attend(): pl.pallas_call(functools.partial(attend_kernel, turn, heads), in_specs=[S...  14.9 us
    ppermute x1, waiting for transfers between devices, on_device(): other = lax.ppermute(half.astype(BF16), 'gene', pairs)  11.7 us
    ppermute x4, waiting for transfers between devices, travel(): return lax.ppermute(x, ('gene', 'peak'), swap_pairs(genes, count, turn))  9.47 us
    ppermute x1, starting transfers between devices, on_device(): other = lax.ppermute(half.astype(BF16), 'gene', pairs)  5.51 us
    pallas_call x1, Pallas kernels, project_kv(): pl.pallas_call(functools.partial(kv_kernel, gene_tiles), in_specs=[VMEM]...  5.25 us
    ppermute x7, starting transfers between devices, core_swap(): return lax.ppermute(x, 'gene', [(0, 1), (1, 0), (2, 3), (3, 2)])  2.44 us
    unnamed x20, local copies, waits for them, and re-layouts  2.32 us
  transfers between devices with their start and end apart: 12, of which 4 were waited for; matrix products, arithmetic and copies ran while one was open for 0% of the time, Pallas kernels for 27%

profile of v7, /device:TPU:3, one launch (start us, length us, event | category | flops | bytes accessed | tf_op | source)
XLA Modules:
  0.0 78.8 jit_solution(4948514115320181033)
XLA Ops:
  0.0 0.7 collective-permute-start.3
  0.7 0.0 collective-permute-start
  0.7 0.5 collective-permute-start.1
  1.2 0.0 copy-start.1
  1.2 1.2 %copy-done.1 = bf16[512,1024]{1,0:T(8,128)(2,1)S(1)} copy-done((bf16[512,1024]{1,0:T(8,128)(2,1)S(1)}, bf16[512,1024]{1,0:T(8,128)(2,1)}, u32[]{:S(2)}) %copy-start.1) | copy-done | bytes 1048600
  2.4 0.0 copy-start.2
  2.4 1.0 %copy-done.2 = bf16[1024,256]{1,0:T(8,128)(2,1)S(1)} copy-done((bf16[1024,256]{1,0:T(8,128)(2,1)S(1)}, bf16[1024,256]{1,0:T(8,128)(2,1)}, u32[]{:S(2)}) %copy-start.2) | copy-done | bytes 524312
  3.5 0.4 project_queries.1.own_ref
  3.9 0.0 copy-start.3
  3.9 0.0 copy-start
  3.9 0.0 copy-start.4
  3.9 0.0 copy-start.5
  3.9 0.0 copy-start.6
  4.0 0.0 copy-start.7
  4.0 0.0 copy-start.8
  4.0 0.0 copy-start.9
  4.0 0.0 collective-permute-done.3.w_ref
  4.0 0.4 join_queries.1.q_ref
  4.4 8.9 %collective-permute-start.6 = (bf16[512,512]{1,0:T(8,128)(2,1)S(1)}, bf16[512,512]{1,0:T(8,128)(2,1)S(1)}, u32[]{:S(2)}, u32[]{:S(2)}) collective-permute-start(bf16[512,512]{1,0:T(8,128)(2,1)S(1)} %join_queries.1.q_ref), channel_id=1, source_target_pairs={{0,1},{1,0},{2,3},{3,2},{4,5},{5,4},{6,7},{7,6},{8,9},{9,8},{10,11... | collective-permute-start | bytes 1572872 | tf_op jit(solution)/shard_map/ppermute | solution.py:324
  13.4 0.0 copy-done.3
  13.4 0.1 collective-permute-start.2
  13.5 0.0 copy-done
  13.5 0.5 collective-permute-start.8
  14.0 0.0 collective-permute-done.wk2
  14.0 1.9 %collective-permute-start.4 = (bf16[512,512]{1,0:T(8,128)(2,1)S(1)}, bf16[512,512]{1,0:T(8,128)(2,1)S(1)}, u32[]{:S(2)}, u32[]{:S(2)}) collective-permute-start(bf16[512,512]{1,0:T(8,128)(2,1)S(1)} %join_queries.1.q_ref), channel_id=1, source_target_pairs={{2,4},{4,2},{3,5},{5,3},{6,8},{8,6},{7,9},{9,7},{10,12},{12,10},{1... | collective-permute-start | bytes 1572872 | tf_op jit(solution)/shard_map/ppermute | solution.py:324
  15.9 0.0 collective-permute-done.1.wv2
  15.9 0.0 copy-done.4
  15.9 0.0 copy-done.5
  16.0 0.0 copy-done.6
  16.0 0.0 copy-done.7
  16.0 0.0 copy-done.8
  16.0 0.0 copy-done.9
  16.0 5.2 %project_kv.1 = (bf16[2048,512]{1,0:T(8,128)(2,1)S(1)}, bf16[2048,512]{1,0:T(8,128)(2,1)S(1)}, s32[8,128]{1,0:T(8,128)S(1)}, s32[32,128]{1,0:T(8,128)S(1)}, s32[16,128]{1,0:T(8,128)S(1)}) custom-call(bf16[2048,1024]{1,0:T(8,128)(2,1)S(1)} %copy-done.4, bf16[1024,256]{1,0:T(8,128)(2,1)S(1)} %copy-done.6, bf16[1024,256]{1,0:T(8,128)(2,1)S(1)} %collective-permute-done.wk2, ...), custom_call_target="tpu_custom_call" | custom-call | flops 4294967296 | bytes 8388608 | tf_op jit(solution)/shard_map/project_kv/pallas_call | solution.py:145
  21.3 0.0 collective-permute-done.2.other_bias
  21.3 1.2 %collective-permute-done.6.q_ref = bf16[512,512]{1,0:T(8,128)(2,1)S(1)} collective-permute-done((bf16[512,512]{1,0:T(8,128)(2,1)S(1)}, bf16[512,512]{1,0:T(8,128)(2,1)S(1)}, u32[]{:S(2)}, u32[]{:S(2)}) %collective-permute-start.6) | collective-permute-done | bytes 524320 | tf_op jit(solution)/shard_map/ppermute | solution.py:324
  22.4 5.4 %shard_map.102 = bf16[512,512]{1,0:T(8,128)(2,1)S(1)} custom-call(s32[8,128]{1,0:T(8,128)S(1)} %get-tuple-element.14.runs_ref, f32[2]{0:T(128)S(1)} %copy-done.3, f32[2]{0:T(128)S(1)} %collective-permute-done.2.other_bias, s32[32,128]{1,0:T(8,128)S(1)} %get-tuple-element.15.gene_ref, s32[16,128]{1,0:T(8,128)S(1)} %get-tuple-element.16.peak_ref, ...), custom_call_target="tpu_custom_call" | custom-call | flops 2147483648 | bytes 5242880 | tf_op jit(solution)/shard_map/pallas_call | solution.py:248
  27.8 11.0 %collective-permute-start.7 = (bf16[512,512]{1,0:T(8,128)(2,1)S(1)}, bf16[512,512]{1,0:T(8,128)(2,1)S(1)}, u32[]{:S(2)}, u32[]{:S(2)}) collective-permute-start(bf16[512,512]{1,0:T(8,128)(2,1)S(1)} %shard_map.102), channel_id=1, source_target_pairs={{0,1},{1,0},{2,3},{3,2},{4,5},{5,4},{6,7},{7,6},{8,9},{9,8},{10,11... | collective-permute-start | bytes 1572872 | tf_op jit(solution)/shard_map/ppermute | solution.py:324
  38.8 0.0 collective-permute-done.4.q_ref
  38.9 6.3 %shard_map.101 = bf16[512,512]{1,0:T(8,128)(2,1)S(1)} custom-call(s32[8,128]{1,0:T(8,128)S(1)} %get-tuple-element.14.runs_ref, f32[2]{0:T(128)S(1)} %copy-done.3, f32[2]{0:T(128)S(1)} %collective-permute-done.2.other_bias, s32[32,128]{1,0:T(8,128)S(1)} %get-tuple-element.15.gene_ref, s32[16,128]{1,0:T(8,128)S(1)} %get-tuple-element.16.peak_ref, ...), custom_call_target="tpu_custom_call" | custom-call | flops 2147483648 | bytes 5242880 | tf_op jit(solution)/shard_map/pallas_call | solution.py:248
  45.2 1.9 %collective-permute-start.5 = (bf16[512,512]{1,0:T(8,128)(2,1)S(1)}, bf16[512,512]{1,0:T(8,128)(2,1)S(1)}, u32[]{:S(2)}, u32[]{:S(2)}) collective-permute-start(bf16[512,512]{1,0:T(8,128)(2,1)S(1)} %shard_map.101), channel_id=1, source_target_pairs={{2,4},{4,2},{3,5},{5,3},{6,8},{8,6},{7,9},{9,7},{10,12},{12,10},{1... | collective-permute-start | bytes 1572872 | tf_op jit(solution)/shard_map/ppermute | solution.py:324
  47.1 3.2 %shard_map.100.own_ref = f32[512,256]{1,0:T(8,128)S(1)} custom-call(s32[8,128]{1,0:T(8,128)S(1)} %get-tuple-element.14.runs_ref, f32[2]{0:T(128)S(1)} %copy-done.3, f32[2]{0:T(128)S(1)} %collective-permute-done.2.other_bias, s32[32,128]{1,0:T(8,128)S(1)} %get-tuple-element.15.gene_ref, s32[16,128]{1,0:T(8,128)S(1)} %get-tuple-element.16.peak_ref, ...), custom_call_target="tpu_custom_call" | custom-call | flops 1073741824 | bytes 5242880 | tf_op jit(solution)/shard_map/pallas_call | solution.py:248
  50.3 0.0 collective-permute-done.8.w2
  50.4 0.0 collective-permute-done.7.second_ref
  50.4 8.3 %collective-permute-done.5.first_ref = bf16[512,512]{1,0:T(8,128)(2,1)S(1)} collective-permute-done((bf16[512,512]{1,0:T(8,128)(2,1)S(1)}, bf16[512,512]{1,0:T(8,128)(2,1)S(1)}, u32[]{:S(2)}, u32[]{:S(2)}) %collective-permute-start.5) | collective-permute-done | bytes 524320 | tf_op jit(solution)/shard_map/ppermute | solution.py:324
  58.7 0.5 mix_across.1
  59.1 0.1 collective-permute-start.10
  59.2 0.5 mix_here.1
  59.7 0.6 collective-permute-start.9
  60.3 0.5 collective-permute-done.10
  60.8 0.1 add_convert_fusion
  60.8 5.5 %collective-permute-start.11 = (bf16[512,256]{1,0:T(8,128)(2,1)S(1)}, bf16[512,256]{1,0:T(8,128)(2,1)S(1)}, u32[]{:S(2)}, u32[]{:S(2)}) collective-permute-start(bf16[512,256]{1,0:T(8,128)(2,1)S(1)} %add_convert_fusion), channel_id=1, source_target_pairs={{0,128},{128,0},{64,192},{192,64},{1,129},{129,1},{65,193},{193,65... | collective-permute-start | bytes 786440 | tf_op jit(solution)/shard_map/ppermute | solution.py:345
  66.3 0.0 collective-permute-done.9.core_ref
  66.3 11.7 %collective-permute-done.11.z_ref = bf16[512,256]{1,0:T(8,128)(2,1)S(1)} collective-permute-done((bf16[512,256]{1,0:T(8,128)(2,1)S(1)}, bf16[512,256]{1,0:T(8,128)(2,1)S(1)}, u32[]{:S(2)}, u32[]{:S(2)}) %collective-permute-start.11) | collective-permute-done | bytes 262176 | tf_op jit(solution)/shard_map/ppermute | solution.py:345
  78.0 0.8 finish.1
Async XLA Ops:
  0.0 4.0 %collective-permute-start.3 = (bf16[1024,256]{1,0:T(8,128)(2,1)}, bf16[1024,256]{1,0:T(8,128)(2,1)S(1)}, u32[]{:S(2)}, u32[]{:S(2)}) collective-permute-start(bf16[1024,256]{1,0:T(8,128)(2,1)} %w_ref.1), channel_id=1, source_target_pairs={{0,64},{64,0},{128,192},{192,128},{1,65},{65,1},{129,193},{193,129... | collective-permute-start | bytes 1572872 | tf_op jit(solution)/shard_map/ppermute | solution.py:46
  0.7 13.3 %collective-permute-start = (bf16[1024,256]{1,0:T(8,128)(2,1)}, bf16[1024,256]{1,0:T(8,128)(2,1)S(1)}, u32[]{:S(2)}, u32[]{:S(2)}) collective-permute-start(bf16[1024,256]{1,0:T(8,128)(2,1)} %wk1.1), channel_id=1, source_target_pairs={{0,64},{64,0},{128,192},{192,128},{1,65},{65,1},{129,193},{193,129... | collective-permute-start | bytes 1572872 | tf_op jit(solution)/shard_map/ppermute | solution.py:46
  0.7 15.2 %collective-permute-start.1 = (bf16[1024,256]{1,0:T(8,128)(2,1)}, bf16[1024,256]{1,0:T(8,128)(2,1)S(1)}, u32[]{:S(2)}, u32[]{:S(2)}) collective-permute-start(bf16[1024,256]{1,0:T(8,128)(2,1)} %wv1.1), channel_id=1, source_target_pairs={{0,64},{64,0},{128,192},{192,128},{1,65},{65,1},{129,193},{193,129... | collective-permute-start | bytes 1572872 | tf_op jit(solution)/shard_map/ppermute | solution.py:46
  1.2 1.2 %copy-start.1 = (bf16[512,1024]{1,0:T(8,128)(2,1)S(1)}, bf16[512,1024]{1,0:T(8,128)(2,1)}, u32[]{:S(2)}) copy-start(bf16[512,1024]{1,0:T(8,128)(2,1)} %act_ref.5) | copy-start | bytes 3145732
  2.4 1.0 %copy-start.2 = (bf16[1024,256]{1,0:T(8,128)(2,1)S(1)}, bf16[1024,256]{1,0:T(8,128)(2,1)}, u32[]{:S(2)}) copy-start(bf16[1024,256]{1,0:T(8,128)(2,1)} %w_ref.1) | copy-start | bytes 1572868
  3.9 9.5 %copy-start.3 = (f32[2]{0:T(128)S(1)}, f32[2]{0:T(128)}, u32[]{:S(2)}) copy-start(f32[2]{0:T(128)} %own_bias.5) | copy-start | bytes 28
  3.9 9.6 %copy-start = (bf16[256,1024]{1,0:T(8,128)(2,1)S(1)}, bf16[256,1024]{1,0:T(8,128)(2,1)}, u32[]{:S(2)}) copy-start(bf16[256,1024]{1,0:T(8,128)(2,1)} %w1.3) | copy-start | bytes 1572868
  3.9 12.0 %copy-start.4 = (bf16[2048,1024]{1,0:T(8,128)(2,1)S(1)}, bf16[2048,1024]{1,0:T(8,128)(2,1)}, u32[]{:S(2)}) copy-start(bf16[2048,1024]{1,0:T(8,128)(2,1)} %act_ref.3) | copy-start | bytes 12582916
  3.9 12.0 %copy-start.5 = (s32[256,1024]{1,0:T(8,128)S(1)}, s32[256,1024]{1,0:T(8,128)}, u32[]{:S(2)}) copy-start(s32[256,1024]{1,0:T(8,128)} %mask_hbm.1) | copy-start | bytes 3145732
  3.9 12.0 %copy-start.6 = (bf16[1024,256]{1,0:T(8,128)(2,1)S(1)}, bf16[1024,256]{1,0:T(8,128)(2,1)}, u32[]{:S(2)}) copy-start(bf16[1024,256]{1,0:T(8,128)(2,1)} %wk1.1) | copy-start | bytes 1572868
  4.0 12.0 %copy-start.7 = (bf16[1024,256]{1,0:T(8,128)(2,1)S(1)}, bf16[1024,256]{1,0:T(8,128)(2,1)}, u32[]{:S(2)}) copy-start(bf16[1024,256]{1,0:T(8,128)(2,1)} %wv1.1) | copy-start | bytes 1572868
  4.0 12.0 %copy-start.8 = (s32[131072]{0:T(1024)S(1)}, s32[131072]{0:T(1024)}, u32[]{:S(2)}) copy-start(s32[131072]{0:T(1024)} %param.19) | copy-start | bytes 1572868
  4.0 12.0 %copy-start.9 = (s32[32768]{0:T(1024)S(1)}, s32[32768]{0:T(1024)}, u32[]{:S(2)}) copy-start(s32[32768]{0:T(1024)} %param.18) | copy-start | bytes 393220
  4.4 18.0 %collective-permute-start.6 = (bf16[512,512]{1,0:T(8,128)(2,1)S(1)}, bf16[512,512]{1,0:T(8,128)(2,1)S(1)}, u32[]{:S(2)}, u32[]{:S(2)}) collective-permute-start(bf16[512,512]{1,0:T(8,128)(2,1)S(1)} %join_queries.1.q_ref), channel_id=1, source_target_pairs={{0,1},{1,0},{2,3},{3,2},{4,5},{5,4},{6,7},{7,6},{8,9},{9,8},{10,11... | collective-permute-start | bytes 1572872 | tf_op jit(solution)/shard_map/ppermute | solution.py:324
  13.4 7.8 %collective-permute-start.2 = (f32[2]{0:T(128)S(1)}, f32[2]{0:T(128)S(1)}, u32[]{:S(2)}, u32[]{:S(2)}) collective-permute-start(f32[2]{0:T(128)S(1)} %copy-done.3), channel_id=1, source_target_pairs={{0,64},{64,0},{128,192},{192,128},{1,65},{65,1},{129,193},{193,129... | collective-permute-start | bytes 32 | tf_op jit(solution)/shard_map/ppermute | solution.py:46
  13.5 36.8 %collective-permute-start.8 = (bf16[256,1024]{1,0:T(8,128)(2,1)S(1)}, bf16[256,1024]{1,0:T(8,128)(2,1)S(1)}, u32[]{:S(2)}, u32[]{:S(2)}) collective-permute-start(bf16[256,1024]{1,0:T(8,128)(2,1)S(1)} %copy-done), channel_id=1, source_target_pairs={{0,64},{64,0},{128,192},{192,128},{1,65},{65,1},{129,193},{193,129... | collective-permute-start | bytes 1572872 | tf_op jit(solution)/shard_map/ppermute | solution.py:46
  14.0 24.8 %collective-permute-start.4 = (bf16[512,512]{1,0:T(8,128)(2,1)S(1)}, bf16[512,512]{1,0:T(8,128)(2,1)S(1)}, u32[]{:S(2)}, u32[]{:S(2)}) collective-permute-start(bf16[512,512]{1,0:T(8,128)(2,1)S(1)} %join_queries.1.q_ref), channel_id=1, source_target_pairs={{2,4},{4,2},{3,5},{5,3},{6,8},{8,6},{7,9},{9,7},{10,12},{12,10},{1... | collective-permute-start | bytes 1572872 | tf_op jit(solution)/shard_map/ppermute | solution.py:324
  27.8 22.5 %collective-permute-start.7 = (bf16[512,512]{1,0:T(8,128)(2,1)S(1)}, bf16[512,512]{1,0:T(8,128)(2,1)S(1)}, u32[]{:S(2)}, u32[]{:S(2)}) collective-permute-start(bf16[512,512]{1,0:T(8,128)(2,1)S(1)} %shard_map.102), channel_id=1, source_target_pairs={{0,1},{1,0},{2,3},{3,2},{4,5},{5,4},{6,7},{7,6},{8,9},{9,8},{10,11... | collective-permute-start | bytes 1572872 | tf_op jit(solution)/shard_map/ppermute | solution.py:324
  45.2 13.5 %collective-permute-start.5 = (bf16[512,512]{1,0:T(8,128)(2,1)S(1)}, bf16[512,512]{1,0:T(8,128)(2,1)S(1)}, u32[]{:S(2)}, u32[]{:S(2)}) collective-permute-start(bf16[512,512]{1,0:T(8,128)(2,1)S(1)} %shard_map.101), channel_id=1, source_target_pairs={{2,4},{4,2},{3,5},{5,3},{6,8},{8,6},{7,9},{9,7},{10,12},{12,10},{1... | collective-permute-start | bytes 1572872 | tf_op jit(solution)/shard_map/ppermute | solution.py:324
  59.1 1.6 %collective-permute-start.10 = (bf16[512,256]{1,0:T(8,128)(2,1)S(1)}, bf16[512,256]{1,0:T(8,128)(2,1)S(1)}, u32[]{:S(2)}, u32[]{:S(2)}) collective-permute-start(bf16[512,256]{1,0:T(8,128)(2,1)S(1)} %get-tuple-element.22), channel_id=1, source_target_pairs={{0,64},{64,0},{128,192},{192,128},{1,65},{65,1},{129,193},{193,129... | collective-permute-start | bytes 786440 | tf_op jit(solution)/shard_map/ppermute | solution.py:46
  59.7 6.6 %collective-permute-start.9 = (bf16[512,256]{1,0:T(8,128)(2,1)S(1)}, bf16[512,256]{1,0:T(8,128)(2,1)S(1)}, u32[]{:S(2)}, u32[]{:S(2)}) collective-permute-start(bf16[512,256]{1,0:T(8,128)(2,1)S(1)} %get-tuple-element.20), channel_id=1, source_target_pairs={{0,64},{64,0},{128,192},{192,128},{1,65},{65,1},{129,193},{193,129... | collective-permute-start | bytes 786440 | tf_op jit(solution)/shard_map/ppermute | solution.py:46
  60.8 17.2 %collective-permute-start.11 = (bf16[512,256]{1,0:T(8,128)(2,1)S(1)}, bf16[512,256]{1,0:T(8,128)(2,1)S(1)}, u32[]{:S(2)}, u32[]{:S(2)}) collective-permute-start(bf16[512,256]{1,0:T(8,128)(2,1)S(1)} %add_convert_fusion), channel_id=1, source_target_pairs={{0,128},{128,0},{64,192},{192,64},{1,129},{129,1},{65,193},{193,65... | collective-permute-start | bytes 786440 | tf_op jit(solution)/shard_map/ppermute | solution.py:345
